TPU v7x, 128 devices: a whole 4x4x4 slice. The times are simulated.
128 devices in a mesh: seq: 16 (over z, x), head: 8 (over y, core).
Axes of the slice: x: 4, y: 4, z: 4, core: 2. Of those that a mesh axis runs over, the one named last changes fastest.
Arguments:
- tokens: bfloat16 [32768, 2048], P('seq'), may hold values from -6 to 6
- norm_gain: float32 [2048], replicated, may hold values from 0.5 to 2
- in_weight: bfloat16 [2048, 3, 2048], P(None, None, 'head')
- out_weight: bfloat16 [2048, 2048], P('head'), may hold values from -0.125 to 0.125
- pattern: int32 [256, 4], replicated, may hold values from 0 to 255, as said below
Outputs:
- mixed: bfloat16 [32768, 2048], P(('seq', 'head'))
Inputs may be any that keep to these rules, and one draw needn't show every extreme that they name: `pattern`: row i names first tile i itself, then 4 - 1 distinct tiles held by other indices of seq (index = tile // 16). Among the rows of one index of seq, at most 4 of these later entries name tiles of any one other index, and every index has one such other index that it names exactly 4 times.
All inputs are finite; a program needn't handle non-finite values.
Results may differ from a plain program's by a relative error of at most 0.019.
Values may be sent and summed in bfloat16 or wider, within the bound.
No kernel may reach another device: no remote copies, remote signals or barrier semaphores. Data moves between devices by JAX's collectives and lax.ppermute only.
A program may use at most 128 MiB of HBM per device.

v0:
```python
import math

import jax
import jax.numpy as jnp
from jax import lax
from jax.sharding import PartitionSpec as P

HD = 128
TILE = 128
KT = 4


def normalize(tokens, norm_gain):
    values = tokens.astype(jnp.float32)
    mean_square = jnp.mean(values * values, axis=-1, keepdims=True)
    return (values * lax.rsqrt(mean_square + 1e-05) * norm_gain).astype(jnp.bfloat16)


def by_request(keyvals, pattern, my_rows, shards, myself, tile_count):
    entries = tile_count * (KT - 1)
    capacity = max(2, 3 * entries // (2 * (shards - 1)))
    wanted = pattern.reshape(shards, tile_count, KT)[:, :, 1:].reshape(shards, entries)
    owners = wanted // tile_count
    local_tile = wanted % tile_count
    owned_here = owners == myself
    ranking = jnp.cumsum(owned_here.astype(jnp.int32), axis=1) - 1
    slot_ids = jnp.arange(capacity, dtype=jnp.int32)
    select = owned_here[:, None, :] & (ranking[:, None, :] == slot_ids[None, :, None])
    filled = jnp.any(select, axis=2)
    chosen = jnp.sum(jnp.where(select, local_tile[:, None, :], 0), axis=2)
    outgoing = jnp.where(filled[:, :, None, None], keyvals[chosen], jnp.zeros((), keyvals.dtype))
    incoming = lax.all_to_all(outgoing, "seq", split_axis=0, concat_axis=0, tiled=True)
    sources = my_rows[:, 1:].reshape(entries) // tile_count
    one_hot = (sources[:, None] == jnp.arange(shards, dtype=jnp.int32)[None, :]).astype(jnp.int32)
    running = jnp.cumsum(one_hot, axis=0)
    position = jnp.sum(running * one_hot, axis=1) - 1
    flat_index = sources * capacity + position
    fetched = incoming.reshape(shards * capacity, TILE, keyvals.shape[2])[flat_index]
    return fetched.reshape(tile_count, KT - 1, TILE, keyvals.shape[2])


def body(tokens, norm_gain, in_weight, out_weight, pattern):
    shards = lax.axis_size("seq")
    myself = lax.axis_index("seq")
    row_count = tokens.shape[0]
    tile_count = row_count // TILE
    head_width = in_weight.shape[2]
    head_count = head_width // HD
    normed = normalize(tokens, norm_gain)
    projected = jnp.dot(
        normed,
        in_weight.reshape(in_weight.shape[0], 3 * head_width),
        preferred_element_type=jnp.float32,
    ).astype(jnp.bfloat16)
    projected = projected.reshape(row_count, 3, head_width)
    queries = projected[:, 0].reshape(tile_count, TILE, head_count, HD)
    keyvals = jnp.concatenate([projected[:, 1], projected[:, 2]], axis=1).reshape(
        tile_count, TILE, 2 * head_width
    )
    my_rows = lax.dynamic_slice_in_dim(pattern, myself * tile_count, tile_count, 0)
    fetched = by_request(keyvals, pattern, my_rows, shards, myself, tile_count)
    gathered = jnp.concatenate([keyvals[:, None], fetched], axis=1).reshape(
        tile_count, KT * TILE, 2 * head_width
    )
    key_block = gathered[:, :, :head_width].reshape(tile_count, KT * TILE, head_count, HD)
    value_block = gathered[:, :, head_width:].reshape(tile_count, KT * TILE, head_count, HD)
    scores = jnp.einsum(
        "tqhd,tkhd->thqk", queries, key_block, preferred_element_type=jnp.float32
    ) * (1.0 / math.sqrt(HD))
    maxima = jnp.max(scores, axis=-1, keepdims=True)
    exponent = jnp.exp(scores - maxima)
    weights = (exponent / jnp.sum(exponent, axis=-1, keepdims=True)).astype(jnp.bfloat16)
    attended = jnp.einsum(
        "thqk,tkhd->tqhd", weights, value_block, preferred_element_type=jnp.float32
    ).astype(jnp.bfloat16)
    attended = attended.reshape(row_count, head_width)
    return lax.psum_scatter(
        jnp.dot(attended, out_weight, preferred_element_type=jnp.float32).astype(jnp.bfloat16),
        "head",
        scatter_dimension=0,
        tiled=True,
    )


def solution(mesh):
    return jax.shard_map(
        body,
        mesh=mesh,
        in_specs=(P("seq", None), P(), P(None, None, "head"), P("head", None), P()),
        out_specs=P(("seq", "head"), None),
        check_vma=False,
    )
```

profile of v0, /device:TPU:7, one launch (start us, length us, event | category | flops | bytes accessed | tf_op | source)
XLA Modules:
  0.0 295.3 jit_solution(7372050165158290330)
XLA Ops:
  6.5 4.8 %copy.29 = bf16[2048,3,256]{0,2,1:T(8,128)(2,1)} copy(bf16[2048,3,256]{2,0,1:T(8,128)(2,1)} %param.7) | data formatting | bytes 6291456 | tf_op args[2]
  11.3 5.2 %fusion.1 = f32[2048]{0:T(1024)S(1)} fusion(bf16[2048,2048]{1,0:T(8,128)(2,1)} %param.5), kind=kLoop, calls=%fused_computation.5 | loop fusion | flops 12580864 | bytes 8396800 | tf_op jit(solution)/shard_map/reduce_sum | solution.py:15
  16.6 0.5 copy-done.4
  17.1 9.0 %fusion.13 = bf16[2048,768]{0,1:T(8,128)(2,1)S(1)} fusion(bf16[2048,768]{0,1:T(8,128)(2,1)} %bitcast.58, bf16[2048,2048]{1,0:T(8,128)(2,1)S(1)} %copy-done.4, f32[2048]{0:T(1024)S(1)} %copy-done.7, f32[2048]{0:T(1024)S(1)} %add_rsqrt_fusion), kind=kOutput, calls=%fused_computation.20 | convolution fusion | flops 6460801024 | bytes 14696448 | tf_op jit(solution)/shard_map/dot_general | solution.py:50
  26.1 0.0 copy-start.6
  26.1 1.2 slice_bitcast_fusion
  27.3 1.3 copy.31
  28.7 1.3 copy.30
  30.0 0.0 copy-done.6
  30.0 0.1 reshape.260
  30.1 0.1 copy.49
  30.2 0.1 copy.33
  30.3 0.2 reduce_window_sum.22
  30.5 0.1 fusion.27
  30.6 0.2 select_reduce_fusion
  30.8 0.1 copy.40
  30.9 0.1 reshape.272
  31.0 0.1 copy.37
  31.1 1.7 pad_maximum_fusion.1
  32.8 5.5 %gather_fusion = bf16[64,128,512]{2,1,0:T(8,128)(2,1)} fusion(bf16[16,128,512]{2,1,0:T(8,128)(2,1)S(1)} %pad_maximum_fusion.1, s32[1024]{0:T(1024)S(1)} %pad_clamp_fusion.1), kind=kCustom, calls=%fused_computation | custom fusion | bytes 16777472 | tf_op jit(solution)/shard_map/gather | solution.py:31
  38.3 7.2 %broadcast_select_fusion = bf16[16,4,128,512]{3,2,1,0:T(8,128)(2,1)} fusion(bf16[16,4,128,512]{3,2,1,0:T(8,128)(2,1)} %bitcast.47, pred[16,4]{1,0:T(8,128)(4,1)S(1)} %copy.37), kind=kLoop, calls=%fused_computation.14 | loop fusion | flops 4194304 | bytes 16777280 | tf_op jit(solution)/shard_map/jit(_where)/select_n | solution.py:31
  45.5 7.7 %all-to-all-start = ((bf16[16,4,128,512]{3,2,1,0:T(8,128)(2,1)}), bf16[16,4,128,512]{3,2,1,0:T(8,128)(2,1)}, u32[]{:S(2)}, u32[]{:S(2)}) async-start(bf16[16,4,128,512]{3,2,1,0:T(8,128)(2,1)} %broadcast_select_fusion), calls=%async_computation | async-start | bytes 16777216 | tf_op jit(solution)/shard_map/all_to_all | solution.py:32
  53.3 0.2 reduce-scatter.2.cloned.1.call-start
  53.5 0.1 constant_dynamic-slice_fusion
  53.6 0.1 copy.41
  53.7 0.1 reshape.264
  53.8 0.1 reshape.263
  53.9 0.1 fusion.28
  54.0 0.1 reduce_window_sum.23
  54.0 2.5 copy.52
  56.5 0.2 select_reduce_fusion.1
  56.7 118.8 %all-to-all-done = bf16[16,4,128,512]{3,2,1,0:T(8,128)(2,1)} async-done(((bf16[16,4,128,512]{3,2,1,0:T(8,128)(2,1)}), bf16[16,4,128,512]{3,2,1,0:T(8,128)(2,1)}, u32[]{:S(2)}, u32[]{:S(2)}) %all-to-all-start) | async-done | bytes 8388640 | tf_op jit(solution)/shard_map/all_to_all | solution.py:32
  175.5 8.4 %gather_fusion.1 = bf16[48,128,512]{2,1,0:T(8,128)(2,1)} fusion(bf16[64,128,512]{2,1,0:T(8,128)(2,1)} %bitcast.8, s32[1024]{0:T(1024)S(1)} %pad_clamp_fusion), kind=kCustom, calls=%fused_computation.1 | custom fusion | bytes 12583104 | tf_op jit(solution)/shard_map/gather | solution.py:38
  183.9 0.0 copy-done.3
  183.9 3.9 %pad_maximum_fusion = bf16[16,4,128,512]{3,2,1,0:T(8,128)(2,1)S(1)} fusion(bf16[16,3,128,512]{3,2,1,0:T(8,128)(2,1)} %bitcast.49, bf16[16,1,128,256]{3,2,1,0:T(8,128)(2,1)S(1)} %bitcast.51, bf16[16,1,128,256]{3,2,1,0:T(8,128)(2,1)S(1)} %bitcast.53), kind=kLoop, calls=%fused_computation.9 | loop fusion | flops 25165824 | bytes 16777216 | tf_op jit(solution)/shard_map/concatenate | solution.py:62
  187.7 3.5 %fusion.39 = (bf16[16,512,256]{2,1,0:T(8,128)(2,1)}, bf16[16,512,256]{2,1,0:T(8,128)(2,1)}) fusion(bf16[16,512,512]{2,1,0:T(8,128)(2,1)S(1)} %bitcast.46), kind=kLoop, calls=%fused_computation.66 | loop fusion | bytes 16777216 | tf_op jit(solution)/shard_map/slice | solution.py:65
  191.3 6.5 %copy.50 = bf16[16,512,256]{1,2,0:T(8,128)(2,1)} copy(bf16[16,512,256]{2,1,0:T(8,128)(2,1)} %get-tuple-element.8) | data formatting | bytes 8388608
  197.7 6.4 %copy.51 = bf16[16,512,256]{1,2,0:T(8,128)(2,1)} copy(bf16[16,512,256]{2,1,0:T(8,128)(2,1)} %get-tuple-element.7) | data formatting | bytes 8388608
  204.2 0.0 copy-done.5
  204.2 3.5 %fusion.20 = f32[16,2,128,512]{3,2,1,0:T(8,128)S(1)} fusion(bf16[16,512,2,128]{1,3,2,0:T(8,128)(2,1)} %bitcast.48, bf16[16,128,2,128]{1,0,3,2:T(8,128)(2,1)S(1)} %bitcast.54), kind=kOutput, calls=%fused_computation.27 | convolution fusion | flops 536870912 | bytes 13631488 | tf_op jit(solution)/shard_map/tqhd,tkhd->thqk/dot_general | solution.py:67
  207.6 0.0 copy-start.1
  207.7 3.2 %copy-done.1 = f32[16,2,128,512]{3,2,1,0:T(8,128)} copy-done((f32[16,2,128,512]{3,2,1,0:T(8,128)}, f32[16,2,128,512]{3,2,1,0:T(8,128)S(1)}, u32[]{:S(2)}) %copy-start.1) | copy-done | bytes 8388632
  210.9 2.6 fusion.40
  213.5 14.4 %fusion.17 = bf16[16,128,2,128]{1,3,2,0:T(8,128)(2,1)S(1)} fusion(bf16[16,512,2,128]{1,3,2,0:T(8,128)(2,1)} %bitcast.56, f32[16,2,128]{2,1,0:T(2,128)S(1)} %fusion.40, f32[16,2,128,512]{3,2,1,0:T(8,128)} %copy-done.1), kind=kOutput, calls=%fused_computation.23 | convolution fusion | flops 547885568 | bytes 13647872 | tf_op jit(solution)/shard_map/thqk,tkhd->tqhd/dot_general | solution.py:73
  227.9 0.7 copy.47
  228.6 5.6 %convolution_convert_fusion = bf16[2048,2048]{1,0:T(8,128)(2,1)} fusion(bf16[256,2048]{1,0:T(8,128)(2,1)S(1)} %copy-done, bf16[32,8,16,128]{3,2,1,0:T(8,128)(2,1)S(1)} %bitcast.55), kind=kOutput, calls=%fused_computation.15 | convolution fusion | flops 2151677952 | bytes 10485760 | tf_op jit(solution)/shard_map/dot_general | solution.py:78
  234.3 0.0 reduce-scatter.2.cloned.1.call-update
  234.3 54.1 %reduce-scatter.2.cloned.1.call-done = bf16[256,2048]{1,0:T(8,128)(2,1)} async-done(((bf16[2048,2048]{1,0:T(8,128)(2,1)}), bf16[256,2048]{1,0:T(8,128)(2,1)}) %reduce-scatter.2.cloned.1.call-update) | async-done | bytes 1048592 | tf_op jit(solution)/shard_map/reduce_scatter | solution.py:77
  (20 shorter events, 0.1 us)
Async XLA Ops:
  6.5 222.1 %copy-start = (bf16[256,2048]{1,0:T(8,128)(2,1)S(1)}, bf16[256,2048]{1,0:T(8,128)(2,1)}, u32[]{:S(2)}) copy-start(bf16[256,2048]{1,0:T(8,128)(2,1)} %param.8) | copy-start | bytes 3145732
  6.5 10.0 %copy-start.7 = (f32[2048]{0:T(1024)S(1)}, f32[2048]{0:T(1024)}, u32[]{:S(2)}) copy-start(f32[2048]{0:T(1024)} %param.6) | copy-start | bytes 24580
  11.3 5.8 %copy-start.4 = (bf16[2048,2048]{1,0:T(8,128)(2,1)S(1)}, bf16[2048,2048]{1,0:T(8,128)(2,1)}, u32[]{:S(2)}) copy-start(bf16[2048,2048]{1,0:T(8,128)(2,1)} %param.5) | copy-start | bytes 25165828
  26.1 3.9 %copy-start.6 = (s32[256,4]{0,1:T(4,128)S(1)}, s32[256,4]{0,1:T(4,128)}, u32[]{:S(2)}) copy-start(s32[256,4]{0,1:T(4,128)} %param.9) | copy-start | bytes 12292
  45.5 129.9 %all-to-all-start = ((bf16[16,4,128,512]{3,2,1,0:T(8,128)(2,1)}), bf16[16,4,128,512]{3,2,1,0:T(8,128)(2,1)}, u32[]{:S(2)}, u32[]{:S(2)}) async-start(bf16[16,4,128,512]{3,2,1,0:T(8,128)(2,1)} %broadcast_select_fusion), calls=%async_computation | async-start | bytes 16777216 | tf_op jit(solution)/shard_map/all_to_all | solution.py:32
  53.3 130.6 %copy-start.2 = (bf16[2048,1,256]{2,0,1:T(8,128)(2,1)S(1)}, bf16[2048,1,256]{2,0,1:T(8,128)(2,1)}, u32[]{:S(2)}) copy-start(bf16[2048,1,256]{2,0,1:T(8,128)(2,1)} %copy.31) | copy-start | bytes 3145732
  53.3 130.6 %copy-start.3 = (bf16[2048,1,256]{2,0,1:T(8,128)(2,1)S(1)}, bf16[2048,1,256]{2,0,1:T(8,128)(2,1)}, u32[]{:S(2)}) copy-start(bf16[2048,1,256]{2,0,1:T(8,128)(2,1)} %copy.30) | copy-start | bytes 3145732
  53.3 235.1 %reduce-scatter.2.cloned.1.call-start = ((), (), s32[]{:S(2)}) async-start(), calls=%async_computation.2 | async-start | bytes 9437184 | tf_op jit(solution)/shard_map/reduce_scatter | solution.py:77
  191.3 12.9 %copy-start.5 = (bf16[32,8,16,128]{3,2,1,0:T(8,128)(2,1)S(1)}, bf16[32,8,16,128]{3,2,1,0:T(8,128)(2,1)}, u32[]{:S(2)}) copy-start(bf16[32,8,16,128]{3,2,1,0:T(8,128)(2,1)} %copy.52) | copy-start | bytes 3145732
  207.6 3.2 %copy-start.1 = (f32[16,2,128,512]{3,2,1,0:T(8,128)}, f32[16,2,128,512]{3,2,1,0:T(8,128)S(1)}, u32[]{:S(2)}) copy-start(f32[16,2,128,512]{3,2,1,0:T(8,128)S(1)} %fusion.20) | copy-start | bytes 25165828
Sparse Core Ops, SparseCore 0:
  234.4 53.9 reduce-scatter.1
where the time goes:
time: 297 us; the launch traced here: 295 us
  waiting for transfers between devices  173 us (58%)
  local copies, waits for them, and re-layouts  46.8 us (16%)
  matrix products  32.5 us (11%)
  other arithmetic  21.6 us (7%)
  between operations  13.6 us (5%)
  starting transfers between devices  7.96 us (3%)
    all_to_all x1, waiting for transfers between devices, by_request(): lax.all_to_all(outgoing, 'seq', split_axis=0, concat_axis=0, tiled=True)  119 us
    reduce_scatter x1, waiting for transfers between devices, body(): lax.psum_scatter(jnp.dot(attended, out_weight, preferred_element_type=jnp...  54.1 us
    unnamed x22, local copies, waits for them, and re-layouts  25.2 us
    dot_general x1, matrix products, body(): jnp.einsum('thqk,tkhd->tqhd', weights, value_block, preferred_element_typ...  14.4 us
    dot_general x1, matrix products, body(): jnp.dot(normed, in_weight.reshape(in_weight.shape[0], 3 * head_width), pr...  8.98 us
    gather x1, local copies, waits for them, and re-layouts, by_request(): incoming.reshape(shards * capacity, TILE, keyvals.shape[2])[flat_index]  8.41 us
    all_to_all x1, starting transfers between devices, by_request(): lax.all_to_all(outgoing, 'seq', split_axis=0, concat_axis=0, tiled=True)  7.73 us
    select_n x1, other arithmetic, by_request(): jnp.where(filled[:, :, None, None], keyvals[chosen], jnp.zeros((), keyval...  7.21 us
  transfers between devices with their start and end apart: 2, of which 2 were waited for; matrix products, arithmetic and copies ran while one was open for 1% of the time, Pallas kernels for 0%

commit v1 on v0

v1 whole, which is shorter than its diff:
```python
import functools
import math

import jax
import jax.numpy as jnp
from jax import lax
from jax.experimental import pallas as pl
from jax.experimental.pallas import tpu as pltpu
from jax.sharding import PartitionSpec as P

HD = 128
TILE = 128
KT = 4
CAP = 4
CHUNKS = 2
BLOCK = 256
GROUP = 4


def tables_kernel(me_ref, pattern_ref, chosen_ref, source_ref, *, shards, tiles):
    total = shards * tiles
    table = pattern_ref[...]
    owner = table // tiles
    local = table % tiles
    row = lax.broadcasted_iota(jnp.int32, (total, total), 0)
    col = lax.broadcasted_iota(jnp.int32, (total, total), 1)
    same = (row // tiles) == (col // tiles)
    every = same.astype(jnp.bfloat16)
    before = (same & (row < col)).astype(jnp.bfloat16)
    index = lax.broadcasted_iota(jnp.int32, (shards, total), 0)
    names = [(owner[c : c + 1] == index).astype(jnp.bfloat16) for c in range(1, KT)]
    dot = functools.partial(jnp.dot, preferred_element_type=jnp.float32)
    earlier = jnp.zeros((shards, total), jnp.float32)
    picked = [jnp.zeros((1, total), jnp.float32) for _ in range(CAP)]
    source_ref[0:1, :] = jnp.zeros((1, total), jnp.int32)
    for c in range(1, KT):
        here = names[c - 1]
        rank = jnp.sum(here.astype(jnp.float32) * (dot(here, before) + earlier), axis=0, keepdims=True)
        earlier = earlier + dot(here, every)
        rank = rank.astype(jnp.int32)
        mine = owner[c : c + 1] == me_ref[0]
        source_ref[c : c + 1, :] = owner[c : c + 1] * CAP + rank
        for k in range(CAP):
            picked[k] += jnp.where(mine & (rank == k), local[c : c + 1], 0).astype(jnp.float32)
    tile_row = lax.broadcasted_iota(jnp.int32, (total, 128), 0)
    lane = lax.broadcasted_iota(jnp.int32, (total, 128), 1)
    spread = ((tile_row // tiles) == lane).astype(jnp.bfloat16)
    for k in range(CAP):
        chosen_ref[k : k + 1, :] = dot(picked[k].astype(jnp.bfloat16), spread).astype(jnp.int32)


def project_kernel(chosen_ref, tokens_ref, gain_ref, weight_ref, queries_ref, *rest, shards, chunks):
    own_refs, send_refs = rest[:chunks], rest[chunks : 2 * chunks]
    held_refs, semaphore = rest[2 * chunks : 3 * chunks], rest[3 * chunks]
    step = pl.program_id(0)
    values = tokens_ref[...].astype(jnp.float32)
    mean_square = jnp.mean(values * values, axis=-1, keepdims=True)
    normed = (values * lax.rsqrt(mean_square + 1e-05) * gain_ref[...]).astype(jnp.bfloat16)
    parts = []
    for c in range(3):
        part = jnp.dot(normed, weight_ref[c], preferred_element_type=jnp.float32)
        parts.append(part.astype(jnp.bfloat16))
    count = BLOCK // TILE
    width = parts[0].shape[1] // chunks
    queries_ref[...] = parts[0].reshape(count, TILE, parts[0].shape[1])
    for h in range(chunks):
        keys = parts[1][:, h * width : (h + 1) * width].reshape(count, TILE, width)
        vals = parts[2][:, h * width : (h + 1) * width].reshape(count, TILE, width)
        own_refs[h][:, :, :width] = keys
        own_refs[h][:, :, width:] = vals
        held_refs[h][pl.ds(step * count, count), :, :width] = keys
        held_refs[h][pl.ds(step * count, count), :, width:] = vals

    @pl.when(step == pl.num_programs(0) - 1)
    def _():
        for h in range(chunks):
            for d in range(shards):
                for k in range(CAP):
                    pltpu.make_async_copy(
                        held_refs[h].at[chosen_ref[k, d]], send_refs[h].at[d, k], semaphore
                    ).start()
        for h in range(chunks):
            for d in range(shards):
                for k in range(CAP):
                    pltpu.make_async_copy(
                        held_refs[h].at[chosen_ref[k, d]], send_refs[h].at[d, k], semaphore
                    ).wait()


def attend_kernel(first_ref, source_ref, queries_ref, own_ref, *rest):
    remote_refs, out_ref = rest[:-1], rest[-1]
    width = queries_ref.shape[2]
    scale = 1.0 / math.sqrt(HD)
    for g in range(GROUP):
        blocks = [own_ref.at[g]] + [remote_refs[g * (KT - 1) + j].at[0] for j in range(KT - 1)]
        for h in range(width // HD):
            lanes = slice(h * HD, (h + 1) * HD)
            upper = slice(width + h * HD, width + (h + 1) * HD)
            query = queries_ref[g, :, lanes]
            scores = [
                lax.dot_general(
                    query, block[:, lanes], (((1,), (1,)), ((), ())), preferred_element_type=jnp.float32
                )
                for block in blocks
            ]
            highest = functools.reduce(jnp.maximum, scores)
            highest = jnp.max(highest, axis=-1, keepdims=True)
            exponents = [jnp.exp((s - highest) * scale) for s in scores]
            total = jnp.sum(functools.reduce(jnp.add, exponents), axis=-1, keepdims=True)
            attended = functools.reduce(
                jnp.add,
                [
                    jnp.dot(e.astype(jnp.bfloat16), block[:, upper], preferred_element_type=jnp.float32)
                    for e, block in zip(exponents, blocks)
                ],
            )
            out_ref[pl.ds(g * TILE, TILE), lanes] = (attended / total).astype(jnp.bfloat16)


def mix_kernel(*refs, chunks):
    attended_refs, weight_refs, out_ref = refs[:chunks], refs[chunks : 2 * chunks], refs[-1]
    total = None
    for attended_ref, weight_ref in zip(attended_refs, weight_refs):
        left = jnp.concatenate([attended_ref[s] for s in range(attended_ref.shape[0])], axis=1)
        right = weight_ref[...].reshape(left.shape[1], weight_ref.shape[3])
        part = jnp.dot(left, right, preferred_element_type=jnp.float32)
        total = part if total is None else total + part
    out_ref[...] = total.astype(jnp.bfloat16)


def body(tokens, norm_gain, in_weight, out_weight, pattern):
    shards = lax.axis_size("seq")
    groups = lax.axis_size("head")
    myself = lax.axis_index("seq")
    row_count, model = tokens.shape
    tiles = row_count // TILE
    head_width = in_weight.shape[2]
    chunks = CHUNKS
    width = head_width // chunks
    me = jnp.reshape(myself, (1,)).astype(jnp.int32)
    bf16 = jnp.bfloat16

    gathered = lax.all_gather(out_weight, "head", axis=0, tiled=True)

    smem = pl.BlockSpec(memory_space=pltpu.SMEM)
    chosen, source = pl.pallas_call(
        functools.partial(tables_kernel, shards=shards, tiles=tiles),
        in_specs=[smem, pl.BlockSpec(memory_space=pltpu.VMEM)],
        out_shape=[
            jax.ShapeDtypeStruct((8, 128), jnp.int32),
            jax.ShapeDtypeStruct((KT, shards * tiles), jnp.int32),
        ],
        name="tables",
    )(me, pattern.T)

    count = BLOCK // TILE
    outs = pl.pallas_call(
        functools.partial(project_kernel, shards=shards, chunks=chunks),
        grid_spec=pltpu.PrefetchScalarGridSpec(
            num_scalar_prefetch=1,
            grid=(row_count // BLOCK,),
            in_specs=[
                pl.BlockSpec((BLOCK, model), lambda i, c: (i, 0)),
                pl.BlockSpec((1, model), lambda i, c: (0, 0)),
                pl.BlockSpec((3, model, head_width), lambda i, c: (0, 0, 0), pipeline_mode=pl.Buffered(1)),
            ],
            out_specs=[pl.BlockSpec((count, TILE, head_width), lambda i, c: (i, 0, 0))]
            + [pl.BlockSpec((count, TILE, 2 * width), lambda i, c: (i, 0, 0))] * chunks
            + [pl.BlockSpec(memory_space=pl.ANY)] * chunks,
            scratch_shapes=[pltpu.VMEM((tiles, TILE, 2 * width), bf16)] * chunks + [pltpu.SemaphoreType.DMA],
        ),
        out_shape=[jax.ShapeDtypeStruct((tiles, TILE, head_width), bf16)]
        + [jax.ShapeDtypeStruct((tiles, TILE, 2 * width), bf16)] * chunks
        + [jax.ShapeDtypeStruct((shards, CAP, TILE, 2 * width), bf16)] * chunks,
        compiler_params=pltpu.CompilerParams(vmem_limit_bytes=48 * 1024 * 1024),
        name="project",
    )(chosen, tokens, norm_gain.reshape(1, model), in_weight.transpose(1, 0, 2))
    queries, owns, sends = outs[0], outs[1 : 1 + chunks], outs[1 + chunks :]

    first = me * tiles
    received = []
    for h in range(chunks):
        incoming = lax.all_to_all(sends[h], "seq", split_axis=0, concat_axis=0, tiled=True)
        incoming = incoming.reshape(shards * CAP, TILE, 2 * width)
        remote_specs = []
        for g in range(GROUP):
            for j in range(1, KT):
                remote_specs.append(
                    pl.BlockSpec(
                        (1, TILE, 2 * width),
                        lambda i, f, s, g=g, j=j: (s[j, f[0] + i * GROUP + g], 0, 0),
                    )
                )
        attended = pl.pallas_call(
            attend_kernel,
            grid_spec=pltpu.PrefetchScalarGridSpec(
                num_scalar_prefetch=2,
                grid=(tiles // GROUP,),
                in_specs=[
                    pl.BlockSpec((GROUP, TILE, width), lambda i, f, s, h=h: (i, 0, h)),
                    pl.BlockSpec((GROUP, TILE, 2 * width), lambda i, f, s: (i, 0, 0)),
                ]
                + remote_specs,
                out_specs=pl.BlockSpec((GROUP * TILE, width), lambda i, f, s: (i, 0)),
            ),
            out_shape=jax.ShapeDtypeStruct((row_count, width), bf16),
            name="attend",
        )(first, source, queries, owns[h], *([incoming] * len(remote_specs)))
        received.append(
            lax.all_to_all(
                attended.reshape(groups, row_count // groups, width), "head", split_axis=0, concat_axis=0, tiled=True
            )
        )

    rows = row_count // groups
    columns = 512
    weights = gathered.reshape(groups, chunks, width, model)
    return pl.pallas_call(
        functools.partial(mix_kernel, chunks=chunks),
        grid=(model // columns,),
        in_specs=[pl.BlockSpec((groups, rows, width), lambda i: (0, 0, 0))] * chunks
        + [
            pl.BlockSpec((groups, 1, width, columns), lambda i, h=h: (0, h, 0, i))
            for h in range(chunks)
        ],
        out_specs=pl.BlockSpec((rows, columns), lambda i: (0, i)),
        out_shape=jax.ShapeDtypeStruct((rows, model), bf16),
        compiler_params=pltpu.CompilerParams(vmem_limit_bytes=48 * 1024 * 1024),
        name="mix",
    )(*received, *([weights] * chunks))


def solution(mesh):
    return jax.shard_map(
        body,
        mesh=mesh,
        in_specs=(P("seq", None), P(), P(None, None, "head"), P("head", None), P()),
        out_specs=P(("seq", "head"), None),
        check_vma=False,
    )
```

time: 297 us -> 194 us (0.65)
  the two profiles are of different devices: /device:TPU:7 before, /device:TPU:1 now
where the time goes in v1:
time: 194 us; the launch traced here: 193 us
  blocking collectives  72.4 us (37%)
  waiting for transfers between devices  51.1 us (26%)
  Pallas kernels  42.8 us (22%)
  between operations  13.5 us (7%)
  starting transfers between devices  11.6 us (6%)
    all_to_all x1, blocking collectives, body(): lax.all_to_all(sends[h], 'seq', split_axis=0, concat_axis=0, tiled=True)  58.4 us
    all_to_all x1, waiting for transfers between devices, body(): lax.all_to_all(sends[h], 'seq', split_axis=0, concat_axis=0, tiled=True)  50.2 us
    pallas_call x2, Pallas kernels, body(): pl.pallas_call(attend_kernel, grid_spec=pltpu.PrefetchScalarGridSpec(num_...  18.7 us
    pallas_call x1, Pallas kernels, body(): pl.pallas_call(functools.partial(project_kernel, shards=shards, chunks=ch...  16.2 us
    all_to_all x1, blocking collectives, body(): lax.all_to_all(attended.reshape(groups, row_count // groups, width), 'hea...  14.1 us
    all_to_all x1, starting transfers between devices, body(): lax.all_to_all(attended.reshape(groups, row_count // groups, width), 'hea...  7.03 us
    pallas_call x1, Pallas kernels, body(): pl.pallas_call(functools.partial(mix_kernel, chunks=chunks), grid=(model...  6.25 us
    all_to_all x1, starting transfers between devices, body(): lax.all_to_all(sends[h], 'seq', split_axis=0, concat_axis=0, tiled=True)  4.56 us
  transfers between devices with their start and end apart: 3, of which 2 were waited for; matrix products, arithmetic and copies ran while one was open for 0% of the time, Pallas kernels for 19%

profile of v1, /device:TPU:1, one launch (start us, length us, event | category | flops | bytes accessed | tf_op | source)
XLA Modules:
  0.0 192.8 jit_solution(17141858356428115025)
XLA Ops:
  6.5 0.0 all-gather.2.cloned.1.call-start
  6.5 0.7 all-gather.2.cloned.1.call-update
  7.3 1.7 tables.1
  8.9 0.0 copy-start.3
  8.9 0.7 copy-done.3
  9.6 0.0 copy-start.4
  9.6 0.7 copy-done.4
  10.3 16.2 %project.1 = (bf16[16,128,256]{2,1,0:T(8,128)(2,1)S(1)}, bf16[16,128,256]{2,1,0:T(8,128)(2,1)S(1)}, bf16[16,128,256]{2,1,0:T(8,128)(2,1)S(1)}, bf16[16,4,128,256...) custom-call(s32[8,128]{1,0:T(8,128)S(1)} %copy-done.4, bf16[2048,2048]{1,0:T(8,128)(2,1)} %tokens_ref.1, f32[1,2048]{1,0:T(1,128)S(1)} %bitcast.9, ...), custom_call_target="tpu_custom_call" | custom-call | tf_op jit(solution)/shard_map/project/pallas_call | solution.py:157
  26.5 0.0 copy-start
  26.5 0.0 copy-start.1
  26.5 0.0 copy-start.2
  26.5 58.4 %all_to_all.20 = bf16[16,4,128,256]{3,2,1,0:T(8,128)(2,1)} all-to-all(bf16[16,4,128,256]{3,2,1,0:T(8,128)(2,1)} %get-tuple-element.16), channel_id=1, replica_groups=mesh['seq'=16,'head'=8] {'seq'}, dimensions={0} | all-to-all | bytes 8388608 | tf_op jit(solution)/shard_map/all_to_all | solution.py:183
  84.9 0.0 copy-done
  84.9 0.0 copy-done.1
  84.9 0.0 copy-done.2
  84.9 4.6 %all-to-all-start.2 = ((bf16[16,4,128,256]{3,2,1,0:T(8,128)(2,1)}), bf16[16,4,128,256]{3,2,1,0:T(8,128)(2,1)}, u32[]{:S(2)}, u32[]{:S(2)}) async-start(bf16[16,4,128,256]{3,2,1,0:T(8,128)(2,1)} %get-tuple-element.18), calls=%async_computation.2 | async-start | bytes 8388608 | tf_op jit(solution)/shard_map/all_to_all | solution.py:183
  89.5 9.4 %attend.2 = bf16[2048,128]{1,0:T(8,128)(2,1)} custom-call(s32[1]{0:T(128)S(6)} %mul.3.first_ref, s32[4,256]{1,0:T(4,128)} %get-tuple-element.12.source_ref, bf16[16,128,256]{2,1,0:T(8,128)(2,1)} %copy-done, bf16[16,128,256]{2,1,0:T(8,128)(2,1)} %copy-done.2, bf16[64,128,256]{2,1,0:T(8,128)(2,1)} %bitcast.10, bf16[64,128,256]{2,1,0:T(8,128)(2,1)} %bitcast.11, ...), custom_call_target="tpu_custom_call" | custom-call | tf_op jit(solution)/shard_map/attend/pallas_call | solution.py:194
  98.9 50.2 %all-to-all-done.2 = bf16[16,4,128,256]{3,2,1,0:T(8,128)(2,1)} async-done(((bf16[16,4,128,256]{3,2,1,0:T(8,128)(2,1)}), bf16[16,4,128,256]{3,2,1,0:T(8,128)(2,1)}, u32[]{:S(2)}, u32[]{:S(2)}) %all-to-all-start.2) | async-done | bytes 4194336 | tf_op jit(solution)/shard_map/all_to_all | solution.py:183
  149.1 7.0 %all-to-all-start.1 = ((bf16[8,256,128]{2,1,0:T(8,128)(2,1)}), bf16[8,256,128]{2,1,0:T(8,128)(2,1)S(1)}, u32[]{:S(2)}, u32[]{:S(2)}) async-start(bf16[8,256,128]{2,1,0:T(8,128)(2,1)} %bitcast.25), calls=%async_computation.1 | async-start | bytes 1048576 | tf_op jit(solution)/shard_map/all_to_all | solution.py:210
  156.1 9.4 %attend.3 = bf16[2048,128]{1,0:T(8,128)(2,1)} custom-call(s32[1]{0:T(128)S(6)} %mul.3.first_ref, s32[4,256]{1,0:T(4,128)} %get-tuple-element.12.source_ref, bf16[16,128,256]{2,1,0:T(8,128)(2,1)} %copy-done, bf16[16,128,256]{2,1,0:T(8,128)(2,1)} %copy-done.1, ...), custom_call_target="tpu_custom_call" | custom-call | tf_op jit(solution)/shard_map/attend/pallas_call | solution.py:194
  165.5 0.1 all-to-all-done.1.refs_0_
  165.6 14.1 %all_to_all.21.refs_1_ = bf16[8,256,128]{2,1,0:T(8,128)(2,1)S(1)} all-to-all(bf16[8,256,128]{2,1,0:T(8,128)(2,1)} %bitcast.26), channel_id=1, replica_groups=mesh['seq'=16,'head'=8] {'head'}, dimensions={0} | all-to-all | bytes 1048576 | tf_op jit(solution)/shard_map/all_to_all | solution.py:210
  179.7 0.0 all-gather.2.cloned.1.call-done
  179.7 6.3 %mix.1 = bf16[256,2048]{1,0:T(8,128)(2,1)} custom-call(bf16[8,256,128]{2,1,0:T(8,128)(2,1)S(1)} %all-to-all-done.1.refs_0_, bf16[8,256,128]{2,1,0:T(8,128)(2,1)S(1)} %all_to_all.21.refs_1_, bf16[8,2,128,2048]{3,2,1,0:T(8,128)(2,1)} %bitcast.22, bf16[8,2,128,2048]{3,2,1,0:T(8,128)(2,1)} %bitcast.23), custom_call_target="tpu_custom_call" | custom-call | tf_op jit(solution)/shard_map/mix/pallas_call | solution.py:218
Async XLA Ops:
  6.5 173.1 %all-gather.2.cloned.1.call-start = ((), (), s32[]{:S(2)}) async-start(), calls=%async_computation.4 | async-start | bytes 9437184 | tf_op jit(solution)/shard_map/all_gather | solution.py:143
  8.9 0.7 copy-start.3
  9.6 0.7 copy-start.4
  26.5 58.4 %copy-start = (bf16[16,128,256]{2,1,0:T(8,128)(2,1)}, bf16[16,128,256]{2,1,0:T(8,128)(2,1)S(1)}, u32[]{:S(2)}) copy-start(bf16[16,128,256]{2,1,0:T(8,128)(2,1)S(1)} %get-tuple-element.14.queries_ref) | copy-start | bytes 3145732
  26.5 58.4 %copy-start.1 = (bf16[16,128,256]{2,1,0:T(8,128)(2,1)}, bf16[16,128,256]{2,1,0:T(8,128)(2,1)S(1)}, u32[]{:S(2)}) copy-start(bf16[16,128,256]{2,1,0:T(8,128)(2,1)S(1)} %get-tuple-element.17.own_ref) | copy-start | bytes 3145732
  26.5 58.4 %copy-start.2 = (bf16[16,128,256]{2,1,0:T(8,128)(2,1)}, bf16[16,128,256]{2,1,0:T(8,128)(2,1)S(1)}, u32[]{:S(2)}) copy-start(bf16[16,128,256]{2,1,0:T(8,128)(2,1)S(1)} %get-tuple-element.15.own_ref) | copy-start | bytes 3145732
  84.9 64.2 %all-to-all-start.2 = ((bf16[16,4,128,256]{3,2,1,0:T(8,128)(2,1)}), bf16[16,4,128,256]{3,2,1,0:T(8,128)(2,1)}, u32[]{:S(2)}, u32[]{:S(2)}) async-start(bf16[16,4,128,256]{3,2,1,0:T(8,128)(2,1)} %get-tuple-element.18), calls=%async_computation.2 | async-start | bytes 8388608 | tf_op jit(solution)/shard_map/all_to_all | solution.py:183
  149.1 16.5 %all-to-all-start.1 = ((bf16[8,256,128]{2,1,0:T(8,128)(2,1)}), bf16[8,256,128]{2,1,0:T(8,128)(2,1)S(1)}, u32[]{:S(2)}, u32[]{:S(2)}) async-start(bf16[8,256,128]{2,1,0:T(8,128)(2,1)} %bitcast.25), calls=%async_computation.1 | async-start | bytes 1048576 | tf_op jit(solution)/shard_map/all_to_all | solution.py:210
Sparse Core Ops, SparseCore 0:
  9.1 53.3 all-gather.1

commit v2 on v1

v2 whole, which is shorter than its diff:
```python
import functools
import math

import jax
import jax.numpy as jnp
from jax import lax
from jax.experimental import pallas as pl
from jax.experimental.pallas import tpu as pltpu
from jax.sharding import PartitionSpec as P

HD = 128
TILE = 128
KT = 4
CAP = 4
BLOCK = 512
GROUP = 4
PARTS = 8
VMEM = 48 * 1024 * 1024
MOST = 60 * 1024 * 1024


def tables_kernel(me_ref, pattern_ref, chosen_ref, source_ref, *, shards, tiles):
    total = shards * tiles
    table = pattern_ref[...]
    owner = table // tiles
    local = table % tiles
    row = lax.broadcasted_iota(jnp.int32, (total, total), 0)
    col = lax.broadcasted_iota(jnp.int32, (total, total), 1)
    same = (row // tiles) == (col // tiles)
    every = same.astype(jnp.bfloat16)
    before = (same & (row < col)).astype(jnp.bfloat16)
    index = lax.broadcasted_iota(jnp.int32, (shards, total), 0)
    names = [(owner[c : c + 1] == index).astype(jnp.bfloat16) for c in range(1, KT)]
    dot = functools.partial(jnp.dot, preferred_element_type=jnp.float32)
    earlier = jnp.zeros((shards, total), jnp.float32)
    picked = [jnp.zeros((1, total), jnp.float32) for _ in range(CAP)]
    source_ref[0:1, :] = jnp.zeros((1, total), jnp.int32)
    for c in range(1, KT):
        here = names[c - 1]
        rank = jnp.sum(here.astype(jnp.float32) * (dot(here, before) + earlier), axis=0, keepdims=True)
        earlier = earlier + dot(here, every)
        rank = rank.astype(jnp.int32)
        mine = owner[c : c + 1] == me_ref[0]
        source_ref[c : c + 1, :] = owner[c : c + 1] * CAP + rank
        for k in range(CAP):
            picked[k] += jnp.where(mine & (rank == k), local[c : c + 1], 0).astype(jnp.float32)
    tile_row = lax.broadcasted_iota(jnp.int32, (total, 128), 0)
    lane = lax.broadcasted_iota(jnp.int32, (total, 128), 1)
    spread = ((tile_row // tiles) == lane).astype(jnp.bfloat16)
    for k in range(CAP):
        chosen_ref[k : k + 1, :] = dot(picked[k].astype(jnp.bfloat16), spread).astype(jnp.int32)


def project_kernel(*refs, widths, scales):
    count = len(widths)
    tokens_ref, gain_ref = refs[0], refs[1]
    weight_refs = refs[2 : 2 + count]
    out_refs = refs[2 + count : 2 + count + scales]
    scaled_ref = refs[-1]
    model = scaled_ref.shape[0]
    step = pl.program_id(0)

    @pl.when(step == 0)
    def _():
        gains = jnp.transpose(gain_ref[...])
        for j in range(model // HD):
            rows = slice(j * HD, (j + 1) * HD)
            at = 0
            for ref, width in zip(weight_refs, widths):
                part = ref[0, rows, :].astype(jnp.float32) * gains[:, j : j + 1]
                scaled_ref[rows, at : at + width] = part.astype(jnp.bfloat16)
                at += width

    tokens = tokens_ref[...]
    values = tokens.astype(jnp.float32)
    inverse = lax.rsqrt(jnp.mean(values * values, axis=-1, keepdims=True) + 1e-05)
    result = jnp.dot(tokens, scaled_ref[...], preferred_element_type=jnp.float32) * inverse
    result = result.astype(jnp.bfloat16)
    at = 0
    for ref in out_refs:
        width = ref.shape[2]
        ref[...] = result[:, at : at + width].reshape(ref.shape)
        at += width


def project(tokens, gain, weights, columns, outs):
    rows, model = tokens.shape
    tiles, count = rows // TILE, BLOCK // TILE
    widths = [n * HD for _, _, n in columns]
    return pl.pallas_call(
        functools.partial(project_kernel, widths=widths, scales=len(outs)),
        grid=(rows // BLOCK,),
        in_specs=[
            pl.BlockSpec((BLOCK, model), lambda i: (i, 0)),
            pl.BlockSpec(gain.shape, lambda i: (0, 0)),
        ]
        + [
            pl.BlockSpec((1, model, n * HD), lambda i, c=c, b=b: (c, 0, b), pipeline_mode=pl.Buffered(1))
            for c, b, n in columns
        ],
        out_specs=[pl.BlockSpec((count, TILE, width), lambda i: (i, 0, 0)) for width in outs],
        out_shape=[jax.ShapeDtypeStruct((tiles, TILE, width), jnp.bfloat16) for width in outs],
        scratch_shapes=[pltpu.VMEM((model, sum(widths)), jnp.bfloat16)],
        compiler_params=pltpu.CompilerParams(vmem_limit_bytes=MOST),
        name="project",
    )(tokens, gain, *([weights] * len(columns)))


def dispatch_kernel(chosen_ref, held_ref, send_ref, staged, semaphores, *, shards):
    copies = []
    for part in range(PARTS):
        owners = shards // PARTS
        for d in range(part * owners, (part + 1) * owners):
            for k in range(CAP):
                staged[d, k] = held_ref[chosen_ref[k, d]]
        span = pl.ds(part * owners, owners)
        copy = pltpu.make_async_copy(staged.at[span], send_ref.at[span], semaphores.at[part])
        copy.start()
        copies.append(copy)
    for copy in copies:
        copy.wait()


def dispatch(chosen, held, shards):
    shape = (shards, CAP) + held.shape[1:]
    return pl.pallas_call(
        functools.partial(dispatch_kernel, shards=shards),
        in_specs=[pl.BlockSpec(memory_space=pltpu.SMEM), pl.BlockSpec(memory_space=pltpu.VMEM)],
        out_specs=pl.BlockSpec(memory_space=pltpu.HBM),
        out_shape=jax.ShapeDtypeStruct(shape, held.dtype),
        scratch_shapes=[pltpu.VMEM(shape, held.dtype), pltpu.SemaphoreType.DMA((PARTS,))],
        compiler_params=pltpu.CompilerParams(vmem_limit_bytes=MOST),
        name="dispatch",
    )(chosen, held)


def attend_kernel(first_ref, source_ref, queries_ref, own_ref, incoming_ref, out_ref, held, semaphores, *, tiles):
    share = held.shape[0] // PARTS
    copies = []
    for part in range(PARTS):
        span = pl.ds(part * share, share)
        copies.append(pltpu.make_async_copy(incoming_ref.at[span], held.at[span], semaphores.at[part]))
        copies[-1].start()
    for copy in copies:
        copy.wait()
    scale = 1.0 / math.sqrt(HD) * math.log2(math.e)
    for start in range(0, tiles, GROUP):
        group = range(start, start + GROUP)
        blocks = [
            [own_ref.at[i]] + [held.at[source_ref[j, first_ref[0] + i]] for j in range(1, KT)] for i in group
        ]
        scores = [
            [
                lax.dot_general(
                    queries_ref[i], b[:, :HD], (((1,), (1,)), ((), ())), preferred_element_type=jnp.float32
                )
                for b in bs
            ]
            for i, bs in zip(group, blocks)
        ]
        highest = [jnp.max(functools.reduce(jnp.maximum, s), axis=-1, keepdims=True) * scale for s in scores]
        exponents = [[jnp.exp2(x * scale - m) for x in s] for s, m in zip(scores, highest)]
        totals = [jnp.sum(functools.reduce(jnp.add, e), axis=-1, keepdims=True) for e in exponents]
        for i, e, total, bs in zip(group, exponents, totals, blocks):
            weights = jnp.concatenate([x.astype(jnp.bfloat16) for x in e], axis=1)
            values = jnp.concatenate([b[:, HD:] for b in bs], axis=0)
            attended = jnp.dot(weights, values, preferred_element_type=jnp.float32)
            out_ref[i * TILE : (i + 1) * TILE, :] = (attended * (1.0 / total)).astype(jnp.bfloat16)


def attend(first, source, queries, own, incoming):
    tiles = own.shape[0]
    vmem, smem = pl.BlockSpec(memory_space=pltpu.VMEM), pl.BlockSpec(memory_space=pltpu.SMEM)
    return pl.pallas_call(
        functools.partial(attend_kernel, tiles=tiles),
        in_specs=[smem, smem, vmem, vmem, pl.BlockSpec(memory_space=pl.ANY)],
        out_specs=vmem,
        out_shape=jax.ShapeDtypeStruct((tiles * TILE, HD), jnp.bfloat16),
        scratch_shapes=[pltpu.VMEM(incoming.shape, jnp.bfloat16), pltpu.SemaphoreType.DMA((PARTS,))],
        compiler_params=pltpu.CompilerParams(vmem_limit_bytes=VMEM),
        name="attend",
    )(first, source, queries, own, incoming)


def mix_kernel(*refs, chunks):
    attended_refs, weight_refs, out_ref = refs[:chunks], refs[chunks : 2 * chunks], refs[-1]
    total = None
    for attended_ref, weight_ref in zip(attended_refs, weight_refs):
        left = jnp.concatenate([attended_ref[s] for s in range(attended_ref.shape[0])], axis=1)
        right = weight_ref[...].reshape(left.shape[1], weight_ref.shape[3])
        part = jnp.dot(left, right, preferred_element_type=jnp.float32)
        total = part if total is None else total + part
    out_ref[...] = total.astype(jnp.bfloat16)


def body(tokens, norm_gain, in_weight, out_weight, pattern):
    shards = lax.axis_size("seq")
    groups = lax.axis_size("head")
    myself = lax.axis_index("seq")
    row_count, model = tokens.shape
    tiles = row_count // TILE
    heads = in_weight.shape[2] // HD
    me = jnp.reshape(myself, (1,)).astype(jnp.int32)

    gathered = lax.all_gather(out_weight, "head", axis=0, tiled=True)

    chosen, source = pl.pallas_call(
        functools.partial(tables_kernel, shards=shards, tiles=tiles),
        in_specs=[pl.BlockSpec(memory_space=pltpu.SMEM), pl.BlockSpec(memory_space=pltpu.VMEM)],
        out_shape=[
            jax.ShapeDtypeStruct((8, 128), jnp.int32),
            jax.ShapeDtypeStruct((KT, shards * tiles), jnp.int32),
        ],
        name="tables",
    )(me, pattern.T)

    gain = norm_gain.reshape(model // HD, HD)
    weights = in_weight.transpose(1, 0, 2)
    queries, owns, incoming = [], [], []
    for h in range(heads):
        if h == 0:
            (own,) = project(tokens, gain, weights, [(1, h, 1), (2, h, 1)], [2 * HD])
        else:
            columns = [(1, h, 1), (2, h, 1)] + ([(0, 0, heads)] if h == 1 else [])
            outs = project(tokens, gain, weights, columns, [2 * HD] + [HD] * (heads if h == 1 else 0))
            own, queries = outs[0], queries + list(outs[1:])
        owns.append(own)
        send = dispatch(chosen, own, shards)
        send, tokens = lax.optimization_barrier((send, tokens))
        arrived = lax.all_to_all(send, "seq", split_axis=0, concat_axis=0, tiled=True)
        incoming.append(arrived.reshape(shards * CAP, TILE, 2 * HD))

    received = []
    for h in range(heads):
        attended = attend(me * tiles, source, queries[h], owns[h], incoming[h])
        received.append(
            lax.all_to_all(
                attended.reshape(groups, row_count // groups, HD), "head", split_axis=0, concat_axis=0, tiled=True
            )
        )

    rows = row_count // groups
    columns = 1024
    weights = gathered.reshape(groups, heads, HD, model)
    return pl.pallas_call(
        functools.partial(mix_kernel, chunks=heads),
        grid=(model // columns,),
        in_specs=[pl.BlockSpec((groups, rows, HD), lambda i: (0, 0, 0))] * heads
        + [pl.BlockSpec((groups, 1, HD, columns), lambda i, h=h: (0, h, 0, i)) for h in range(heads)],
        out_specs=pl.BlockSpec((rows, columns), lambda i: (0, i)),
        out_shape=jax.ShapeDtypeStruct((rows, model), jnp.bfloat16),
        compiler_params=pltpu.CompilerParams(vmem_limit_bytes=VMEM),
        name="mix",
    )(*received, *([weights] * heads))


def solution(mesh):
    return jax.shard_map(
        body,
        mesh=mesh,
        in_specs=(P("seq", None), P(), P(None, None, "head"), P("head", None), P()),
        out_specs=P(("seq", "head"), None),
        check_vma=False,
    )
```

time: 194 us -> 197 us (1.015)
  blocking collectives: 72.4 us -> 12.6 us
  waiting for transfers between devices: 51.1 us -> 108 us
  starting transfers between devices: 11.6 us -> 20.4 us
    all_to_all x2 -> x1, blocking collectives: 72.4 us -> 12.6 us  [body(): lax.all_to_all(attended.reshape(groups, row_count // groups, HD), 'head',...]
    all_to_all x2 -> x3, waiting for transfers between devices: 50.4 us -> 107 us  [the longest x2 103 us: body(): lax.all_to_all(send, 'seq', split_axis=0, concat_axis=0, tiled=True)]
    all_to_all x2 -> x3, starting transfers between devices: 11.6 us -> 20.4 us  [the longest x2 13.1 us: body(): lax.all_to_all(send, 'seq', split_axis=0, concat_axis=0, tiled=True)]
    pallas_call x4 -> x7, Pallas kernels: 41.2 us -> 40.3 us  [the longest x2 16.5 us: project(): pl.pallas_call(functools.partial(project_kernel, widths=widths, scales=le...]
  transfers between devices with their start and end apart: 3 -> 4, of which waited for: 2 -> 3; matrix products, arithmetic and copies ran while one was open for 0% -> 0% of each run, Pallas kernels for 19% -> 19%
where the time goes in v2:
time: 197 us; the launch traced here: 196 us
  waiting for transfers between devices  108 us (55%)
  Pallas kernels  42 us (21%)
  starting transfers between devices  20.4 us (10%)
  between operations  13.5 us (7%)
  blocking collectives  12.6 us (6%)
    all_to_all x2, waiting for transfers between devices, body(): lax.all_to_all(send, 'seq', split_axis=0, concat_axis=0, tiled=True)  103 us
    pallas_call x2, Pallas kernels, project(): pl.pallas_call(functools.partial(project_kernel, widths=widths, scales=le...  16.5 us
    all_to_all x2, starting transfers between devices, body(): lax.all_to_all(send, 'seq', split_axis=0, concat_axis=0, tiled=True)  13.1 us
    all_to_all x1, blocking collectives, body(): lax.all_to_all(attended.reshape(groups, row_count // groups, HD), 'head',...  12.6 us
    pallas_call x2, Pallas kernels, attend(): pl.pallas_call(functools.partial(attend_kernel, tiles=tiles), in_specs=[s...  11.7 us
    all_to_all x1, starting transfers between devices, body(): lax.all_to_all(attended.reshape(groups, row_count // groups, HD), 'head',...  7.3 us
    pallas_call x2, Pallas kernels, dispatch(): pl.pallas_call(functools.partial(dispatch_kernel, shards=shards), in_spec...  6.6 us
    pallas_call x1, Pallas kernels, body(): pl.pallas_call(functools.partial(mix_kernel, chunks=heads), grid=(model /...  5.58 us
  transfers between devices with their start and end apart: 4, of which 3 were waited for; matrix products, arithmetic and copies ran while one was open for 0% of the time, Pallas kernels for 19%

profile of v2, /device:TPU:1, one launch (start us, length us, event | category | flops | bytes accessed | tf_op | source)
XLA Modules:
  0.0 196.2 jit_solution(6865373879809876301)
XLA Ops:
  6.5 0.0 all-gather.2.cloned.1.call-start
  6.5 0.7 all-gather.2.cloned.1.call-update
  7.3 1.7 tables.1
  8.9 7.2 %project.2.held_ref.own_ref = bf16[16,128,256]{2,1,0:T(8,128)(2,1)} custom-call(bf16[2048,2048]{1,0:T(8,128)(2,1)} %refs_0_.2, f32[16,128]{1,0:T(8,128)} %bitcast.17, bf16[3,2048,256]{2,1,0:T(8,128)(2,1)} %bitcast.10, bf16[3,2048,256]{2,1,0:T(8,128)(2,1)} %bitcast.11), custom_call_target="tpu_custom_call" | custom-call | tf_op jit(solution)/shard_map/project/pallas_call | solution.py:90
  16.1 3.3 %dispatch.2 = bf16[16,4,128,256]{3,2,1,0:T(8,128)(2,1)} custom-call(s32[8,128]{1,0:T(8,128)} %get-tuple-element.14.chosen_ref, bf16[16,128,256]{2,1,0:T(8,128)(2,1)} %project.2.held_ref.own_ref), custom_call_target="tpu_custom_call" | custom-call | tf_op jit(solution)/shard_map/dispatch/pallas_call | solution.py:126
  19.4 8.5 %all-to-all-start = ((bf16[16,4,128,256]{3,2,1,0:T(8,128)(2,1)}), bf16[16,4,128,256]{3,2,1,0:T(8,128)(2,1)}, u32[]{:S(2)}, u32[]{:S(2)}) async-start(bf16[16,4,128,256]{3,2,1,0:T(8,128)(2,1)} %dispatch.2), calls=%async_computation | async-start | bytes 8388608 | tf_op jit(solution)/shard_map/all_to_all | solution.py:230
  28.0 9.3 %project.3 = (bf16[16,128,256]{2,1,0:T(8,128)(2,1)}, bf16[16,128,128]{2,1,0:T(8,128)(2,1)}, bf16[16,128,128]{2,1,0:T(8,128)(2,1)}) custom-call(bf16[2048,2048]{1,0:T(8,128)(2,1)} %refs_0_.2, f32[16,128]{1,0:T(8,128)} %bitcast.18, bf16[3,2048,256]{2,1,0:T(8,128)(2,1)} %bitcast.12, bf16[3,2048,256]{2,1,0:T(8,128)(2,1)} %bitcast.13, bf16[3,2048,256]{2,1,0:T(8,128)(2,1)} %bitcast.14), custom_call_target="tpu_custom_call" | custom-call | tf_op jit(solution)/shard_map/project/pallas_call | solution.py:90
  37.3 3.3 %dispatch.3 = bf16[16,4,128,256]{3,2,1,0:T(8,128)(2,1)} custom-call(s32[8,128]{1,0:T(8,128)} %get-tuple-element.14.chosen_ref, bf16[16,128,256]{2,1,0:T(8,128)(2,1)} %get-tuple-element.19.held_ref.own_ref), custom_call_target="tpu_custom_call" | custom-call | tf_op jit(solution)/shard_map/dispatch/pallas_call | solution.py:126
  40.6 0.0 copy-start
  40.6 0.0 copy-start.3
  40.6 0.0 copy-start.4
  40.6 49.7 %all-to-all-done = bf16[16,4,128,256]{3,2,1,0:T(8,128)(2,1)} async-done(((bf16[16,4,128,256]{3,2,1,0:T(8,128)(2,1)}), bf16[16,4,128,256]{3,2,1,0:T(8,128)(2,1)}, u32[]{:S(2)}, u32[]{:S(2)}) %all-to-all-start) | async-done | bytes 4194336 | tf_op jit(solution)/shard_map/all_to_all | solution.py:230
  90.3 4.5 %all-to-all-start.2 = ((bf16[16,4,128,256]{3,2,1,0:T(8,128)(2,1)}), bf16[16,4,128,256]{3,2,1,0:T(8,128)(2,1)}, u32[]{:S(2)}, u32[]{:S(2)}) async-start(bf16[16,4,128,256]{3,2,1,0:T(8,128)(2,1)} %dispatch.3), calls=%async_computation.2 | async-start | bytes 8388608 | tf_op jit(solution)/shard_map/all_to_all | solution.py:230
  94.9 0.0 copy-start.1
  94.9 0.0 copy-start.2
  94.9 0.0 copy-done
  94.9 0.0 copy-done.3
  94.9 0.0 copy-done.4
  94.9 6.2 %attend.2 = bf16[2048,128]{1,0:T(8,128)(2,1)} custom-call(s32[1]{0:T(128)S(6)} %mul.4.first_ref, s32[4,256]{1,0:T(4,128)S(1)} %copy-done.4, bf16[16,128,128]{2,1,0:T(8,128)(2,1)S(1)} %copy-done.3, bf16[16,128,256]{2,1,0:T(8,128)(2,1)S(1)} %copy-done, bf16[64,128,256]{2,1,0:T(8,128)(2,1)} %bitcast.4.incoming_ref), custom_call_target="tpu_custom_call" | custom-call | tf_op jit(solution)/shard_map/attend/pallas_call | solution.py:174
  101.2 53.2 %all-to-all-done.2 = bf16[16,4,128,256]{3,2,1,0:T(8,128)(2,1)} async-done(((bf16[16,4,128,256]{3,2,1,0:T(8,128)(2,1)}), bf16[16,4,128,256]{3,2,1,0:T(8,128)(2,1)}, u32[]{:S(2)}, u32[]{:S(2)}) %all-to-all-start.2) | async-done | bytes 4194336 | tf_op jit(solution)/shard_map/all_to_all | solution.py:230
  154.3 7.3 %all-to-all-start.1 = ((bf16[8,256,128]{2,1,0:T(8,128)(2,1)}), bf16[8,256,128]{2,1,0:T(8,128)(2,1)S(1)}, u32[]{:S(2)}, u32[]{:S(2)}) async-start(bf16[8,256,128]{2,1,0:T(8,128)(2,1)} %bitcast.5), calls=%async_computation.1 | async-start | bytes 1048576 | tf_op jit(solution)/shard_map/all_to_all | solution.py:237
  161.7 0.0 copy-done.1
  161.7 0.0 copy-done.2
  161.7 5.4 %attend.3 = bf16[2048,128]{1,0:T(8,128)(2,1)S(1)} custom-call(s32[1]{0:T(128)S(6)} %mul.4.first_ref, s32[4,256]{1,0:T(4,128)S(1)} %copy-done.4, bf16[16,128,128]{2,1,0:T(8,128)(2,1)S(1)} %copy-done.2, bf16[16,128,256]{2,1,0:T(8,128)(2,1)S(1)} %copy-done.1, bf16[64,128,256]{2,1,0:T(8,128)(2,1)} %bitcast.6.incoming_ref), custom_call_target="tpu_custom_call" | custom-call | tf_op jit(solution)/shard_map/attend/pallas_call | solution.py:174
  167.1 4.0 %all-to-all-done.1.refs_0_ = bf16[8,256,128]{2,1,0:T(8,128)(2,1)S(1)} async-done(((bf16[8,256,128]{2,1,0:T(8,128)(2,1)}), bf16[8,256,128]{2,1,0:T(8,128)(2,1)S(1)}, u32[]{:S(2)}, u32[]{:S(2)}) %all-to-all-start.1) | async-done | bytes 524320 | tf_op jit(solution)/shard_map/all_to_all | solution.py:237
  171.1 12.6 %all_to_all.20.refs_1_ = bf16[8,256,128]{2,1,0:T(8,128)(2,1)S(1)} all-to-all(bf16[8,256,128]{2,1,0:T(8,128)(2,1)S(1)} %bitcast.9), channel_id=1, replica_groups=mesh['seq'=16,'head'=8] {'head'}, dimensions={0} | all-to-all | bytes 1048576 | tf_op jit(solution)/shard_map/all_to_all | solution.py:237
  183.8 0.0 all-gather.2.cloned.1.call-done
  183.8 5.6 %mix.1 = bf16[256,2048]{1,0:T(8,128)(2,1)} custom-call(bf16[8,256,128]{2,1,0:T(8,128)(2,1)S(1)} %all-to-all-done.1.refs_0_, bf16[8,256,128]{2,1,0:T(8,128)(2,1)S(1)} %all_to_all.20.refs_1_, bf16[8,2,128,2048]{3,2,1,0:T(8,128)(2,1)} %bitcast.15, bf16[8,2,128,2048]{3,2,1,0:T(8,128)(2,1)} %bitcast.16), custom_call_target="tpu_custom_call" | custom-call | tf_op jit(solution)/shard_map/mix/pallas_call | solution.py:245
Async XLA Ops:
  6.5 177.2 %all-gather.2.cloned.1.call-start = ((), (), s32[]{:S(2)}) async-start(), calls=%async_computation.4 | async-start | bytes 9437184 | tf_op jit(solution)/shard_map/all_gather | solution.py:205
  19.4 70.9 %all-to-all-start = ((bf16[16,4,128,256]{3,2,1,0:T(8,128)(2,1)}), bf16[16,4,128,256]{3,2,1,0:T(8,128)(2,1)}, u32[]{:S(2)}, u32[]{:S(2)}) async-start(bf16[16,4,128,256]{3,2,1,0:T(8,128)(2,1)} %dispatch.2), calls=%async_computation | async-start | bytes 8388608 | tf_op jit(solution)/shard_map/all_to_all | solution.py:230
  40.6 54.3 %copy-start = (bf16[16,128,256]{2,1,0:T(8,128)(2,1)S(1)}, bf16[16,128,256]{2,1,0:T(8,128)(2,1)}, u32[]{:S(2)}) copy-start(bf16[16,128,256]{2,1,0:T(8,128)(2,1)} %project.2.held_ref.own_ref) | copy-start | bytes 3145732
  40.6 54.3 %copy-start.3 = (bf16[16,128,128]{2,1,0:T(8,128)(2,1)S(1)}, bf16[16,128,128]{2,1,0:T(8,128)(2,1)}, u32[]{:S(2)}) copy-start(bf16[16,128,128]{2,1,0:T(8,128)(2,1)} %get-tuple-element.16.queries_ref) | copy-start | bytes 1572868
  40.6 54.3 %copy-start.4 = (s32[4,256]{1,0:T(4,128)S(1)}, s32[4,256]{1,0:T(4,128)}, u32[]{:S(2)}) copy-start(s32[4,256]{1,0:T(4,128)} %get-tuple-element.13.source_ref) | copy-start | bytes 12292
  90.3 64.0 %all-to-all-start.2 = ((bf16[16,4,128,256]{3,2,1,0:T(8,128)(2,1)}), bf16[16,4,128,256]{3,2,1,0:T(8,128)(2,1)}, u32[]{:S(2)}, u32[]{:S(2)}) async-start(bf16[16,4,128,256]{3,2,1,0:T(8,128)(2,1)} %dispatch.3), calls=%async_computation.2 | async-start | bytes 8388608 | tf_op jit(solution)/shard_map/all_to_all | solution.py:230
  94.9 66.8 %copy-start.1 = (bf16[16,128,256]{2,1,0:T(8,128)(2,1)S(1)}, bf16[16,128,256]{2,1,0:T(8,128)(2,1)}, u32[]{:S(2)}) copy-start(bf16[16,128,256]{2,1,0:T(8,128)(2,1)} %get-tuple-element.19.held_ref.own_ref) | copy-start | bytes 3145732
  94.9 66.8 %copy-start.2 = (bf16[16,128,128]{2,1,0:T(8,128)(2,1)S(1)}, bf16[16,128,128]{2,1,0:T(8,128)(2,1)}, u32[]{:S(2)}) copy-start(bf16[16,128,128]{2,1,0:T(8,128)(2,1)} %get-tuple-element.18.queries_ref) | copy-start | bytes 1572868
  154.3 16.8 %all-to-all-start.1 = ((bf16[8,256,128]{2,1,0:T(8,128)(2,1)}), bf16[8,256,128]{2,1,0:T(8,128)(2,1)S(1)}, u32[]{:S(2)}, u32[]{:S(2)}) async-start(bf16[8,256,128]{2,1,0:T(8,128)(2,1)} %bitcast.5), calls=%async_computation.1 | async-start | bytes 1048576 | tf_op jit(solution)/shard_map/all_to_all | solution.py:237
Sparse Core Ops, SparseCore 0:
  9.1 53.3 all-gather.1

commit v3 on v2

v3 whole, which is shorter than its diff:
```python
import functools
import math

import jax
import jax.numpy as jnp
from jax import lax
from jax.experimental import pallas as pl
from jax.experimental.pallas import tpu as pltpu
from jax.sharding import PartitionSpec as P

HD = 128
TILE = 128
KT = 4
CAP = 4
BLOCK = 512
GROUP = 2
SIDE = 4
SHIFTS = (10, 6, 12, 14, 4, 9, 3, 11, 1, 5, 15, 7, 13, 2, 8)
FLIGHT = 5
QUERIES_AFTER = 4
VMEM = 48 * 1024 * 1024
MOST = 60 * 1024 * 1024


def shift_of(source, target):
    rows = (target // SIDE - source // SIDE + SIDE) % SIDE
    return rows * SIDE + (target % SIDE - source % SIDE + SIDE) % SIDE


def shifted(source, shift):
    return (source // SIDE + shift // SIDE) % SIDE * SIDE + (source % SIDE + shift % SIDE) % SIDE


def tables_kernel(me_ref, pattern_ref, chosen_ref, source_ref, *, shards, tiles):
    total = shards * tiles
    table = pattern_ref[...]
    owner = table // tiles
    local = table % tiles
    row = lax.broadcasted_iota(jnp.int32, (total, total), 0)
    col = lax.broadcasted_iota(jnp.int32, (total, total), 1)
    same = (row // tiles) == (col // tiles)
    every = same.astype(jnp.bfloat16)
    before = (same & (row < col)).astype(jnp.bfloat16)
    index = lax.broadcasted_iota(jnp.int32, (shards, total), 0)
    names = [(owner[c : c + 1] == index).astype(jnp.bfloat16) for c in range(1, KT)]
    dot = functools.partial(jnp.dot, preferred_element_type=jnp.float32)
    earlier = jnp.zeros((shards, total), jnp.float32)
    picked = [jnp.zeros((1, total), jnp.float32) for _ in range(CAP)]
    source_ref[0:1, :] = jnp.zeros((1, total), jnp.int32)
    for c in range(1, KT):
        here = names[c - 1]
        rank = jnp.sum(here.astype(jnp.float32) * (dot(here, before) + earlier), axis=0, keepdims=True)
        earlier = earlier + dot(here, every)
        rank = rank.astype(jnp.int32)
        mine = owner[c : c + 1] == me_ref[0]
        source_ref[c : c + 1, :] = shift_of(owner[c : c + 1], me_ref[0]) * CAP + rank
        for k in range(CAP):
            picked[k] += jnp.where(mine & (rank == k), local[c : c + 1], 0).astype(jnp.float32)
    tile_row = lax.broadcasted_iota(jnp.int32, (total, 128), 0)
    lane = lax.broadcasted_iota(jnp.int32, (total, 128), 1)
    spread = ((tile_row // tiles) == lane).astype(jnp.bfloat16)
    for k in range(CAP):
        chosen_ref[k : k + 1, :] = dot(picked[k].astype(jnp.bfloat16), spread).astype(jnp.int32)


def project_kernel(*refs, widths, scales):
    count = len(widths)
    tokens_ref, gain_ref = refs[0], refs[1]
    weight_refs = refs[2 : 2 + count]
    out_refs = refs[2 + count : 2 + count + scales]
    scaled_ref = refs[-1]
    model = scaled_ref.shape[0]
    step = pl.program_id(0)

    @pl.when(step == 0)
    def _():
        gains = jnp.transpose(gain_ref[...])
        for j in range(model // HD):
            rows = slice(j * HD, (j + 1) * HD)
            at = 0
            for ref, width in zip(weight_refs, widths):
                part = ref[0, rows, :].astype(jnp.float32) * gains[:, j : j + 1]
                scaled_ref[rows, at : at + width] = part.astype(jnp.bfloat16)
                at += width

    tokens = tokens_ref[...]
    values = tokens.astype(jnp.float32)
    inverse = lax.rsqrt(jnp.mean(values * values, axis=-1, keepdims=True) + 1e-05)
    result = jnp.dot(tokens, scaled_ref[...], preferred_element_type=jnp.float32) * inverse
    result = result.astype(jnp.bfloat16)
    at = 0
    for ref in out_refs:
        width = ref.shape[2]
        ref[...] = result[:, at : at + width].reshape(ref.shape)
        at += width


def project(tokens, gain, weights, columns, outs):
    rows, model = tokens.shape
    tiles, count = rows // TILE, BLOCK // TILE
    widths = [n * HD for _, _, n in columns]
    return pl.pallas_call(
        functools.partial(project_kernel, widths=widths, scales=len(outs)),
        grid=(rows // BLOCK,),
        in_specs=[
            pl.BlockSpec((BLOCK, model), lambda i: (i, 0)),
            pl.BlockSpec(gain.shape, lambda i: (0, 0)),
        ]
        + [
            pl.BlockSpec((1, model, n * HD), lambda i, c=c, b=b: (c, 0, b), pipeline_mode=pl.Buffered(1))
            for c, b, n in columns
        ],
        out_specs=[pl.BlockSpec((count, TILE, width), lambda i: (i, 0, 0)) for width in outs],
        out_shape=[jax.ShapeDtypeStruct((tiles, TILE, width), jnp.bfloat16) for width in outs],
        scratch_shapes=[pltpu.VMEM((model, sum(widths)), jnp.bfloat16)],
        compiler_params=pltpu.CompilerParams(vmem_limit_bytes=MOST),
        name="project",
    )(tokens, gain, *([weights] * len(columns)))


def dispatch_kernel(me_ref, chosen_ref, held_ref, *rest, shifts):
    send_refs, staged, semaphores = rest[:-2], rest[-2], rest[-1]
    copies = []
    for p, shift in enumerate(shifts):
        target = shifted(me_ref[0], shift)
        for k in range(CAP):
            staged[p, k] = held_ref[chosen_ref[k, target]]
        copies.append(pltpu.make_async_copy(staged.at[p], send_refs[p], semaphores.at[p]))
        copies[-1].start()
    for copy in copies:
        copy.wait()


def dispatch(me, chosen, held, shifts):
    shape = (CAP,) + held.shape[1:]
    smem = pl.BlockSpec(memory_space=pltpu.SMEM)
    return pl.pallas_call(
        functools.partial(dispatch_kernel, shifts=shifts),
        in_specs=[smem, smem, pl.BlockSpec(memory_space=pltpu.VMEM)],
        out_specs=[pl.BlockSpec(memory_space=pltpu.HBM)] * len(shifts),
        out_shape=[jax.ShapeDtypeStruct(shape, held.dtype)] * len(shifts),
        scratch_shapes=[
            pltpu.VMEM((len(shifts),) + shape, held.dtype),
            pltpu.SemaphoreType.DMA((len(shifts),)),
        ],
        compiler_params=pltpu.CompilerParams(vmem_limit_bytes=MOST),
        name="dispatch",
    )(me, chosen, held)


def attend_kernel(first_ref, source_ref, queries_ref, own_ref, *rest, tiles, heads):
    incoming_refs, out_ref, held, semaphores = rest[:-3], rest[-3], rest[-2], rest[-1]
    copies = []
    for p, shift in enumerate(SHIFTS):
        copies.append(
            pltpu.make_async_copy(incoming_refs[p], held.at[pl.ds(shift * CAP, CAP)], semaphores.at[p])
        )
        copies[-1].start()
    for copy in copies:
        copy.wait()
    scale = 1.0 / math.sqrt(HD) * math.log2(math.e)
    for start in range(0, tiles, GROUP):
        group = range(start, start + GROUP)
        blocks = [
            [own_ref.at[i]] + [held.at[source_ref[j, first_ref[0] + i]] for j in range(1, KT)] for i in group
        ]
        pairs = [(i, bs, h) for i, bs in zip(group, blocks) for h in range(heads)]
        scores = [
            [
                lax.dot_general(
                    queries_ref[i, :, h * HD : (h + 1) * HD],
                    b[:, h * HD : (h + 1) * HD],
                    (((1,), (1,)), ((), ())),
                    preferred_element_type=jnp.float32,
                )
                for b in bs
            ]
            for i, bs, h in pairs
        ]
        highest = [jnp.max(functools.reduce(jnp.maximum, s), axis=-1, keepdims=True) * scale for s in scores]
        exponents = [[jnp.exp2(x * scale - m) for x in s] for s, m in zip(scores, highest)]
        totals = [jnp.sum(functools.reduce(jnp.add, e), axis=-1, keepdims=True) for e in exponents]
        for (i, bs, h), e, total in zip(pairs, exponents, totals):
            weights = jnp.concatenate([x.astype(jnp.bfloat16) for x in e], axis=1)
            upper = slice((heads + h) * HD, (heads + h + 1) * HD)
            values = jnp.concatenate([b[:, upper] for b in bs], axis=0)
            attended = jnp.dot(weights, values, preferred_element_type=jnp.float32)
            out_ref[i * TILE : (i + 1) * TILE, h * HD : (h + 1) * HD] = (attended * (1.0 / total)).astype(
                jnp.bfloat16
            )


def attend(first, source, queries, own, incoming):
    tiles = own.shape[0]
    vmem, smem = pl.BlockSpec(memory_space=pltpu.VMEM), pl.BlockSpec(memory_space=pltpu.SMEM)
    return pl.pallas_call(
        functools.partial(attend_kernel, tiles=tiles, heads=queries.shape[2] // HD),
        in_specs=[smem, smem, vmem, vmem] + [pl.BlockSpec(memory_space=pl.ANY)] * len(incoming),
        out_specs=vmem,
        out_shape=jax.ShapeDtypeStruct((tiles * TILE, queries.shape[2]), jnp.bfloat16),
        scratch_shapes=[
            pltpu.VMEM((SIDE * SIDE * CAP,) + own.shape[1:], jnp.bfloat16),
            pltpu.SemaphoreType.DMA((len(incoming),)),
        ],
        compiler_params=pltpu.CompilerParams(vmem_limit_bytes=VMEM),
        name="attend",
    )(first, source, queries, own, *incoming)


def mix_kernel(attended_ref, weight_ref, out_ref):
    left = jnp.concatenate([attended_ref[s] for s in range(attended_ref.shape[0])], axis=1)
    out_ref[...] = jnp.dot(left, weight_ref[...], preferred_element_type=jnp.float32).astype(jnp.bfloat16)


def body(tokens, norm_gain, in_weight, out_weight, pattern):
    shards = lax.axis_size("seq")
    groups = lax.axis_size("head")
    myself = lax.axis_index("seq")
    row_count, model = tokens.shape
    tiles = row_count // TILE
    width = in_weight.shape[2]
    heads = width // HD
    me = jnp.reshape(myself, (1,)).astype(jnp.int32)

    gathered = lax.all_gather(out_weight, "head", axis=0, tiled=True)

    chosen, source = pl.pallas_call(
        functools.partial(tables_kernel, shards=shards, tiles=tiles),
        in_specs=[pl.BlockSpec(memory_space=pltpu.SMEM), pl.BlockSpec(memory_space=pltpu.VMEM)],
        out_shape=[
            jax.ShapeDtypeStruct((8, 128), jnp.int32),
            jax.ShapeDtypeStruct((KT, shards * tiles), jnp.int32),
        ],
        name="tables",
    )(me, pattern.T)

    gain = norm_gain.reshape(model // HD, HD)
    weights = in_weight.transpose(1, 0, 2)
    (own,) = project(tokens, gain, weights, [(1, 0, heads), (2, 0, heads)], [2 * width])
    sends = list(dispatch(me, chosen, own, SHIFTS[:FLIGHT]))
    incoming = []
    for p, shift in enumerate(SHIFTS):
        if p == FLIGHT:
            held, incoming[0] = lax.optimization_barrier((own, incoming[0]))
            sends += list(dispatch(me, chosen, held, SHIFTS[FLIGHT:]))
        send = sends[p]
        if p >= FLIGHT:
            send, incoming[p - FLIGHT] = lax.optimization_barrier((send, incoming[p - FLIGHT]))
        incoming.append(lax.ppermute(send, "seq", [(s, shifted(s, shift)) for s in range(shards)]))
    tokens, incoming[QUERIES_AFTER] = lax.optimization_barrier((tokens, incoming[QUERIES_AFTER]))
    (queries,) = project(tokens, gain, weights, [(0, 0, heads)], [width])
    attended = attend(me * tiles, source, queries, own, incoming)
    rows = row_count // groups
    attended = lax.all_to_all(
        attended.reshape(groups, rows, width), "head", split_axis=0, concat_axis=0, tiled=True
    )
    columns = 1024
    return pl.pallas_call(
        mix_kernel,
        grid=(model // columns,),
        in_specs=[
            pl.BlockSpec((groups, rows, width), lambda i: (0, 0, 0)),
            pl.BlockSpec((groups * width, columns), lambda i: (0, i)),
        ],
        out_specs=pl.BlockSpec((rows, columns), lambda i: (0, i)),
        out_shape=jax.ShapeDtypeStruct((rows, model), jnp.bfloat16),
        compiler_params=pltpu.CompilerParams(vmem_limit_bytes=VMEM),
        name="mix",
    )(attended, gathered)


def solution(mesh):
    return jax.shard_map(
        body,
        mesh=mesh,
        in_specs=(P("seq", None), P(), P(None, None, "head"), P("head", None), P()),
        out_specs=P(("seq", "head"), None),
        check_vma=False,
    )
```

time: 197 us -> 196 us (level)
  the two profiles are of different devices: /device:TPU:1 before, /device:TPU:7 now
where the time goes in v3:
time: 196 us; the launch traced here: 194 us
  waiting for transfers between devices  87.1 us (44%)
  Pallas kernels  41 us (21%)
  starting transfers between devices  26.4 us (13%)
  blocking collectives  20.6 us (11%)
  between operations  13.5 us (7%)
  local copies, waits for them, and re-layouts  5.54 us (3%)
    ppermute x15, waiting for transfers between devices, body(): lax.ppermute(send, 'seq', [(s, shifted(s, shift)) for s in range(shards)])  86.4 us
    ppermute x15, starting transfers between devices, body(): lax.ppermute(send, 'seq', [(s, shifted(s, shift)) for s in range(shards)])  26.3 us
    all_to_all x1, blocking collectives, body(): lax.all_to_all(attended.reshape(groups, rows, width), 'head', split_axis=...  20.6 us
    pallas_call x2, Pallas kernels, project(): pl.pallas_call(functools.partial(project_kernel, widths=widths, scales=le...  16.4 us
    pallas_call x1, Pallas kernels, attend(): pl.pallas_call(functools.partial(attend_kernel, tiles=tiles, heads=querie...  10.1 us
    pallas_call x2, Pallas kernels, dispatch(): pl.pallas_call(functools.partial(dispatch_kernel, shifts=shifts), in_spec...  7.28 us
    unnamed x14, local copies, waits for them, and re-layouts  5.54 us
    pallas_call x1, Pallas kernels, body(): pl.pallas_call(mix_kernel, grid=(model // columns,), in_specs=[pl.BlockSp...  5.51 us
  transfers between devices with their start and end apart: 16, of which 9 were waited for; matrix products, arithmetic and copies ran while one was open for 0% of the time, Pallas kernels for 18%

profile of v3, /device:TPU:7, one launch (start us, length us, event | category | flops | bytes accessed | tf_op | source)
XLA Modules:
  0.0 194.0 jit_solution(2393253094514006680)
XLA Ops:
  6.5 0.0 all-gather.2.cloned.1.call-start
  6.5 0.7 all-gather.2.cloned.1.call-update
  7.3 1.7 tables.1
  9.0 9.2 %project.2.held_ref.own_ref = bf16[16,128,512]{2,1,0:T(8,128)(2,1)} custom-call(bf16[2048,2048]{1,0:T(8,128)(2,1)} %refs_0_.2, f32[16,128]{1,0:T(8,128)} %bitcast.9, bf16[3,2048,256]{2,1,0:T(8,128)(2,1)} %bitcast.5, bf16[3,2048,256]{2,1,0:T(8,128)(2,1)} %bitcast.6), custom_call_target="tpu_custom_call" | custom-call | tf_op jit(solution)/shard_map/project/pallas_call | solution.py:102
  18.2 0.0 copy-start.6
  18.2 3.2 %dispatch.2 = (bf16[4,128,512]{2,1,0:T(8,128)(2,1)}, bf16[4,128,512]{2,1,0:T(8,128)(2,1)}, bf16[4,128,512]{2,1,0:T(8,128)(2,1)}, bf16[4,128,512]{2,1,0:T(8,128)(2,1)}, bf16[4,128,512]{2,1,0:T(8,128)(2,1)}) custom-call(s32[1]{0:T(128)} %bitcast.me_ref, s32[8,128]{1,0:T(8,128)} %get-tuple-element.47.chosen_ref, bf16[16,128,512]{2,1,0:T(8,128)(2,1)} %project.2.held_ref.own_ref), custom_call_target="tpu_custom_call" | custom-call | tf_op jit(solution)/shard_map/dispatch/pallas_call | solution.py:137
  21.4 4.5 %collective-permute-start = (bf16[4,128,512]{2,1,0:T(8,128)(2,1)}, bf16[4,128,512]{2,1,0:T(8,128)(2,1)S(1)}, u32[]{:S(2)}, u32[]{:S(2)}) collective-permute-start(bf16[4,128,512]{2,1,0:T(8,128)(2,1)} %get-tuple-element.48), channel_id=1, source_target_pairs={{0,80},{8,88},{16,64},{24,72},{32,112},{40,120},{48,96},{56,104},{... | collective-permute-start | bytes 1572872 | tf_op jit(solution)/shard_map/ppermute | solution.py:249
  25.9 0.9 collective-permute-start.1
  26.8 3.4 %collective-permute-start.4 = (bf16[4,128,512]{2,1,0:T(8,128)(2,1)}, bf16[4,128,512]{2,1,0:T(8,128)(2,1)S(1)}, u32[]{:S(2)}, u32[]{:S(2)}) collective-permute-start(bf16[4,128,512]{2,1,0:T(8,128)(2,1)} %get-tuple-element.64), channel_id=1, source_target_pairs={{0,112},{8,120},{16,96},{24,104},{32,16},{40,24},{48,0},{56,8},{64... | collective-permute-start | bytes 1572872 | tf_op jit(solution)/shard_map/ppermute | solution.py:249
  30.2 0.0 collective-permute-start.3
  30.2 2.3 %collective-permute-start.2 = (bf16[4,128,512]{2,1,0:T(8,128)(2,1)}, bf16[4,128,512]{2,1,0:T(8,128)(2,1)S(1)}, u32[]{:S(2)}, u32[]{:S(2)}) collective-permute-start(bf16[4,128,512]{2,1,0:T(8,128)(2,1)} %get-tuple-element.58), channel_id=1, source_target_pairs={{0,48},{8,56},{16,32},{24,40},{32,80},{40,88},{48,64},{56,72},{64,... | collective-permute-start | bytes 1572872 | tf_op jit(solution)/shard_map/ppermute | solution.py:249
  32.5 5.9 %collective-permute-done.rest_0_ = bf16[4,128,512]{2,1,0:T(8,128)(2,1)S(1)} collective-permute-done((bf16[4,128,512]{2,1,0:T(8,128)(2,1)}, bf16[4,128,512]{2,1,0:T(8,128)(2,1)S(1)}, u32[]{:S(2)}, u32[]{:S(2)}) %collective-permute-start) | collective-permute-done | bytes 524320 | tf_op jit(solution)/shard_map/ppermute | solution.py:249
  38.4 4.1 %dispatch.3 = (bf16[4,128,512]{2,1,0:T(8,128)(2,1)}, bf16[4,128,512]{2,1,0:T(8,128)(2,1)}, bf16[4,128,512]{2,1,0:T(8,128)(2,1)}, bf16[4,128,512]{2,1,0:T(8,128)(...) custom-call(s32[1]{0:T(128)} %bitcast.me_ref, ...), custom_call_target="tpu_custom_call" | custom-call | tf_op jit(solution)/shard_map/dispatch/pallas_call | solution.py:137
  42.5 3.4 %collective-permute-start.5 = (bf16[4,128,512]{2,1,0:T(8,128)(2,1)}, bf16[4,128,512]{2,1,0:T(8,128)(2,1)S(1)}, u32[]{:S(2)}, u32[]{:S(2)}) collective-permute-start(bf16[4,128,512]{2,1,0:T(8,128)(2,1)} %get-tuple-element.68), channel_id=1, source_target_pairs={{0,72},{8,80},{16,88},{24,64},{32,104},{40,112},{48,120},{56,96},{... | collective-permute-start | bytes 1572872 | tf_op jit(solution)/shard_map/ppermute | solution.py:249
  45.9 5.0 %collective-permute-done.1.rest_4_ = bf16[4,128,512]{2,1,0:T(8,128)(2,1)S(1)} collective-permute-done((bf16[4,128,512]{2,1,0:T(8,128)(2,1)}, bf16[4,128,512]{2,1,0:T(8,128)(2,1)S(1)}, u32[]{:S(2)}, u32[]{:S(2)}) %collective-permute-start.1) | collective-permute-done | bytes 524320 | tf_op jit(solution)/shard_map/ppermute | solution.py:249
  50.9 2.5 %collective-permute-start.9 = (bf16[4,128,512]{2,1,0:T(8,128)(2,1)}, bf16[4,128,512]{2,1,0:T(8,128)(2,1)S(1)}, u32[]{:S(2)}, u32[]{:S(2)}) collective-permute-start(bf16[4,128,512]{2,1,0:T(8,128)(2,1)} %get-tuple-element.80), channel_id=1, source_target_pairs={{0,40},{8,48},{16,56},{24,32},{32,72},{40,80},{48,88},{56,64},{64,... | collective-permute-start | bytes 1572872 | tf_op jit(solution)/shard_map/ppermute | solution.py:249
  53.4 0.0 collective-permute-done.4.rest_3_
  53.4 1.1 collective-permute-start.8
  54.5 20.1 %collective-permute-done.3.rest_2_ = bf16[4,128,512]{2,1,0:T(8,128)(2,1)S(1)} collective-permute-done((bf16[4,128,512]{2,1,0:T(8,128)(2,1)}, bf16[4,128,512]{2,1,0:T(8,128)(2,1)S(1)}, u32[]{:S(2)}, u32[]{:S(2)}) %collective-permute-start.3) | collective-permute-done | bytes 524320 | tf_op jit(solution)/shard_map/ppermute | solution.py:249
  74.6 0.0 collective-permute-start.7
  74.6 0.0 collective-permute-done.2.rest_1_
  74.6 0.0 collective-permute-start.6
  74.6 1.5 collective-permute-done.5.rest_5_
  76.2 1.2 collective-permute-start.10
  77.3 18.2 %collective-permute-done.9.rest_9_ = bf16[4,128,512]{2,1,0:T(8,128)(2,1)S(1)} collective-permute-done((bf16[4,128,512]{2,1,0:T(8,128)(2,1)}, bf16[4,128,512]{2,1,0:T(8,128)(2,1)S(1)}, u32[]{:S(2)}, u32[]{:S(2)}) %collective-permute-start.9) | collective-permute-done | bytes 524320 | tf_op jit(solution)/shard_map/ppermute | solution.py:249
  95.5 0.0 collective-permute-start.14
  95.5 11.2 %collective-permute-done.8.rest_8_ = bf16[4,128,512]{2,1,0:T(8,128)(2,1)S(1)} collective-permute-done((bf16[4,128,512]{2,1,0:T(8,128)(2,1)}, bf16[4,128,512]{2,1,0:T(8,128)(2,1)S(1)}, u32[]{:S(2)}, u32[]{:S(2)}) %collective-permute-start.8) | collective-permute-done | bytes 524320 | tf_op jit(solution)/shard_map/ppermute | solution.py:249
  106.8 0.8 copy-done
  107.6 4.7 %collective-permute-start.13 = (bf16[4,128,512]{2,1,0:T(8,128)(2,1)}, bf16[4,128,512]{2,1,0:T(8,128)(2,1)}, u32[]{:S(2)}, u32[]{:S(2)}) collective-permute-start(bf16[4,128,512]{2,1,0:T(8,128)(2,1)} %get-tuple-element.85), channel_id=1, source_target_pairs={{0,16},{8,24},{16,0},{24,8},{32,48},{40,56},{48,32},{56,40},{64,80... | collective-permute-start | bytes 1572872 | tf_op jit(solution)/shard_map/ppermute | solution.py:249
  112.3 0.0 collective-permute-done.7.rest_7_
  112.3 0.8 copy-done.2
  113.1 0.0 collective-permute-start.12
  113.1 0.0 collective-permute-done.6.rest_6_
  113.1 0.8 copy-done.4
  113.9 2.4 %collective-permute-start.11 = (bf16[4,128,512]{2,1,0:T(8,128)(2,1)}, bf16[4,128,512]{2,1,0:T(8,128)(2,1)}, u32[]{:S(2)}, u32[]{:S(2)}) collective-permute-start(bf16[4,128,512]{2,1,0:T(8,128)(2,1)} %get-tuple-element.83), channel_id=1, source_target_pairs={{0,56},{8,32},{16,40},{24,48},{32,88},{40,64},{48,72},{56,80},{64,... | collective-permute-start | bytes 1572872 | tf_op jit(solution)/shard_map/ppermute | solution.py:249
  116.2 7.2 %project.3.queries_ref = bf16[16,128,256]{2,1,0:T(8,128)(2,1)} custom-call(bf16[2048,2048]{1,0:T(8,128)(2,1)} %refs_0_.2, f32[16,128]{1,0:T(8,128)} %bitcast.10, bf16[3,2048,256]{2,1,0:T(8,128)(2,1)} %bitcast.7), custom_call_target="tpu_custom_call" | custom-call | tf_op jit(solution)/shard_map/project/pallas_call | solution.py:102
  123.4 2.3 %collective-permute-done.10.rest_10_ = bf16[4,128,512]{2,1,0:T(8,128)(2,1)} collective-permute-done((bf16[4,128,512]{2,1,0:T(8,128)(2,1)}, bf16[4,128,512]{2,1,0:T(8,128)(2,1)}, u32[]{:S(2)}, u32[]{:S(2)}) %collective-permute-start.10) | collective-permute-done | bytes 524320 | tf_op jit(solution)/shard_map/ppermute | solution.py:249
  125.8 0.0 collective-permute-done.14.rest_14_
  125.8 10.8 %collective-permute-done.13.rest_13_ = bf16[4,128,512]{2,1,0:T(8,128)(2,1)} collective-permute-done((bf16[4,128,512]{2,1,0:T(8,128)(2,1)}, bf16[4,128,512]{2,1,0:T(8,128)(2,1)}, u32[]{:S(2)}, u32[]{:S(2)}) %collective-permute-start.13) | collective-permute-done | bytes 524320 | tf_op jit(solution)/shard_map/ppermute | solution.py:249
  136.6 0.0 collective-permute-done.12.rest_12_
  136.6 11.2 %collective-permute-done.11.rest_11_ = bf16[4,128,512]{2,1,0:T(8,128)(2,1)} collective-permute-done((bf16[4,128,512]{2,1,0:T(8,128)(2,1)}, bf16[4,128,512]{2,1,0:T(8,128)(2,1)}, u32[]{:S(2)}, u32[]{:S(2)}) %collective-permute-start.11) | collective-permute-done | bytes 524320 | tf_op jit(solution)/shard_map/ppermute | solution.py:249
  147.8 0.0 copy-done.6
  147.8 1.0 copy-done.1
  148.9 1.0 copy-done.3
  149.9 1.0 copy-done.5
  151.0 10.1 %attend.1 = bf16[2048,256]{1,0:T(8,128)(2,1)} custom-call(s32[1]{0:T(128)S(6)} %mul.3.first_ref, s32[4,256]{1,0:T(4,128)S(1)} %copy-done.6, bf16[16,128,256]{2,1,0:T(8,128)(2,1)} %project.3.queries_ref, bf16[16,128,512]{2,1,0:T(8,128)(2,1)} %project.2.held_ref.own_ref, bf16[4,128,512]{2,1,0:T(8,128)(2,1)S(1)} %collective-permute-done.rest_0_, ...), custom_call_target="tpu_custom_call" | custom-call | tf_op jit(solution)/shard_map/attend/pallas_call | solution.py:196
  161.0 20.6 %all_to_all.5.attended_ref = bf16[8,256,256]{2,1,0:T(8,128)(2,1)S(1)} all-to-all(bf16[8,256,256]{2,1,0:T(8,128)(2,1)} %bitcast.8), channel_id=1, replica_groups=mesh['seq'=16,'head'=8] {'head'}, dimensions={0} | all-to-all | bytes 2097152 | tf_op jit(solution)/shard_map/all_to_all | solution.py:254
  181.7 5.5 %mix.1 = bf16[256,2048]{1,0:T(8,128)(2,1)} custom-call(bf16[8,256,256]{2,1,0:T(8,128)(2,1)S(1)} %all_to_all.5.attended_ref, bf16[2048,2048]{1,0:T(8,128)(2,1)} %all-gather.2.cloned.1.call-done.weight_ref), custom_call_target="tpu_custom_call" | custom-call | tf_op jit(solution)/shard_map/mix/pallas_call | solution.py:258
  (7 shorter events, 0.0 us)
Async XLA Ops:
  6.5 175.1 %all-gather.2.cloned.1.call-start = ((), (), s32[]{:S(2)}) async-start(), calls=%async_computation.1 | async-start | bytes 9437184 | tf_op jit(solution)/shard_map/all_gather | solution.py:225
  18.2 129.6 %copy-start.6 = (s32[4,256]{1,0:T(4,128)S(1)}, s32[4,256]{1,0:T(4,128)}, u32[]{:S(2)}) copy-start(s32[4,256]{1,0:T(4,128)} %get-tuple-element.46.source_ref) | copy-start | bytes 12292
  21.4 17.0 %collective-permute-start = (bf16[4,128,512]{2,1,0:T(8,128)(2,1)}, bf16[4,128,512]{2,1,0:T(8,128)(2,1)S(1)}, u32[]{:S(2)}, u32[]{:S(2)}) collective-permute-start(bf16[4,128,512]{2,1,0:T(8,128)(2,1)} %get-tuple-element.48), channel_id=1, source_target_pairs={{0,80},{8,88},{16,64},{24,72},{32,112},{40,120},{48,96},{56,104},{... | collective-permute-start | bytes 1572872 | tf_op jit(solution)/shard_map/ppermute | solution.py:249
  25.9 25.0 %collective-permute-start.1 = (bf16[4,128,512]{2,1,0:T(8,128)(2,1)}, bf16[4,128,512]{2,1,0:T(8,128)(2,1)S(1)}, u32[]{:S(2)}, u32[]{:S(2)}) collective-permute-start(bf16[4,128,512]{2,1,0:T(8,128)(2,1)} %get-tuple-element.51), channel_id=1, source_target_pairs={{0,32},{8,40},{16,48},{24,56},{32,64},{40,72},{48,80},{56,88},{64,... | collective-permute-start | bytes 1572872 | tf_op jit(solution)/shard_map/ppermute | solution.py:249
  26.8 26.6 %collective-permute-start.4 = (bf16[4,128,512]{2,1,0:T(8,128)(2,1)}, bf16[4,128,512]{2,1,0:T(8,128)(2,1)S(1)}, u32[]{:S(2)}, u32[]{:S(2)}) collective-permute-start(bf16[4,128,512]{2,1,0:T(8,128)(2,1)} %get-tuple-element.64), channel_id=1, source_target_pairs={{0,112},{8,120},{16,96},{24,104},{32,16},{40,24},{48,0},{56,8},{64... | collective-permute-start | bytes 1572872 | tf_op jit(solution)/shard_map/ppermute | solution.py:249
  30.2 44.5 %collective-permute-start.3 = (bf16[4,128,512]{2,1,0:T(8,128)(2,1)}, bf16[4,128,512]{2,1,0:T(8,128)(2,1)S(1)}, u32[]{:S(2)}, u32[]{:S(2)}) collective-permute-start(bf16[4,128,512]{2,1,0:T(8,128)(2,1)} %get-tuple-element.61), channel_id=1, source_target_pairs={{0,96},{8,104},{16,112},{24,120},{32,0},{40,8},{48,16},{56,24},{64... | collective-permute-start | bytes 1572872 | tf_op jit(solution)/shard_map/ppermute | solution.py:249
  30.2 44.5 %collective-permute-start.2 = (bf16[4,128,512]{2,1,0:T(8,128)(2,1)}, bf16[4,128,512]{2,1,0:T(8,128)(2,1)S(1)}, u32[]{:S(2)}, u32[]{:S(2)}) collective-permute-start(bf16[4,128,512]{2,1,0:T(8,128)(2,1)} %get-tuple-element.58), channel_id=1, source_target_pairs={{0,48},{8,56},{16,32},{24,40},{32,80},{40,88},{48,64},{56,72},{64,... | collective-permute-start | bytes 1572872 | tf_op jit(solution)/shard_map/ppermute | solution.py:249
  42.5 33.7 %collective-permute-start.5 = (bf16[4,128,512]{2,1,0:T(8,128)(2,1)}, bf16[4,128,512]{2,1,0:T(8,128)(2,1)S(1)}, u32[]{:S(2)}, u32[]{:S(2)}) collective-permute-start(bf16[4,128,512]{2,1,0:T(8,128)(2,1)} %get-tuple-element.68), channel_id=1, source_target_pairs={{0,72},{8,80},{16,88},{24,64},{32,104},{40,112},{48,120},{56,96},{... | collective-permute-start | bytes 1572872 | tf_op jit(solution)/shard_map/ppermute | solution.py:249
  50.9 44.7 %collective-permute-start.9 = (bf16[4,128,512]{2,1,0:T(8,128)(2,1)}, bf16[4,128,512]{2,1,0:T(8,128)(2,1)S(1)}, u32[]{:S(2)}, u32[]{:S(2)}) collective-permute-start(bf16[4,128,512]{2,1,0:T(8,128)(2,1)} %get-tuple-element.80), channel_id=1, source_target_pairs={{0,40},{8,48},{16,56},{24,32},{32,72},{40,80},{48,88},{56,64},{64,... | collective-permute-start | bytes 1572872 | tf_op jit(solution)/shard_map/ppermute | solution.py:249
  53.4 53.4 %collective-permute-start.8 = (bf16[4,128,512]{2,1,0:T(8,128)(2,1)}, bf16[4,128,512]{2,1,0:T(8,128)(2,1)S(1)}, u32[]{:S(2)}, u32[]{:S(2)}) collective-permute-start(bf16[4,128,512]{2,1,0:T(8,128)(2,1)} %get-tuple-element.77), channel_id=1, source_target_pairs={{0,8},{8,16},{16,24},{24,0},{32,40},{40,48},{48,56},{56,32},{64,72... | collective-permute-start | bytes 1572872 | tf_op jit(solution)/shard_map/ppermute | solution.py:249
  74.6 37.6 %collective-permute-start.7 = (bf16[4,128,512]{2,1,0:T(8,128)(2,1)}, bf16[4,128,512]{2,1,0:T(8,128)(2,1)S(1)}, u32[]{:S(2)}, u32[]{:S(2)}) collective-permute-start(bf16[4,128,512]{2,1,0:T(8,128)(2,1)} %get-tuple-element.74), channel_id=1, source_target_pairs={{0,88},{8,64},{16,72},{24,80},{32,120},{40,96},{48,104},{56,112},{... | collective-permute-start | bytes 1572872 | tf_op jit(solution)/shard_map/ppermute | solution.py:249
  74.6 38.4 %collective-permute-start.6 = (bf16[4,128,512]{2,1,0:T(8,128)(2,1)}, bf16[4,128,512]{2,1,0:T(8,128)(2,1)S(1)}, u32[]{:S(2)}, u32[]{:S(2)}) collective-permute-start(bf16[4,128,512]{2,1,0:T(8,128)(2,1)} %get-tuple-element.71), channel_id=1, source_target_pairs={{0,24},{8,0},{16,8},{24,16},{32,56},{40,32},{48,40},{56,48},{64,88... | collective-permute-start | bytes 1572872 | tf_op jit(solution)/shard_map/ppermute | solution.py:249
  76.2 49.6 %collective-permute-start.10 = (bf16[4,128,512]{2,1,0:T(8,128)(2,1)}, bf16[4,128,512]{2,1,0:T(8,128)(2,1)}, u32[]{:S(2)}, u32[]{:S(2)}) collective-permute-start(bf16[4,128,512]{2,1,0:T(8,128)(2,1)} %get-tuple-element.82), channel_id=1, source_target_pairs={{0,120},{8,96},{16,104},{24,112},{32,24},{40,0},{48,8},{56,16},{64... | collective-permute-start | bytes 1572872 | tf_op jit(solution)/shard_map/ppermute | solution.py:249
  95.5 30.3 %collective-permute-start.14 = (bf16[4,128,512]{2,1,0:T(8,128)(2,1)}, bf16[4,128,512]{2,1,0:T(8,128)(2,1)}, u32[]{:S(2)}, u32[]{:S(2)}) collective-permute-start(bf16[4,128,512]{2,1,0:T(8,128)(2,1)} %get-tuple-element.86), channel_id=1, source_target_pairs={{0,64},{8,72},{16,80},{24,88},{32,96},{40,104},{48,112},{56,120},{... | collective-permute-start | bytes 1572872 | tf_op jit(solution)/shard_map/ppermute | solution.py:249
  106.8 0.8 copy-start
  107.6 29.0 %collective-permute-start.13 = (bf16[4,128,512]{2,1,0:T(8,128)(2,1)}, bf16[4,128,512]{2,1,0:T(8,128)(2,1)}, u32[]{:S(2)}, u32[]{:S(2)}) collective-permute-start(bf16[4,128,512]{2,1,0:T(8,128)(2,1)} %get-tuple-element.85), channel_id=1, source_target_pairs={{0,16},{8,24},{16,0},{24,8},{32,48},{40,56},{48,32},{56,40},{64,80... | collective-permute-start | bytes 1572872 | tf_op jit(solution)/shard_map/ppermute | solution.py:249
  112.3 0.8 copy-start.2
  113.1 23.5 %collective-permute-start.12 = (bf16[4,128,512]{2,1,0:T(8,128)(2,1)}, bf16[4,128,512]{2,1,0:T(8,128)(2,1)}, u32[]{:S(2)}, u32[]{:S(2)}) collective-permute-start(bf16[4,128,512]{2,1,0:T(8,128)(2,1)} %get-tuple-element.84), channel_id=1, source_target_pairs={{0,104},{8,112},{16,120},{24,96},{32,8},{40,16},{48,24},{56,0},{64... | collective-permute-start | bytes 1572872 | tf_op jit(solution)/shard_map/ppermute | solution.py:249
  113.1 0.8 copy-start.4
  113.9 33.9 %collective-permute-start.11 = (bf16[4,128,512]{2,1,0:T(8,128)(2,1)}, bf16[4,128,512]{2,1,0:T(8,128)(2,1)}, u32[]{:S(2)}, u32[]{:S(2)}) collective-permute-start(bf16[4,128,512]{2,1,0:T(8,128)(2,1)} %get-tuple-element.83), channel_id=1, source_target_pairs={{0,56},{8,32},{16,40},{24,48},{32,88},{40,64},{48,72},{56,80},{64,... | collective-permute-start | bytes 1572872 | tf_op jit(solution)/shard_map/ppermute | solution.py:249
  147.8 1.0 copy-start.1
  148.9 1.0 copy-start.3
  149.9 1.0 copy-start.5
Sparse Core Ops, SparseCore 0:
  9.1 52.4 all-gather.1

commit v4 on v3

--- a/solution.py
+++ b/solution.py
@@ -15,11 +15,12 @@
 BLOCK = 512
 GROUP = 2
 SIDE = 4
-SHIFTS = (10, 6, 12, 14, 4, 9, 3, 11, 1, 5, 15, 7, 13, 2, 8)
-FLIGHT = 5
-QUERIES_AFTER = 4
-VMEM = 48 * 1024 * 1024
+SHIFTS = (10, 6, 12, 14, 4, 3, 11, 1, 5, 15, 9, 7, 13, 2, 8)
+LATE = 10
+COLUMNS = 1024
+VMEM = 60 * 1024 * 1024
 MOST = 60 * 1024 * 1024
+LEAST = 16 * 1024 * 1024
 
 
 def shift_of(source, target):
@@ -95,7 +96,7 @@
         at += width
 
 
-def project(tokens, gain, weights, columns, outs):
+def project(tokens, gain, weights, columns, outs, limit):
     rows, model = tokens.shape
     tiles, count = rows // TILE, BLOCK // TILE
     widths = [n * HD for _, _, n in columns]
@@ -113,7 +114,7 @@
         out_specs=[pl.BlockSpec((count, TILE, width), lambda i: (i, 0, 0)) for width in outs],
         out_shape=[jax.ShapeDtypeStruct((tiles, TILE, width), jnp.bfloat16) for width in outs],
         scratch_shapes=[pltpu.VMEM((model, sum(widths)), jnp.bfloat16)],
-        compiler_params=pltpu.CompilerParams(vmem_limit_bytes=MOST),
+        compiler_params=pltpu.CompilerParams(vmem_limit_bytes=limit),
         name="project",
     )(tokens, gain, *([weights] * len(columns)))
 
@@ -148,8 +149,8 @@
     )(me, chosen, held)
 
 
-def attend_kernel(first_ref, source_ref, queries_ref, own_ref, *rest, tiles, heads):
-    incoming_refs, out_ref, held, semaphores = rest[:-3], rest[-3], rest[-2], rest[-1]
+def attend_kernel(first_ref, source_ref, queries_ref, own_ref, *rest, tiles, heads, pairs):
+    incoming_refs, out_refs, held, semaphores = rest[: -2 - pairs], rest[-2 - pairs : -2], rest[-2], rest[-1]
     copies = []
     for p, shift in enumerate(SHIFTS):
         copies.append(
@@ -159,45 +160,48 @@
     for copy in copies:
         copy.wait()
     scale = 1.0 / math.sqrt(HD) * math.log2(math.e)
+    share = tiles // pairs
     for start in range(0, tiles, GROUP):
-        group = range(start, start + GROUP)
+        block = (first_ref[1] + start // share) % pairs * share
+        group = [block + (start + g) % share for g in range(GROUP)]
         blocks = [
             [own_ref.at[i]] + [held.at[source_ref[j, first_ref[0] + i]] for j in range(1, KT)] for i in group
         ]
-        pairs = [(i, bs, h) for i, bs in zip(group, blocks) for h in range(heads)]
+        work = [(g, h) for g in range(GROUP) for h in range(heads)]
         scores = [
             [
                 lax.dot_general(
-                    queries_ref[i, :, h * HD : (h + 1) * HD],
+                    queries_ref[group[g], :, h * HD : (h + 1) * HD],
                     b[:, h * HD : (h + 1) * HD],
                     (((1,), (1,)), ((), ())),
                     preferred_element_type=jnp.float32,
                 )
-                for b in bs
+                for b in blocks[g]
             ]
-            for i, bs, h in pairs
+            for g, h in work
         ]
         highest = [jnp.max(functools.reduce(jnp.maximum, s), axis=-1, keepdims=True) * scale for s in scores]
         exponents = [[jnp.exp2(x * scale - m) for x in s] for s, m in zip(scores, highest)]
         totals = [jnp.sum(functools.reduce(jnp.add, e), axis=-1, keepdims=True) for e in exponents]
-        for (i, bs, h), e, total in zip(pairs, exponents, totals):
+        for (g, h), e, total in zip(work, exponents, totals):
             weights = jnp.concatenate([x.astype(jnp.bfloat16) for x in e], axis=1)
             upper = slice((heads + h) * HD, (heads + h + 1) * HD)
-            values = jnp.concatenate([b[:, upper] for b in bs], axis=0)
+            values = jnp.concatenate([b[:, upper] for b in blocks[g]], axis=0)
             attended = jnp.dot(weights, values, preferred_element_type=jnp.float32)
-            out_ref[i * TILE : (i + 1) * TILE, h * HD : (h + 1) * HD] = (attended * (1.0 / total)).astype(
-                jnp.bfloat16
-            )
-
-
-def attend(first, source, queries, own, incoming):
+            row = (start + g) % share * TILE
+            out_refs[start // share][row : row + TILE, h * HD : (h + 1) * HD] = (
+                attended * (1.0 / total)
+            ).astype(jnp.bfloat16)
+
+
+def attend(first, source, queries, own, incoming, pairs):
     tiles = own.shape[0]
     vmem, smem = pl.BlockSpec(memory_space=pltpu.VMEM), pl.BlockSpec(memory_space=pltpu.SMEM)
     return pl.pallas_call(
-        functools.partial(attend_kernel, tiles=tiles, heads=queries.shape[2] // HD),
+        functools.partial(attend_kernel, tiles=tiles, heads=queries.shape[2] // HD, pairs=pairs),
         in_specs=[smem, smem, vmem, vmem] + [pl.BlockSpec(memory_space=pl.ANY)] * len(incoming),
-        out_specs=vmem,
-        out_shape=jax.ShapeDtypeStruct((tiles * TILE, queries.shape[2]), jnp.bfloat16),
+        out_specs=[vmem] * pairs,
+        out_shape=[jax.ShapeDtypeStruct((tiles * TILE // pairs, queries.shape[2]), jnp.bfloat16)] * pairs,
         scratch_shapes=[
             pltpu.VMEM((SIDE * SIDE * CAP,) + own.shape[1:], jnp.bfloat16),
             pltpu.SemaphoreType.DMA((len(incoming),)),
@@ -207,9 +211,31 @@
     )(first, source, queries, own, *incoming)
 
 
-def mix_kernel(attended_ref, weight_ref, out_ref):
-    left = jnp.concatenate([attended_ref[s] for s in range(attended_ref.shape[0])], axis=1)
-    out_ref[...] = jnp.dot(left, weight_ref[...], preferred_element_type=jnp.float32).astype(jnp.bfloat16)
+def mix_kernel(half_ref, *refs):
+    out_ref, count = refs[-1], len(refs) // 2
+    parts = [
+        jnp.dot(left[0], right[...], preferred_element_type=jnp.float32)
+        for left, right in zip(refs[:count], refs[count:])
+    ]
+    out_ref[...] = functools.reduce(jnp.add, parts).astype(out_ref.dtype)
+
+
+def mix(half, attended, weights, dtype):
+    rows, width = attended[0].shape
+    model = weights[0].shape[1]
+    return pl.pallas_call(
+        mix_kernel,
+        grid_spec=pltpu.PrefetchScalarGridSpec(
+            num_scalar_prefetch=1,
+            grid=(model // COLUMNS,),
+            in_specs=[pl.BlockSpec((1, rows // 2, width), lambda i, h: (h[0], 0, 0))] * len(attended)
+            + [pl.BlockSpec((width, COLUMNS), lambda i, h: (0, i))] * len(weights),
+            out_specs=pl.BlockSpec((rows // 2, COLUMNS), lambda i, h: (0, i)),
+        ),
+        out_shape=jax.ShapeDtypeStruct((rows // 2, model), dtype),
+        compiler_params=pltpu.CompilerParams(vmem_limit_bytes=LEAST),
+        name="mix",
+    )(half, *[x.reshape(2, rows // 2, width) for x in attended], *weights)
 
 
 def body(tokens, norm_gain, in_weight, out_weight, pattern):
@@ -222,7 +248,12 @@
     heads = width // HD
     me = jnp.reshape(myself, (1,)).astype(jnp.int32)
 
-    gathered = lax.all_gather(out_weight, "head", axis=0, tiled=True)
+    pairs = groups // 2
+    place = lax.axis_index("head")
+    pair, core = place // 2, place % 2
+
+    def along(x, shift):
+        return lax.ppermute(x, "head", [(s, (s // 2 + shift) % pairs * 2 + s % 2) for s in range(groups)])
 
     chosen, source = pl.pallas_call(
         functools.partial(tables_kernel, shards=shards, tiles=tiles),
@@ -236,37 +267,26 @@
 
     gain = norm_gain.reshape(model // HD, HD)
     weights = in_weight.transpose(1, 0, 2)
-    (own,) = project(tokens, gain, weights, [(1, 0, heads), (2, 0, heads)], [2 * width])
-    sends = list(dispatch(me, chosen, own, SHIFTS[:FLIGHT]))
+    mixers = {shift: along(out_weight, shift) for shift in (1, 3)}
+    own, queries = project(
+        tokens, gain, weights, [(1, 0, heads), (2, 0, heads), (0, 0, heads)], [2 * width, width], MOST
+    )
+    sends = dispatch(me, chosen, own, SHIFTS)
+    sends, mixers = lax.optimization_barrier((sends, mixers))
     incoming = []
     for p, shift in enumerate(SHIFTS):
-        if p == FLIGHT:
-            held, incoming[0] = lax.optimization_barrier((own, incoming[0]))
-            sends += list(dispatch(me, chosen, held, SHIFTS[FLIGHT:]))
         send = sends[p]
-        if p >= FLIGHT:
-            send, incoming[p - FLIGHT] = lax.optimization_barrier((send, incoming[p - FLIGHT]))
         incoming.append(lax.ppermute(send, "seq", [(s, shifted(s, shift)) for s in range(shards)]))
-    tokens, incoming[QUERIES_AFTER] = lax.optimization_barrier((tokens, incoming[QUERIES_AFTER]))
-    (queries,) = project(tokens, gain, weights, [(0, 0, heads)], [width])
-    attended = attend(me * tiles, source, queries, own, incoming)
-    rows = row_count // groups
-    attended = lax.all_to_all(
-        attended.reshape(groups, rows, width), "head", split_axis=0, concat_axis=0, tiled=True
-    )
-    columns = 1024
-    return pl.pallas_call(
-        mix_kernel,
-        grid=(model // columns,),
-        in_specs=[
-            pl.BlockSpec((groups, rows, width), lambda i: (0, 0, 0)),
-            pl.BlockSpec((groups * width, columns), lambda i: (0, i)),
-        ],
-        out_specs=pl.BlockSpec((rows, columns), lambda i: (0, i)),
-        out_shape=jax.ShapeDtypeStruct((rows, model), jnp.bfloat16),
-        compiler_params=pltpu.CompilerParams(vmem_limit_bytes=VMEM),
-        name="mix",
-    )(attended, gathered)
+    late, incoming[LATE] = lax.optimization_barrier((out_weight, incoming[LATE]))
+    mixers[2] = along(late, 2)
+    first = jnp.stack([myself * tiles, pair]).astype(jnp.int32)
+    attended = attend(first, source, queries, own, incoming, pairs)
+    lefts = [attended[0]] + [along(attended[shift], shift) for shift in range(1, pairs)]
+    rights = [out_weight] + [mixers[shift] for shift in range(1, pairs)]
+    give = mix(jnp.reshape(1 - core, (1,)).astype(jnp.int32), lefts, rights, jnp.bfloat16)
+    got = lax.ppermute(give, "head", [(s, s + 1 - s % 2 * 2) for s in range(groups)])
+    keep = mix(jnp.reshape(core, (1,)).astype(jnp.int32), lefts, rights, jnp.float32)
+    return (keep + got.astype(jnp.float32)).astype(jnp.bfloat16)
 
 
 def solution(mesh):

time: 196 us -> 165 us (0.84)
  starting transfers between devices: 26.4 us -> 60.3 us
  waiting for transfers between devices: 87.1 us -> 66.4 us
  blocking collectives: 20.6 us -> 0 us
  between operations: 13.5 us -> 0.12 us
  Pallas kernels: 41 us -> 34.5 us
  local copies, waits for them, and re-layouts: 5.54 us -> 1.8 us
    ppermute x15, waiting for transfers between devices: 86.4 us -> 50.9 us  [body(): lax.ppermute(send, 'seq', [(s, shifted(s, shift)) for s in range(shards)])]
    ppermute x15, starting transfers between devices: 26.3 us -> 49 us  [body(): lax.ppermute(send, 'seq', [(s, shifted(s, shift)) for s in range(shards)])]
    all_to_all x1 -> x0, blocking collectives: 20.6 us -> none  [body(): lax.all_to_all(attended.reshape(groups, rows, width), 'head', split_axis=...]
    ppermute x0 -> x7, waiting for transfers between devices: none -> 15.5 us  [the longest x6 15.5 us: along(): lax.ppermute(x, 'head', [(s, (s // 2 + shift) % pairs * 2 + s % 2) for s...]
    ppermute x0 -> x7, starting transfers between devices: none -> 11.3 us  [the longest x6 9.81 us: along(): lax.ppermute(x, 'head', [(s, (s // 2 + shift) % pairs * 2 + s % 2) for s...]
    pallas_call x2 -> x1, Pallas kernels: 16.4 us -> 11.4 us  [project(): pl.pallas_call(functools.partial(project_kernel, widths=widths, scales=le...]
    unnamed x14 -> x26, local copies, waits for them, and re-layouts: 5.54 us -> 1.8 us
    pallas_call x2 -> x1, Pallas kernels: 7.28 us -> 4.91 us  [dispatch(): pl.pallas_call(functools.partial(dispatch_kernel, shifts=shifts), in_spec...]
  transfers between devices with their start and end apart: 16 -> 22, of which waited for: 9 -> 11; matrix products, arithmetic and copies ran while one was open for 0% -> 0% of each run, Pallas kernels for 18% -> 19%
where the time goes in v4:
time: 165 us
  waiting for transfers between devices  66.4 us (40%)
  starting transfers between devices  60.3 us (37%)
  Pallas kernels  34.5 us (21%)
  other arithmetic  1.85 us (1%)
  local copies, waits for them, and re-layouts  1.8 us (1%)
    ppermute x15, waiting for transfers between devices, body(): lax.ppermute(send, 'seq', [(s, shifted(s, shift)) for s in range(shards)])  50.9 us
    ppermute x15, starting transfers between devices, body(): lax.ppermute(send, 'seq', [(s, shifted(s, shift)) for s in range(shards)])  49 us
    ppermute x6, waiting for transfers between devices, along(): lax.ppermute(x, 'head', [(s, (s // 2 + shift) % pairs * 2 + s % 2) for s...  15.5 us
    pallas_call x1, Pallas kernels, project(): pl.pallas_call(functools.partial(project_kernel, widths=widths, scales=le...  11.4 us
    pallas_call x1, Pallas kernels, attend(): pl.pallas_call(functools.partial(attend_kernel, tiles=tiles, heads=querie...  11.1 us
    ppermute x6, starting transfers between devices, along(): lax.ppermute(x, 'head', [(s, (s // 2 + shift) % pairs * 2 + s % 2) for s...  9.81 us
    pallas_call x2, Pallas kernels, mix(): pl.pallas_call(mix_kernel, grid_spec=pltpu.PrefetchScalarGridSpec(num_sca...  5.45 us
    pallas_call x1, Pallas kernels, dispatch(): pl.pallas_call(functools.partial(dispatch_kernel, shifts=shifts), in_spec...  4.91 us
  transfers between devices with their start and end apart: 22, of which 11 were waited for; matrix products, arithmetic and copies ran while one was open for 0% of the time, Pallas kernels for 19%

profile of v4, /device:TPU:7, one launch (start us, length us, event | category | flops | bytes accessed | tf_op | source)
XLA Modules:
  0.0 165.0 jit_solution(4451120182755781520)
XLA Ops:
  0.0 1.3 collective-permute-start
  1.3 1.4 collective-permute-start.1
  2.7 1.7 %tables.1 = (s32[8,128]{1,0:T(8,128)}, s32[4,256]{1,0:T(4,128)}) custom-call(s32[1]{0:T(128)} %bitcast.3.me_ref, s32[4,256]{1,0:T(4,128)} %bitcast.20), custom_call_target="tpu_custom_call" | custom-call | tf_op jit(solution)/shard_map/tables/pallas_call | solution.py:258
  4.4 11.4 %project.1 = (bf16[16,128,512]{2,1,0:T(8,128)(2,1)}, bf16[16,128,256]{2,1,0:T(8,128)(2,1)}) custom-call(bf16[2048,2048]{1,0:T(8,128)(2,1)} %refs_0_.1, f32[16,128]{1,0:T(8,128)} %bitcast.19, bf16[3,2048,256]{2,1,0:T(8,128)(2,1)} %bitcast.16, bf16[3,2048,256]{2,1,0:T(8,128)(2,1)} %bitcast.17, bf16[3,2048,256]{2,1,0:T(8,128)(2,1)} %bitcast.18), custom_call_target="tpu_custom_call" | custom-call | tf_op jit(solution)/shard_map/project/pallas_call | solution.py:103
  15.9 4.9 %dispatch.1 = (bf16[4,128,512]{2,1,0:T(8,128)(2,1)}, bf16[4,128,512]{2,1,0:T(8,128)(2,1)}, bf16[4,128,512]{2,1,0:T(8,128)(2,1)}, bf16[4,128,512]{2,1,0:T(8,128)(...) custom-call(s32[1]{0:T(128)} %bitcast.3.me_ref, ...), custom_call_target="tpu_custom_call" | custom-call | tf_op jit(solution)/shard_map/dispatch/pallas_call | solution.py:138
  20.8 4.8 %collective-permute-done.refs_5_ = bf16[256,2048]{1,0:T(8,128)(2,1)S(1)} collective-permute-done((bf16[256,2048]{1,0:T(8,128)(2,1)}, bf16[256,2048]{1,0:T(8,128)(2,1)S(1)}, u32[]{:S(2)}, u32[]{:S(2)}) %collective-permute-start) | collective-permute-done | bytes 1048608 | tf_op jit(solution)/shard_map/ppermute | solution.py:256
  25.6 0.0 collective-permute-done.1.refs_7_
  25.6 4.4 %collective-permute-start.2 = (bf16[4,128,512]{2,1,0:T(8,128)(2,1)}, bf16[4,128,512]{2,1,0:T(8,128)(2,1)S(1)}, u32[]{:S(2)}, u32[]{:S(2)}) collective-permute-start(bf16[4,128,512]{2,1,0:T(8,128)(2,1)} %get-tuple-element.66), channel_id=1, source_target_pairs={{0,80},{8,88},{16,64},{24,72},{32,112},{40,120},{48,96},{56,104},{... | collective-permute-start | bytes 1572872 | tf_op jit(solution)/shard_map/ppermute | solution.py:279
  30.0 2.3 %collective-permute-start.3 = (bf16[4,128,512]{2,1,0:T(8,128)(2,1)}, bf16[4,128,512]{2,1,0:T(8,128)(2,1)S(1)}, u32[]{:S(2)}, u32[]{:S(2)}) collective-permute-start(bf16[4,128,512]{2,1,0:T(8,128)(2,1)} %get-tuple-element.67), channel_id=1, source_target_pairs={{0,48},{8,56},{16,32},{24,40},{32,80},{40,88},{48,64},{56,72},{64,... | collective-permute-start | bytes 1572872 | tf_op jit(solution)/shard_map/ppermute | solution.py:279
  32.3 1.9 %collective-permute-start.4 = (bf16[4,128,512]{2,1,0:T(8,128)(2,1)}, bf16[4,128,512]{2,1,0:T(8,128)(2,1)S(1)}, u32[]{:S(2)}, u32[]{:S(2)}) collective-permute-start(bf16[4,128,512]{2,1,0:T(8,128)(2,1)} %get-tuple-element.68), channel_id=1, source_target_pairs={{0,96},{8,104},{16,112},{24,120},{32,0},{40,8},{48,16},{56,24},{64... | collective-permute-start | bytes 1572872 | tf_op jit(solution)/shard_map/ppermute | solution.py:279
  34.3 0.8 collective-permute-start.5
  35.1 1.5 collective-permute-start.6
  36.6 5.1 %collective-permute-done.2.rest_0_ = bf16[4,128,512]{2,1,0:T(8,128)(2,1)S(1)} collective-permute-done((bf16[4,128,512]{2,1,0:T(8,128)(2,1)}, bf16[4,128,512]{2,1,0:T(8,128)(2,1)S(1)}, u32[]{:S(2)}, u32[]{:S(2)}) %collective-permute-start.2) | collective-permute-done | bytes 524320 | tf_op jit(solution)/shard_map/ppermute | solution.py:279
  41.6 3.6 %collective-permute-start.12 = (bf16[4,128,512]{2,1,0:T(8,128)(2,1)}, bf16[4,128,512]{2,1,0:T(8,128)(2,1)S(1)}, u32[]{:S(2)}, u32[]{:S(2)}) collective-permute-start(bf16[4,128,512]{2,1,0:T(8,128)(2,1)} %get-tuple-element.76), channel_id=1, source_target_pairs={{0,72},{8,80},{16,88},{24,64},{32,104},{40,112},{48,120},{56,96},{... | collective-permute-start | bytes 1572872 | tf_op jit(solution)/shard_map/ppermute | solution.py:279
  45.2 8.7 %collective-permute-done.3.rest_1_ = bf16[4,128,512]{2,1,0:T(8,128)(2,1)S(1)} collective-permute-done((bf16[4,128,512]{2,1,0:T(8,128)(2,1)}, bf16[4,128,512]{2,1,0:T(8,128)(2,1)S(1)}, u32[]{:S(2)}, u32[]{:S(2)}) %collective-permute-start.3) | collective-permute-done | bytes 524320 | tf_op jit(solution)/shard_map/ppermute | solution.py:279
  54.0 0.6 collective-permute-start.7
  54.6 2.9 %collective-permute-done.4.rest_2_ = bf16[4,128,512]{2,1,0:T(8,128)(2,1)S(1)} collective-permute-done((bf16[4,128,512]{2,1,0:T(8,128)(2,1)}, bf16[4,128,512]{2,1,0:T(8,128)(2,1)S(1)}, u32[]{:S(2)}, u32[]{:S(2)}) %collective-permute-start.4) | collective-permute-done | bytes 524320 | tf_op jit(solution)/shard_map/ppermute | solution.py:279
  57.5 11.4 %collective-permute-start.8 = (bf16[4,128,512]{2,1,0:T(8,128)(2,1)}, bf16[4,128,512]{2,1,0:T(8,128)(2,1)S(1)}, u32[]{:S(2)}, u32[]{:S(2)}) collective-permute-start(bf16[4,128,512]{2,1,0:T(8,128)(2,1)} %get-tuple-element.72), channel_id=1, source_target_pairs={{0,88},{8,64},{16,72},{24,80},{32,120},{40,96},{48,104},{56,112},{... | collective-permute-start | bytes 1572872 | tf_op jit(solution)/shard_map/ppermute | solution.py:279
  69.0 3.0 %collective-permute-start.9 = (bf16[4,128,512]{2,1,0:T(8,128)(2,1)}, bf16[4,128,512]{2,1,0:T(8,128)(2,1)S(1)}, u32[]{:S(2)}, u32[]{:S(2)}) collective-permute-start(bf16[4,128,512]{2,1,0:T(8,128)(2,1)} %get-tuple-element.73), channel_id=1, source_target_pairs={{0,8},{8,16},{16,24},{24,0},{32,40},{40,48},{48,56},{56,32},{64,72... | collective-permute-start | bytes 1572872 | tf_op jit(solution)/shard_map/ppermute | solution.py:279
  72.0 4.7 %collective-permute-done.6.rest_4_ = bf16[4,128,512]{2,1,0:T(8,128)(2,1)S(1)} collective-permute-done((bf16[4,128,512]{2,1,0:T(8,128)(2,1)}, bf16[4,128,512]{2,1,0:T(8,128)(2,1)S(1)}, u32[]{:S(2)}, u32[]{:S(2)}) %collective-permute-start.6) | collective-permute-done | bytes 524320 | tf_op jit(solution)/shard_map/ppermute | solution.py:279
  76.7 0.0 collective-permute-start.10
  76.7 0.0 collective-permute-done.12.rest_10_
  76.8 5.9 %collective-permute-start.11 = (bf16[4,128,512]{2,1,0:T(8,128)(2,1)}, bf16[4,128,512]{2,1,0:T(8,128)(2,1)S(1)}, u32[]{:S(2)}, u32[]{:S(2)}) collective-permute-start(bf16[4,128,512]{2,1,0:T(8,128)(2,1)} %get-tuple-element.75), channel_id=1, source_target_pairs={{0,120},{8,96},{16,104},{24,112},{32,24},{40,0},{48,8},{56,16},{64... | collective-permute-start | bytes 1572872 | tf_op jit(solution)/shard_map/ppermute | solution.py:279
  82.7 1.6 collective-permute-start.20
  84.2 4.9 %collective-permute-done.8.rest_6_ = bf16[4,128,512]{2,1,0:T(8,128)(2,1)S(1)} collective-permute-done((bf16[4,128,512]{2,1,0:T(8,128)(2,1)}, bf16[4,128,512]{2,1,0:T(8,128)(2,1)S(1)}, u32[]{:S(2)}, u32[]{:S(2)}) %collective-permute-start.8) | collective-permute-done | bytes 524320 | tf_op jit(solution)/shard_map/ppermute | solution.py:279
  89.1 0.9 collective-permute-start.13
  90.1 3.9 %collective-permute-start.14 = (bf16[4,128,512]{2,1,0:T(8,128)(2,1)}, bf16[4,128,512]{2,1,0:T(8,128)(2,1)}, u32[]{:S(2)}, u32[]{:S(2)}) collective-permute-start(bf16[4,128,512]{2,1,0:T(8,128)(2,1)} %get-tuple-element.79), channel_id=1, source_target_pairs={{0,104},{8,112},{16,120},{24,96},{32,8},{40,16},{48,24},{56,0},{64... | collective-permute-start | bytes 1572872 | tf_op jit(solution)/shard_map/ppermute | solution.py:279
  94.0 5.1 %collective-permute-done.10.rest_8_ = bf16[4,128,512]{2,1,0:T(8,128)(2,1)S(1)} collective-permute-done((bf16[4,128,512]{2,1,0:T(8,128)(2,1)}, bf16[4,128,512]{2,1,0:T(8,128)(2,1)S(1)}, u32[]{:S(2)}, u32[]{:S(2)}) %collective-permute-start.10) | collective-permute-done | bytes 524320 | tf_op jit(solution)/shard_map/ppermute | solution.py:279
  99.1 4.3 %collective-permute-start.15 = (bf16[4,128,512]{2,1,0:T(8,128)(2,1)}, bf16[4,128,512]{2,1,0:T(8,128)(2,1)}, u32[]{:S(2)}, u32[]{:S(2)}) collective-permute-start(bf16[4,128,512]{2,1,0:T(8,128)(2,1)} %get-tuple-element.80), channel_id=1, source_target_pairs={{0,16},{8,24},{16,0},{24,8},{32,48},{40,56},{48,32},{56,40},{64,80... | collective-permute-start | bytes 1572872 | tf_op jit(solution)/shard_map/ppermute | solution.py:279
  103.4 0.1 collective-permute-done.11.rest_9_
  103.5 0.8 copy-done.12
  104.3 4.3 %collective-permute-start.16 = (bf16[4,128,512]{2,1,0:T(8,128)(2,1)}, bf16[4,128,512]{2,1,0:T(8,128)(2,1)}, u32[]{:S(2)}, u32[]{:S(2)}) collective-permute-start(bf16[4,128,512]{2,1,0:T(8,128)(2,1)} %get-tuple-element.81), channel_id=1, source_target_pairs={{0,64},{8,72},{16,80},{24,88},{32,96},{40,104},{48,112},{56,120},{... | collective-permute-start | bytes 1572872 | tf_op jit(solution)/shard_map/ppermute | solution.py:279
  108.6 0.6 pad_add_fusion.first_ref
  109.2 19.3 %collective-permute-done.13.rest_11_ = bf16[4,128,512]{2,1,0:T(8,128)(2,1)} collective-permute-done((bf16[4,128,512]{2,1,0:T(8,128)(2,1)}, bf16[4,128,512]{2,1,0:T(8,128)(2,1)}, u32[]{:S(2)}, u32[]{:S(2)}) %collective-permute-start.13) | collective-permute-done | bytes 524320 | tf_op jit(solution)/shard_map/ppermute | solution.py:279
  128.5 0.0 collective-permute-done.15.rest_13_
  128.5 0.0 collective-permute-done.16.rest_14_
  128.5 11.1 %attend.1 = (bf16[512,256]{1,0:T(8,128)(2,1)}, bf16[512,256]{1,0:T(8,128)(2,1)}, bf16[512,256]{1,0:T(8,128)(2,1)}, bf16[512,256]{1,0:T(8,128)(2,1)}) custom-call(s32[2]{0:T(128)} %pad_add_fusion.first_ref, s32[4,256]{1,0:T(4,128)} %get-tuple-element.47.source_ref, bf16[16,128,256]{2,1,0:T(8,128)(2,1)} %get-tuple-element.48.queries_ref, ...), custom_call_target="tpu_custom_call" | custom-call | tf_op jit(solution)/shard_map/attend/pallas_call | solution.py:200
  139.6 2.1 %collective-permute-start.17 = (bf16[512,256]{1,0:T(8,128)(2,1)}, bf16[512,256]{1,0:T(8,128)(2,1)S(1)}, u32[]{:S(2)}, u32[]{:S(2)}) collective-permute-start(bf16[512,256]{1,0:T(8,128)(2,1)} %get-tuple-element.83), channel_id=1, source_target_pairs={{0,2},{1,3},{2,4},{3,5},{4,6},{5,7},{6,0},{7,1},{8,10},{9,11},{10,... | collective-permute-start | bytes 786440 | tf_op jit(solution)/shard_map/ppermute | solution.py:256
  141.7 2.3 %collective-permute-start.18 = (bf16[512,256]{1,0:T(8,128)(2,1)}, bf16[512,256]{1,0:T(8,128)(2,1)}, u32[]{:S(2)}, u32[]{:S(2)}) collective-permute-start(bf16[512,256]{1,0:T(8,128)(2,1)} %get-tuple-element.84), channel_id=1, source_target_pairs={{0,4},{1,5},{2,6},{3,7},{4,0},{5,1},{6,2},{7,3},{8,12},{9,13},{10,... | collective-permute-start | bytes 786440 | tf_op jit(solution)/shard_map/ppermute | solution.py:256
  144.0 1.1 collective-permute-start.19
  145.1 4.1 %collective-permute-done.17 = bf16[512,256]{1,0:T(8,128)(2,1)S(1)} collective-permute-done((bf16[512,256]{1,0:T(8,128)(2,1)}, bf16[512,256]{1,0:T(8,128)(2,1)S(1)}, u32[]{:S(2)}, u32[]{:S(2)}) %collective-permute-start.17) | collective-permute-done | bytes 262176 | tf_op jit(solution)/shard_map/ppermute | solution.py:256
  149.2 6.6 %collective-permute-done.18 = bf16[512,256]{1,0:T(8,128)(2,1)} collective-permute-done((bf16[512,256]{1,0:T(8,128)(2,1)}, bf16[512,256]{1,0:T(8,128)(2,1)}, u32[]{:S(2)}, u32[]{:S(2)}) %collective-permute-start.18) | collective-permute-done | bytes 262176 | tf_op jit(solution)/shard_map/ppermute | solution.py:256
  155.8 0.0 collective-permute-done.19
  155.8 0.9 copy-done.1
  156.7 2.7 %mix.3 = bf16[256,2048]{1,0:T(8,128)(2,1)S(1)} custom-call(s32[1]{0:T(128)} %bitcast.11.half_ref, bf16[2,256,256]{2,1,0:T(8,128)(2,1)S(1)} %bitcast.12, bf16[2,256,256]{2,1,0:T(8,128)(2,1)S(1)} %bitcast.14, bf16[2,256,256]{2,1,0:T(8,128)(2,1)} %bitcast.9.refs_2_, bf16[2,256,256]{2,1,0:T(8,128)(2,1)} %bitcast.10.refs_3_, bf16[256,2048]{1,0:T(8,128)(2,1)S(1)} %copy-done, ...), custom_call_target="tpu_custom_call" | custom-call | tf_op jit(solution)/shard_map/mix/pallas_call | solution.py:226
  159.4 1.5 collective-permute-start.21
  160.9 2.8 %mix.2 = f32[256,2048]{1,0:T(8,128)S(1)} custom-call(s32[1]{0:T(128)} %bitcast.half_ref, bf16[2,256,256]{2,1,0:T(8,128)(2,1)S(1)} %bitcast.13, bf16[2,256,256]{2,1,0:T(8,128)(2,1)S(1)} %bitcast.15, bf16[2,256,256]{2,1,0:T(8,128)(2,1)} %bitcast.9.refs_2_, bf16[2,256,256]{2,1,0:T(8,128)(2,1)} %bitcast.10.refs_3_, bf16[256,2048]{1,0:T(8,128)(2,1)S(1)} %copy-done, ...), custom_call_target="tpu_custom_call" | custom-call | tf_op jit(solution)/shard_map/mix/pallas_call | solution.py:226
  163.7 1.3 add_convert_fusion
  (30 shorter events, 0.1 us)
Async XLA Ops:
  0.0 25.6 %collective-permute-start = (bf16[256,2048]{1,0:T(8,128)(2,1)}, bf16[256,2048]{1,0:T(8,128)(2,1)S(1)}, u32[]{:S(2)}, u32[]{:S(2)}) collective-permute-start(bf16[256,2048]{1,0:T(8,128)(2,1)} %refs_4_.3), channel_id=1, source_target_pairs={{0,2},{1,3},{2,4},{3,5},{4,6},{5,7},{6,0},{7,1},{8,10},{9,11},{10,... | collective-permute-start | bytes 3145736 | tf_op jit(solution)/shard_map/ppermute | solution.py:256
  1.3 24.3 %collective-permute-start.1 = (bf16[256,2048]{1,0:T(8,128)(2,1)}, bf16[256,2048]{1,0:T(8,128)(2,1)S(1)}, u32[]{:S(2)}, u32[]{:S(2)}) collective-permute-start(bf16[256,2048]{1,0:T(8,128)(2,1)} %refs_4_.3), channel_id=1, source_target_pairs={{0,6},{1,7},{2,0},{3,1},{4,2},{5,3},{6,4},{7,5},{8,14},{9,15},{10,... | collective-permute-start | bytes 3145736 | tf_op jit(solution)/shard_map/ppermute | solution.py:256
  15.9 66.8 %copy-start = (bf16[256,2048]{1,0:T(8,128)(2,1)S(1)}, bf16[256,2048]{1,0:T(8,128)(2,1)}, u32[]{:S(2)}) copy-start(bf16[256,2048]{1,0:T(8,128)(2,1)} %refs_4_.3) | copy-start | bytes 3145732
  25.6 16.0 %collective-permute-start.2 = (bf16[4,128,512]{2,1,0:T(8,128)(2,1)}, bf16[4,128,512]{2,1,0:T(8,128)(2,1)S(1)}, u32[]{:S(2)}, u32[]{:S(2)}) collective-permute-start(bf16[4,128,512]{2,1,0:T(8,128)(2,1)} %get-tuple-element.66), channel_id=1, source_target_pairs={{0,80},{8,88},{16,64},{24,72},{32,112},{40,120},{48,96},{56,104},{... | collective-permute-start | bytes 1572872 | tf_op jit(solution)/shard_map/ppermute | solution.py:279
  30.0 23.9 %collective-permute-start.3 = (bf16[4,128,512]{2,1,0:T(8,128)(2,1)}, bf16[4,128,512]{2,1,0:T(8,128)(2,1)S(1)}, u32[]{:S(2)}, u32[]{:S(2)}) collective-permute-start(bf16[4,128,512]{2,1,0:T(8,128)(2,1)} %get-tuple-element.67), channel_id=1, source_target_pairs={{0,48},{8,56},{16,32},{24,40},{32,80},{40,88},{48,64},{56,72},{64,... | collective-permute-start | bytes 1572872 | tf_op jit(solution)/shard_map/ppermute | solution.py:279
  32.3 25.2 %collective-permute-start.4 = (bf16[4,128,512]{2,1,0:T(8,128)(2,1)}, bf16[4,128,512]{2,1,0:T(8,128)(2,1)S(1)}, u32[]{:S(2)}, u32[]{:S(2)}) collective-permute-start(bf16[4,128,512]{2,1,0:T(8,128)(2,1)} %get-tuple-element.68), channel_id=1, source_target_pairs={{0,96},{8,104},{16,112},{24,120},{32,0},{40,8},{48,16},{56,24},{64... | collective-permute-start | bytes 1572872 | tf_op jit(solution)/shard_map/ppermute | solution.py:279
  34.3 34.7 %collective-permute-start.5 = (bf16[4,128,512]{2,1,0:T(8,128)(2,1)}, bf16[4,128,512]{2,1,0:T(8,128)(2,1)S(1)}, u32[]{:S(2)}, u32[]{:S(2)}) collective-permute-start(bf16[4,128,512]{2,1,0:T(8,128)(2,1)} %get-tuple-element.69), channel_id=1, source_target_pairs={{0,112},{8,120},{16,96},{24,104},{32,16},{40,24},{48,0},{56,8},{64... | collective-permute-start | bytes 1572872 | tf_op jit(solution)/shard_map/ppermute | solution.py:279
  35.1 41.6 %collective-permute-start.6 = (bf16[4,128,512]{2,1,0:T(8,128)(2,1)}, bf16[4,128,512]{2,1,0:T(8,128)(2,1)S(1)}, u32[]{:S(2)}, u32[]{:S(2)}) collective-permute-start(bf16[4,128,512]{2,1,0:T(8,128)(2,1)} %get-tuple-element.70), channel_id=1, source_target_pairs={{0,32},{8,40},{16,48},{24,56},{32,64},{40,72},{48,80},{56,88},{64,... | collective-permute-start | bytes 1572872 | tf_op jit(solution)/shard_map/ppermute | solution.py:279
  41.6 41.0 %copy-start.2 = (bf16[4,128,512]{2,1,0:T(8,128)(2,1)}, bf16[4,128,512]{2,1,0:T(8,128)(2,1)S(1)}, u32[]{:S(2)}) copy-start(bf16[4,128,512]{2,1,0:T(8,128)(2,1)S(1)} %collective-permute-done.2.rest_0_) | copy-start | bytes 1572868
  41.6 35.1 %collective-permute-start.12 = (bf16[4,128,512]{2,1,0:T(8,128)(2,1)}, bf16[4,128,512]{2,1,0:T(8,128)(2,1)S(1)}, u32[]{:S(2)}, u32[]{:S(2)}) collective-permute-start(bf16[4,128,512]{2,1,0:T(8,128)(2,1)} %get-tuple-element.76), channel_id=1, source_target_pairs={{0,72},{8,80},{16,88},{24,64},{32,104},{40,112},{48,120},{56,96},{... | collective-permute-start | bytes 1572872 | tf_op jit(solution)/shard_map/ppermute | solution.py:279
  53.9 28.7 %copy-start.3 = (bf16[4,128,512]{2,1,0:T(8,128)(2,1)}, bf16[4,128,512]{2,1,0:T(8,128)(2,1)S(1)}, u32[]{:S(2)}) copy-start(bf16[4,128,512]{2,1,0:T(8,128)(2,1)S(1)} %collective-permute-done.3.rest_1_) | copy-start | bytes 1572868
  54.0 28.7 %collective-permute-start.7 = (bf16[4,128,512]{2,1,0:T(8,128)(2,1)}, bf16[4,128,512]{2,1,0:T(8,128)(2,1)S(1)}, u32[]{:S(2)}, u32[]{:S(2)}) collective-permute-start(bf16[4,128,512]{2,1,0:T(8,128)(2,1)} %get-tuple-element.71), channel_id=1, source_target_pairs={{0,24},{8,0},{16,8},{24,16},{32,56},{40,32},{48,40},{56,48},{64,88... | collective-permute-start | bytes 1572872 | tf_op jit(solution)/shard_map/ppermute | solution.py:279
  57.5 26.7 %copy-start.4 = (bf16[4,128,512]{2,1,0:T(8,128)(2,1)}, bf16[4,128,512]{2,1,0:T(8,128)(2,1)S(1)}, u32[]{:S(2)}) copy-start(bf16[4,128,512]{2,1,0:T(8,128)(2,1)S(1)} %collective-permute-done.4.rest_2_) | copy-start | bytes 1572868
  57.5 31.6 %collective-permute-start.8 = (bf16[4,128,512]{2,1,0:T(8,128)(2,1)}, bf16[4,128,512]{2,1,0:T(8,128)(2,1)S(1)}, u32[]{:S(2)}, u32[]{:S(2)}) collective-permute-start(bf16[4,128,512]{2,1,0:T(8,128)(2,1)} %get-tuple-element.72), channel_id=1, source_target_pairs={{0,88},{8,64},{16,72},{24,80},{32,120},{40,96},{48,104},{56,112},{... | collective-permute-start | bytes 1572872 | tf_op jit(solution)/shard_map/ppermute | solution.py:279
  69.0 20.2 %copy-start.5 = (bf16[4,128,512]{2,1,0:T(8,128)(2,1)}, bf16[4,128,512]{2,1,0:T(8,128)(2,1)S(1)}, u32[]{:S(2)}) copy-start(bf16[4,128,512]{2,1,0:T(8,128)(2,1)S(1)} %collective-permute-done.5.rest_3_) | copy-start | bytes 1572868
  69.0 21.1 %collective-permute-start.9 = (bf16[4,128,512]{2,1,0:T(8,128)(2,1)}, bf16[4,128,512]{2,1,0:T(8,128)(2,1)S(1)}, u32[]{:S(2)}, u32[]{:S(2)}) collective-permute-start(bf16[4,128,512]{2,1,0:T(8,128)(2,1)} %get-tuple-element.73), channel_id=1, source_target_pairs={{0,8},{8,16},{16,24},{24,0},{32,40},{40,48},{48,56},{56,32},{64,72... | collective-permute-start | bytes 1572872 | tf_op jit(solution)/shard_map/ppermute | solution.py:279
  76.7 13.3 %copy-start.6 = (bf16[4,128,512]{2,1,0:T(8,128)(2,1)}, bf16[4,128,512]{2,1,0:T(8,128)(2,1)S(1)}, u32[]{:S(2)}) copy-start(bf16[4,128,512]{2,1,0:T(8,128)(2,1)S(1)} %collective-permute-done.6.rest_4_) | copy-start | bytes 1572868
  76.7 22.4 %collective-permute-start.10 = (bf16[4,128,512]{2,1,0:T(8,128)(2,1)}, bf16[4,128,512]{2,1,0:T(8,128)(2,1)S(1)}, u32[]{:S(2)}, u32[]{:S(2)}) collective-permute-start(bf16[4,128,512]{2,1,0:T(8,128)(2,1)} %get-tuple-element.74), channel_id=1, source_target_pairs={{0,40},{8,48},{16,56},{24,32},{32,72},{40,80},{48,88},{56,64},{64,... | collective-permute-start | bytes 1572872 | tf_op jit(solution)/shard_map/ppermute | solution.py:279
  76.8 13.3 %copy-start.7 = (bf16[4,128,512]{2,1,0:T(8,128)(2,1)}, bf16[4,128,512]{2,1,0:T(8,128)(2,1)S(1)}, u32[]{:S(2)}) copy-start(bf16[4,128,512]{2,1,0:T(8,128)(2,1)S(1)} %collective-permute-done.12.rest_10_) | copy-start | bytes 1572868
  76.8 26.7 %collective-permute-start.11 = (bf16[4,128,512]{2,1,0:T(8,128)(2,1)}, bf16[4,128,512]{2,1,0:T(8,128)(2,1)S(1)}, u32[]{:S(2)}, u32[]{:S(2)}) collective-permute-start(bf16[4,128,512]{2,1,0:T(8,128)(2,1)} %get-tuple-element.75), channel_id=1, source_target_pairs={{0,120},{8,96},{16,104},{24,112},{32,24},{40,0},{48,8},{56,16},{64... | collective-permute-start | bytes 1572872 | tf_op jit(solution)/shard_map/ppermute | solution.py:279
  82.6 11.4 %copy-start.8 = (bf16[4,128,512]{2,1,0:T(8,128)(2,1)}, bf16[4,128,512]{2,1,0:T(8,128)(2,1)S(1)}, u32[]{:S(2)}) copy-start(bf16[4,128,512]{2,1,0:T(8,128)(2,1)S(1)} %collective-permute-done.7.rest_5_) | copy-start | bytes 1572868
  82.7 73.1 %collective-permute-start.20 = (bf16[256,2048]{1,0:T(8,128)(2,1)S(1)}, bf16[256,2048]{1,0:T(8,128)(2,1)}, u32[]{:S(2)}, u32[]{:S(2)}) collective-permute-start(bf16[256,2048]{1,0:T(8,128)(2,1)S(1)} %copy-done), channel_id=1, source_target_pairs={{0,4},{1,5},{2,6},{3,7},{4,0},{5,1},{6,2},{7,3},{8,12},{9,13},{10,... | collective-permute-start | bytes 3145736 | tf_op jit(solution)/shard_map/ppermute | solution.py:256
  89.1 10.0 %copy-start.9 = (bf16[4,128,512]{2,1,0:T(8,128)(2,1)}, bf16[4,128,512]{2,1,0:T(8,128)(2,1)S(1)}, u32[]{:S(2)}) copy-start(bf16[4,128,512]{2,1,0:T(8,128)(2,1)S(1)} %collective-permute-done.8.rest_6_) | copy-start | bytes 1572868
  89.1 39.4 %collective-permute-start.13 = (bf16[4,128,512]{2,1,0:T(8,128)(2,1)}, bf16[4,128,512]{2,1,0:T(8,128)(2,1)}, u32[]{:S(2)}, u32[]{:S(2)}) collective-permute-start(bf16[4,128,512]{2,1,0:T(8,128)(2,1)} %get-tuple-element.78), channel_id=1, source_target_pairs={{0,56},{8,32},{16,40},{24,48},{32,88},{40,64},{48,72},{56,80},{64,... | collective-permute-start | bytes 1572872 | tf_op jit(solution)/shard_map/ppermute | solution.py:279
  90.1 13.3 %copy-start.10 = (bf16[4,128,512]{2,1,0:T(8,128)(2,1)}, bf16[4,128,512]{2,1,0:T(8,128)(2,1)S(1)}, u32[]{:S(2)}) copy-start(bf16[4,128,512]{2,1,0:T(8,128)(2,1)S(1)} %collective-permute-done.9.rest_7_) | copy-start | bytes 1572868
  90.1 38.4 %collective-permute-start.14 = (bf16[4,128,512]{2,1,0:T(8,128)(2,1)}, bf16[4,128,512]{2,1,0:T(8,128)(2,1)}, u32[]{:S(2)}, u32[]{:S(2)}) collective-permute-start(bf16[4,128,512]{2,1,0:T(8,128)(2,1)} %get-tuple-element.79), channel_id=1, source_target_pairs={{0,104},{8,112},{16,120},{24,96},{32,8},{40,16},{48,24},{56,0},{64... | collective-permute-start | bytes 1572872 | tf_op jit(solution)/shard_map/ppermute | solution.py:279
  99.1 4.4 %copy-start.11 = (bf16[4,128,512]{2,1,0:T(8,128)(2,1)}, bf16[4,128,512]{2,1,0:T(8,128)(2,1)S(1)}, u32[]{:S(2)}) copy-start(bf16[4,128,512]{2,1,0:T(8,128)(2,1)S(1)} %collective-permute-done.10.rest_8_) | copy-start | bytes 1572868
  99.1 29.4 %collective-permute-start.15 = (bf16[4,128,512]{2,1,0:T(8,128)(2,1)}, bf16[4,128,512]{2,1,0:T(8,128)(2,1)}, u32[]{:S(2)}, u32[]{:S(2)}) collective-permute-start(bf16[4,128,512]{2,1,0:T(8,128)(2,1)} %get-tuple-element.80), channel_id=1, source_target_pairs={{0,16},{8,24},{16,0},{24,8},{32,48},{40,56},{48,32},{56,40},{64,80... | collective-permute-start | bytes 1572872 | tf_op jit(solution)/shard_map/ppermute | solution.py:279
  103.5 0.8 copy-start.12
  104.3 24.2 %collective-permute-start.16 = (bf16[4,128,512]{2,1,0:T(8,128)(2,1)}, bf16[4,128,512]{2,1,0:T(8,128)(2,1)}, u32[]{:S(2)}, u32[]{:S(2)}) collective-permute-start(bf16[4,128,512]{2,1,0:T(8,128)(2,1)} %get-tuple-element.81), channel_id=1, source_target_pairs={{0,64},{8,72},{16,80},{24,88},{32,96},{40,104},{48,112},{56,120},{... | collective-permute-start | bytes 1572872 | tf_op jit(solution)/shard_map/ppermute | solution.py:279
  139.6 9.6 %collective-permute-start.17 = (bf16[512,256]{1,0:T(8,128)(2,1)}, bf16[512,256]{1,0:T(8,128)(2,1)S(1)}, u32[]{:S(2)}, u32[]{:S(2)}) collective-permute-start(bf16[512,256]{1,0:T(8,128)(2,1)} %get-tuple-element.83), channel_id=1, source_target_pairs={{0,2},{1,3},{2,4},{3,5},{4,6},{5,7},{6,0},{7,1},{8,10},{9,11},{10,... | collective-permute-start | bytes 786440 | tf_op jit(solution)/shard_map/ppermute | solution.py:256
  141.7 14.1 %collective-permute-start.18 = (bf16[512,256]{1,0:T(8,128)(2,1)}, bf16[512,256]{1,0:T(8,128)(2,1)}, u32[]{:S(2)}, u32[]{:S(2)}) collective-permute-start(bf16[512,256]{1,0:T(8,128)(2,1)} %get-tuple-element.84), channel_id=1, source_target_pairs={{0,4},{1,5},{2,6},{3,7},{4,0},{5,1},{6,2},{7,3},{8,12},{9,13},{10,... | collective-permute-start | bytes 786440 | tf_op jit(solution)/shard_map/ppermute | solution.py:256
  144.0 11.8 %collective-permute-start.19 = (bf16[512,256]{1,0:T(8,128)(2,1)}, bf16[512,256]{1,0:T(8,128)(2,1)}, u32[]{:S(2)}, u32[]{:S(2)}) collective-permute-start(bf16[512,256]{1,0:T(8,128)(2,1)} %get-tuple-element.85), channel_id=1, source_target_pairs={{0,6},{1,7},{2,0},{3,1},{4,2},{5,3},{6,4},{7,5},{8,14},{9,15},{10,... | collective-permute-start | bytes 786440 | tf_op jit(solution)/shard_map/ppermute | solution.py:256
  155.8 1.0 copy-start.1
  159.4 4.3 %collective-permute-start.21 = (bf16[256,2048]{1,0:T(8,128)(2,1)S(1)}, bf16[256,2048]{1,0:T(8,128)(2,1)S(1)}, u32[]{:S(2)}, u32[]{:S(2)}) collective-permute-start(bf16[256,2048]{1,0:T(8,128)(2,1)S(1)} %mix.3), channel_id=1, source_target_pairs={{0,1},{1,0},{2,3},{3,2},{4,5},{5,4},{6,7},{7,6},{8,9},{9,8},{10,11... | collective-permute-start | bytes 3145736 | tf_op jit(solution)/shard_map/ppermute | solution.py:287

commit v5 on v4

--- a/solution.py
+++ b/solution.py
@@ -16,6 +16,8 @@
 GROUP = 2
 SIDE = 4
 SHIFTS = (10, 6, 12, 14, 4, 3, 11, 1, 5, 15, 9, 7, 13, 2, 8)
+FIRST = 5
+ALONE = 2
 LATE = 10
 COLUMNS = 1024
 VMEM = 60 * 1024 * 1024
@@ -268,11 +270,12 @@
     gain = norm_gain.reshape(model // HD, HD)
     weights = in_weight.transpose(1, 0, 2)
     mixers = {shift: along(out_weight, shift) for shift in (1, 3)}
-    own, queries = project(
-        tokens, gain, weights, [(1, 0, heads), (2, 0, heads), (0, 0, heads)], [2 * width, width], MOST
-    )
-    sends = dispatch(me, chosen, own, SHIFTS)
-    sends, mixers = lax.optimization_barrier((sends, mixers))
+    (own,) = project(tokens, gain, weights, [(1, 0, heads), (2, 0, heads)], [2 * width], MOST)
+    sends = list(dispatch(me, chosen, own, SHIFTS[:FIRST]))
+    held, tokens, sends = lax.optimization_barrier((own, tokens, sends))
+    sends += list(dispatch(me, chosen, held, SHIFTS[FIRST:]))
+    (queries,) = project(tokens, gain, weights, [(0, 0, heads)], [width], MOST)
+    sends[ALONE:], mixers = lax.optimization_barrier((sends[ALONE:], mixers))
     incoming = []
     for p, shift in enumerate(SHIFTS):
         send = sends[p]

time: 165 us -> 156 us (0.945)
  waiting for transfers between devices: 66.4 us -> 55.9 us
  Pallas kernels: 34.5 us -> 41.9 us
  starting transfers between devices: 60.3 us -> 53 us
    ppermute x15, starting transfers between devices: 49 us -> 41.4 us  [body(): lax.ppermute(send, 'seq', [(s, shifted(s, shift)) for s in range(shards)])]
    ppermute x6, waiting for transfers between devices: 15.5 us -> 10.1 us  [along(): lax.ppermute(x, 'head', [(s, (s // 2 + shift) % pairs * 2 + s % 2) for s...]
    ppermute x15, waiting for transfers between devices: 50.9 us -> 45.9 us  [body(): lax.ppermute(send, 'seq', [(s, shifted(s, shift)) for s in range(shards)])]
    pallas_call x1 -> x2, Pallas kernels: 11.4 us -> 16.4 us  [project(): pl.pallas_call(functools.partial(project_kernel, widths=widths, scales=le...]
    pallas_call x1 -> x2, Pallas kernels: 4.91 us -> 7.34 us  [dispatch(): pl.pallas_call(functools.partial(dispatch_kernel, shifts=shifts), in_spec...]
  transfers between devices with their start and end apart: 22 -> 22, of which waited for: 11 -> 9; matrix products, arithmetic and copies ran while one was open for 0% -> 0% of each run, Pallas kernels for 19% -> 25%
where the time goes in v5:
time: 156 us
  waiting for transfers between devices  55.9 us (36%)
  starting transfers between devices  53 us (34%)
  Pallas kernels  41.9 us (27%)
  local copies, waits for them, and re-layouts  2.71 us (2%)
  other arithmetic  1.87 us (1%)
    ppermute x15, waiting for transfers between devices, body(): lax.ppermute(send, 'seq', [(s, shifted(s, shift)) for s in range(shards)])  45.9 us
    ppermute x15, starting transfers between devices, body(): lax.ppermute(send, 'seq', [(s, shifted(s, shift)) for s in range(shards)])  41.4 us
    pallas_call x2, Pallas kernels, project(): pl.pallas_call(functools.partial(project_kernel, widths=widths, scales=le...  16.4 us
    pallas_call x1, Pallas kernels, attend(): pl.pallas_call(functools.partial(attend_kernel, tiles=tiles, heads=querie...  11 us
    ppermute x6, waiting for transfers between devices, along(): lax.ppermute(x, 'head', [(s, (s // 2 + shift) % pairs * 2 + s % 2) for s...  10.1 us
    ppermute x6, starting transfers between devices, along(): lax.ppermute(x, 'head', [(s, (s // 2 + shift) % pairs * 2 + s % 2) for s...  9.64 us
    pallas_call x2, Pallas kernels, dispatch(): pl.pallas_call(functools.partial(dispatch_kernel, shifts=shifts), in_spec...  7.34 us
    pallas_call x2, Pallas kernels, mix(): pl.pallas_call(mix_kernel, grid_spec=pltpu.PrefetchScalarGridSpec(num_sca...  5.45 us
  transfers between devices with their start and end apart: 22, of which 9 were waited for; matrix products, arithmetic and copies ran while one was open for 0% of the time, Pallas kernels for 25%

profile of v5, /device:TPU:7, one launch (start us, length us, event | category | flops | bytes accessed | tf_op | source)
XLA Modules:
  0.0 155.6 jit_solution(7301584645759076891)
XLA Ops:
  0.0 1.3 collective-permute-start.2
  1.3 1.4 collective-permute-start.3
  2.7 1.7 %tables.1 = (s32[8,128]{1,0:T(8,128)}, s32[4,256]{1,0:T(4,128)}) custom-call(s32[1]{0:T(128)} %bitcast.3.me_ref, s32[4,256]{1,0:T(4,128)} %bitcast.21), custom_call_target="tpu_custom_call" | custom-call | tf_op jit(solution)/shard_map/tables/pallas_call | solution.py:260
  4.4 9.2 %project.2.held_ref.own_ref = bf16[16,128,512]{2,1,0:T(8,128)(2,1)} custom-call(bf16[2048,2048]{1,0:T(8,128)(2,1)} %refs_0_.2, f32[16,128]{1,0:T(8,128)} %bitcast.19, bf16[3,2048,256]{2,1,0:T(8,128)(2,1)} %bitcast.16, bf16[3,2048,256]{2,1,0:T(8,128)(2,1)} %bitcast.17), custom_call_target="tpu_custom_call" | custom-call | tf_op jit(solution)/shard_map/project/pallas_call | solution.py:105
  13.6 3.3 %dispatch.2 = (bf16[4,128,512]{2,1,0:T(8,128)(2,1)}, bf16[4,128,512]{2,1,0:T(8,128)(2,1)}, bf16[4,128,512]{2,1,0:T(8,128)(2,1)}, bf16[4,128,512]{2,1,0:T(8,128)(2,1)}, bf16[4,128,512]{2,1,0:T(8,128)(2,1)}) custom-call(s32[1]{0:T(128)} %bitcast.3.me_ref, s32[8,128]{1,0:T(8,128)} %get-tuple-element.51.chosen_ref, bf16[16,128,512]{2,1,0:T(8,128)(2,1)} %project.2.held_ref.own_ref), custom_call_target="tpu_custom_call" | custom-call | tf_op jit(solution)/shard_map/dispatch/pallas_call | solution.py:140
  16.9 4.5 %collective-permute-start = (bf16[4,128,512]{2,1,0:T(8,128)(2,1)}, bf16[4,128,512]{2,1,0:T(8,128)(2,1)S(1)}, u32[]{:S(2)}, u32[]{:S(2)}) collective-permute-start(bf16[4,128,512]{2,1,0:T(8,128)(2,1)} %get-tuple-element.58), channel_id=1, source_target_pairs={{0,80},{8,88},{16,64},{24,72},{32,112},{40,120},{48,96},{56,104},{... | collective-permute-start | bytes 1572872 | tf_op jit(solution)/shard_map/ppermute | solution.py:282
  21.4 2.3 %collective-permute-start.1 = (bf16[4,128,512]{2,1,0:T(8,128)(2,1)}, bf16[4,128,512]{2,1,0:T(8,128)(2,1)}, u32[]{:S(2)}, u32[]{:S(2)}) collective-permute-start(bf16[4,128,512]{2,1,0:T(8,128)(2,1)} %get-tuple-element.59), channel_id=1, source_target_pairs={{0,48},{8,56},{16,32},{24,40},{32,80},{40,88},{48,64},{56,72},{64,... | collective-permute-start | bytes 1572872 | tf_op jit(solution)/shard_map/ppermute | solution.py:282
  23.7 4.1 %dispatch.3 = (bf16[4,128,512]{2,1,0:T(8,128)(2,1)}, bf16[4,128,512]{2,1,0:T(8,128)(2,1)}, bf16[4,128,512]{2,1,0:T(8,128)(2,1)}, bf16[4,128,512]{2,1,0:T(8,128)(...) custom-call(s32[1]{0:T(128)} %bitcast.3.me_ref, ...), custom_call_target="tpu_custom_call" | custom-call | tf_op jit(solution)/shard_map/dispatch/pallas_call | solution.py:140
  27.8 0.0 collective-permute-done.3.refs_7_
  27.8 2.0 %collective-permute-start.4 = (bf16[4,128,512]{2,1,0:T(8,128)(2,1)}, bf16[4,128,512]{2,1,0:T(8,128)(2,1)S(1)}, u32[]{:S(2)}, u32[]{:S(2)}) collective-permute-start(bf16[4,128,512]{2,1,0:T(8,128)(2,1)} %get-tuple-element.74), channel_id=1, source_target_pairs={{0,96},{8,104},{16,112},{24,120},{32,0},{40,8},{48,16},{56,24},{64... | collective-permute-start | bytes 1572872 | tf_op jit(solution)/shard_map/ppermute | solution.py:282
  29.8 0.9 collective-permute-start.5
  30.7 1.4 collective-permute-start.6
  32.1 1.2 collective-permute-done.rest_0_
  33.3 3.5 %collective-permute-start.12 = (bf16[4,128,512]{2,1,0:T(8,128)(2,1)}, bf16[4,128,512]{2,1,0:T(8,128)(2,1)S(1)}, u32[]{:S(2)}, u32[]{:S(2)}) collective-permute-start(bf16[4,128,512]{2,1,0:T(8,128)(2,1)} %get-tuple-element.82), channel_id=1, source_target_pairs={{0,72},{8,80},{16,88},{24,64},{32,104},{40,112},{48,120},{56,96},{... | collective-permute-start | bytes 1572872 | tf_op jit(solution)/shard_map/ppermute | solution.py:282
  36.9 8.9 %collective-permute-done.1.rest_1_ = bf16[4,128,512]{2,1,0:T(8,128)(2,1)} collective-permute-done((bf16[4,128,512]{2,1,0:T(8,128)(2,1)}, bf16[4,128,512]{2,1,0:T(8,128)(2,1)}, u32[]{:S(2)}, u32[]{:S(2)}) %collective-permute-start.1) | collective-permute-done | bytes 524320 | tf_op jit(solution)/shard_map/ppermute | solution.py:282
  45.7 0.6 collective-permute-start.7
  46.4 2.4 %collective-permute-done.4.rest_2_ = bf16[4,128,512]{2,1,0:T(8,128)(2,1)S(1)} collective-permute-done((bf16[4,128,512]{2,1,0:T(8,128)(2,1)}, bf16[4,128,512]{2,1,0:T(8,128)(2,1)S(1)}, u32[]{:S(2)}, u32[]{:S(2)}) %collective-permute-start.4) | collective-permute-done | bytes 524320 | tf_op jit(solution)/shard_map/ppermute | solution.py:282
  48.8 11.4 %collective-permute-start.8 = (bf16[4,128,512]{2,1,0:T(8,128)(2,1)}, bf16[4,128,512]{2,1,0:T(8,128)(2,1)S(1)}, u32[]{:S(2)}, u32[]{:S(2)}) collective-permute-start(bf16[4,128,512]{2,1,0:T(8,128)(2,1)} %get-tuple-element.78), channel_id=1, source_target_pairs={{0,88},{8,64},{16,72},{24,80},{32,120},{40,96},{48,104},{56,112},{... | collective-permute-start | bytes 1572872 | tf_op jit(solution)/shard_map/ppermute | solution.py:282
  60.1 0.0 collective-permute-done.5.rest_3_
  60.1 3.0 %collective-permute-start.9 = (bf16[4,128,512]{2,1,0:T(8,128)(2,1)}, bf16[4,128,512]{2,1,0:T(8,128)(2,1)S(1)}, u32[]{:S(2)}, u32[]{:S(2)}) collective-permute-start(bf16[4,128,512]{2,1,0:T(8,128)(2,1)} %get-tuple-element.79), channel_id=1, source_target_pairs={{0,8},{8,16},{16,24},{24,0},{32,40},{40,48},{48,56},{56,32},{64,72... | collective-permute-start | bytes 1572872 | tf_op jit(solution)/shard_map/ppermute | solution.py:282
  63.1 14.9 %collective-permute-done.6.rest_4_ = bf16[4,128,512]{2,1,0:T(8,128)(2,1)S(1)} collective-permute-done((bf16[4,128,512]{2,1,0:T(8,128)(2,1)}, bf16[4,128,512]{2,1,0:T(8,128)(2,1)S(1)}, u32[]{:S(2)}, u32[]{:S(2)}) %collective-permute-start.6) | collective-permute-done | bytes 524320 | tf_op jit(solution)/shard_map/ppermute | solution.py:282
  78.0 3.6 %collective-permute-start.11 = (bf16[4,128,512]{2,1,0:T(8,128)(2,1)}, bf16[4,128,512]{2,1,0:T(8,128)(2,1)S(1)}, u32[]{:S(2)}, u32[]{:S(2)}) collective-permute-start(bf16[4,128,512]{2,1,0:T(8,128)(2,1)} %get-tuple-element.81), channel_id=1, source_target_pairs={{0,120},{8,96},{16,104},{24,112},{32,24},{40,0},{48,8},{56,16},{64... | collective-permute-start | bytes 1572872 | tf_op jit(solution)/shard_map/ppermute | solution.py:282
  81.6 0.1 collective-permute-start.20
  81.7 0.0 collective-permute-done.8.rest_6_
  81.8 0.1 collective-permute-start.13
  81.8 0.0 collective-permute-done.9.rest_7_
  81.9 0.6 copy-done.7
  82.4 4.3 %collective-permute-start.14 = (bf16[4,128,512]{2,1,0:T(8,128)(2,1)}, bf16[4,128,512]{2,1,0:T(8,128)(2,1)}, u32[]{:S(2)}, u32[]{:S(2)}) collective-permute-start(bf16[4,128,512]{2,1,0:T(8,128)(2,1)} %get-tuple-element.85), channel_id=1, source_target_pairs={{0,104},{8,112},{16,120},{24,96},{32,8},{40,16},{48,24},{56,0},{64... | collective-permute-start | bytes 1572872 | tf_op jit(solution)/shard_map/ppermute | solution.py:282
  86.7 6.0 %collective-permute-done.10.rest_8_ = bf16[4,128,512]{2,1,0:T(8,128)(2,1)S(1)} collective-permute-done((bf16[4,128,512]{2,1,0:T(8,128)(2,1)}, bf16[4,128,512]{2,1,0:T(8,128)(2,1)S(1)}, u32[]{:S(2)}, u32[]{:S(2)}) %collective-permute-start.10) | collective-permute-done | bytes 524320 | tf_op jit(solution)/shard_map/ppermute | solution.py:282
  92.7 0.4 collective-permute-start.15
  93.1 0.3 copy-done.10
  93.5 0.8 copy-done.11
  94.3 3.4 %collective-permute-start.16 = (bf16[4,128,512]{2,1,0:T(8,128)(2,1)}, bf16[4,128,512]{2,1,0:T(8,128)(2,1)}, u32[]{:S(2)}, u32[]{:S(2)}) collective-permute-start(bf16[4,128,512]{2,1,0:T(8,128)(2,1)} %get-tuple-element.87), channel_id=1, source_target_pairs={{0,64},{8,72},{16,80},{24,88},{32,96},{40,104},{48,112},{56,120},{... | collective-permute-start | bytes 1572872 | tf_op jit(solution)/shard_map/ppermute | solution.py:282
  97.7 7.2 %project.3.queries_ref = bf16[16,128,256]{2,1,0:T(8,128)(2,1)} custom-call(bf16[2048,2048]{1,0:T(8,128)(2,1)} %refs_0_.2, f32[16,128]{1,0:T(8,128)} %bitcast.20, bf16[3,2048,256]{2,1,0:T(8,128)(2,1)} %bitcast.18), custom_call_target="tpu_custom_call" | custom-call | tf_op jit(solution)/shard_map/project/pallas_call | solution.py:105
  104.9 0.6 pad_add_fusion.first_ref
  105.5 12.3 %collective-permute-done.13.rest_11_ = bf16[4,128,512]{2,1,0:T(8,128)(2,1)} collective-permute-done((bf16[4,128,512]{2,1,0:T(8,128)(2,1)}, bf16[4,128,512]{2,1,0:T(8,128)(2,1)}, u32[]{:S(2)}, u32[]{:S(2)}) %collective-permute-start.13) | collective-permute-done | bytes 524320 | tf_op jit(solution)/shard_map/ppermute | solution.py:282
  117.8 0.2 collective-permute-done.16.rest_14_
  118.0 11.0 %attend.1 = (bf16[512,256]{1,0:T(8,128)(2,1)}, bf16[512,256]{1,0:T(8,128)(2,1)}, bf16[512,256]{1,0:T(8,128)(2,1)}, bf16[512,256]{1,0:T(8,128)(2,1)}) custom-call(s32[2]{0:T(128)} %pad_add_fusion.first_ref, s32[4,256]{1,0:T(4,128)} %get-tuple-element.50.source_ref, bf16[16,128,256]{2,1,0:T(8,128)(2,1)} %project.3.queries_ref, ...), custom_call_target="tpu_custom_call" | custom-call | tf_op jit(solution)/shard_map/attend/pallas_call | solution.py:202
  129.0 2.9 %collective-permute-start.17 = (bf16[512,256]{1,0:T(8,128)(2,1)}, bf16[512,256]{1,0:T(8,128)(2,1)S(1)}, u32[]{:S(2)}, u32[]{:S(2)}) collective-permute-start(bf16[512,256]{1,0:T(8,128)(2,1)} %get-tuple-element.89), channel_id=1, source_target_pairs={{0,2},{1,3},{2,4},{3,5},{4,6},{5,7},{6,0},{7,1},{8,10},{9,11},{10,... | collective-permute-start | bytes 786440 | tf_op jit(solution)/shard_map/ppermute | solution.py:258
  131.9 2.7 %collective-permute-start.18 = (bf16[512,256]{1,0:T(8,128)(2,1)}, bf16[512,256]{1,0:T(8,128)(2,1)}, u32[]{:S(2)}, u32[]{:S(2)}) collective-permute-start(bf16[512,256]{1,0:T(8,128)(2,1)} %get-tuple-element.90), channel_id=1, source_target_pairs={{0,4},{1,5},{2,6},{3,7},{4,0},{5,1},{6,2},{7,3},{8,12},{9,13},{10,... | collective-permute-start | bytes 786440 | tf_op jit(solution)/shard_map/ppermute | solution.py:258
  134.6 1.2 collective-permute-start.19
  135.8 3.5 %collective-permute-done.17 = bf16[512,256]{1,0:T(8,128)(2,1)S(1)} collective-permute-done((bf16[512,256]{1,0:T(8,128)(2,1)}, bf16[512,256]{1,0:T(8,128)(2,1)S(1)}, u32[]{:S(2)}, u32[]{:S(2)}) %collective-permute-start.17) | collective-permute-done | bytes 262176 | tf_op jit(solution)/shard_map/ppermute | solution.py:258
  139.3 6.6 %collective-permute-done.18 = bf16[512,256]{1,0:T(8,128)(2,1)} collective-permute-done((bf16[512,256]{1,0:T(8,128)(2,1)}, bf16[512,256]{1,0:T(8,128)(2,1)}, u32[]{:S(2)}, u32[]{:S(2)}) %collective-permute-start.18) | collective-permute-done | bytes 262176 | tf_op jit(solution)/shard_map/ppermute | solution.py:258
  145.9 0.9 copy-done.1
  146.9 2.7 %mix.3 = bf16[256,2048]{1,0:T(8,128)(2,1)S(1)} custom-call(s32[1]{0:T(128)} %bitcast.11.half_ref, bf16[2,256,256]{2,1,0:T(8,128)(2,1)S(1)} %bitcast.12, bf16[2,256,256]{2,1,0:T(8,128)(2,1)S(1)} %bitcast.14, bf16[2,256,256]{2,1,0:T(8,128)(2,1)} %bitcast.9.refs_2_, bf16[2,256,256]{2,1,0:T(8,128)(2,1)} %bitcast.10.refs_3_, bf16[256,2048]{1,0:T(8,128)(2,1)S(1)} %copy-done, ...), custom_call_target="tpu_custom_call" | custom-call | tf_op jit(solution)/shard_map/mix/pallas_call | solution.py:228
  149.6 2.0 %collective-permute-start.21 = (bf16[256,2048]{1,0:T(8,128)(2,1)S(1)}, bf16[256,2048]{1,0:T(8,128)(2,1)S(1)}, u32[]{:S(2)}, u32[]{:S(2)}) collective-permute-start(bf16[256,2048]{1,0:T(8,128)(2,1)S(1)} %mix.3), channel_id=1, source_target_pairs={{0,1},{1,0},{2,3},{3,2},{4,5},{5,4},{6,7},{7,6},{8,9},{9,8},{10,11... | collective-permute-start | bytes 3145736 | tf_op jit(solution)/shard_map/ppermute | solution.py:290
  151.5 2.8 %mix.2 = f32[256,2048]{1,0:T(8,128)S(1)} custom-call(s32[1]{0:T(128)} %bitcast.half_ref, bf16[2,256,256]{2,1,0:T(8,128)(2,1)S(1)} %bitcast.13, bf16[2,256,256]{2,1,0:T(8,128)(2,1)S(1)} %bitcast.15, bf16[2,256,256]{2,1,0:T(8,128)(2,1)} %bitcast.9.refs_2_, bf16[2,256,256]{2,1,0:T(8,128)(2,1)} %bitcast.10.refs_3_, bf16[256,2048]{1,0:T(8,128)(2,1)S(1)} %copy-done, ...), custom_call_target="tpu_custom_call" | custom-call | tf_op jit(solution)/shard_map/mix/pallas_call | solution.py:228
  154.3 1.3 add_convert_fusion
  (30 shorter events, 0.1 us)
Async XLA Ops:
  0.0 27.8 %collective-permute-start.2 = (bf16[256,2048]{1,0:T(8,128)(2,1)}, bf16[256,2048]{1,0:T(8,128)(2,1)S(1)}, u32[]{:S(2)}, u32[]{:S(2)}) collective-permute-start(bf16[256,2048]{1,0:T(8,128)(2,1)} %refs_4_.3), channel_id=1, source_target_pairs={{0,2},{1,3},{2,4},{3,5},{4,6},{5,7},{6,0},{7,1},{8,10},{9,11},{10,... | collective-permute-start | bytes 3145736 | tf_op jit(solution)/shard_map/ppermute | solution.py:258
  1.3 26.5 %collective-permute-start.3 = (bf16[256,2048]{1,0:T(8,128)(2,1)}, bf16[256,2048]{1,0:T(8,128)(2,1)S(1)}, u32[]{:S(2)}, u32[]{:S(2)}) collective-permute-start(bf16[256,2048]{1,0:T(8,128)(2,1)} %refs_4_.3), channel_id=1, source_target_pairs={{0,6},{1,7},{2,0},{3,1},{4,2},{5,3},{6,4},{7,5},{8,14},{9,15},{10,... | collective-permute-start | bytes 3145736 | tf_op jit(solution)/shard_map/ppermute | solution.py:258
  13.6 68.0 %copy-start = (bf16[256,2048]{1,0:T(8,128)(2,1)S(1)}, bf16[256,2048]{1,0:T(8,128)(2,1)}, u32[]{:S(2)}) copy-start(bf16[256,2048]{1,0:T(8,128)(2,1)} %refs_4_.3) | copy-start | bytes 3145732
  16.9 16.4 %collective-permute-start = (bf16[4,128,512]{2,1,0:T(8,128)(2,1)}, bf16[4,128,512]{2,1,0:T(8,128)(2,1)S(1)}, u32[]{:S(2)}, u32[]{:S(2)}) collective-permute-start(bf16[4,128,512]{2,1,0:T(8,128)(2,1)} %get-tuple-element.58), channel_id=1, source_target_pairs={{0,80},{8,88},{16,64},{24,72},{32,112},{40,120},{48,96},{56,104},{... | collective-permute-start | bytes 1572872 | tf_op jit(solution)/shard_map/ppermute | solution.py:282
  21.4 24.3 %collective-permute-start.1 = (bf16[4,128,512]{2,1,0:T(8,128)(2,1)}, bf16[4,128,512]{2,1,0:T(8,128)(2,1)}, u32[]{:S(2)}, u32[]{:S(2)}) collective-permute-start(bf16[4,128,512]{2,1,0:T(8,128)(2,1)} %get-tuple-element.59), channel_id=1, source_target_pairs={{0,48},{8,56},{16,32},{24,40},{32,80},{40,88},{48,64},{56,72},{64,... | collective-permute-start | bytes 1572872 | tf_op jit(solution)/shard_map/ppermute | solution.py:282
  27.8 20.9 %collective-permute-start.4 = (bf16[4,128,512]{2,1,0:T(8,128)(2,1)}, bf16[4,128,512]{2,1,0:T(8,128)(2,1)S(1)}, u32[]{:S(2)}, u32[]{:S(2)}) collective-permute-start(bf16[4,128,512]{2,1,0:T(8,128)(2,1)} %get-tuple-element.74), channel_id=1, source_target_pairs={{0,96},{8,104},{16,112},{24,120},{32,0},{40,8},{48,16},{56,24},{64... | collective-permute-start | bytes 1572872 | tf_op jit(solution)/shard_map/ppermute | solution.py:282
  29.8 30.3 %collective-permute-start.5 = (bf16[4,128,512]{2,1,0:T(8,128)(2,1)}, bf16[4,128,512]{2,1,0:T(8,128)(2,1)S(1)}, u32[]{:S(2)}, u32[]{:S(2)}) collective-permute-start(bf16[4,128,512]{2,1,0:T(8,128)(2,1)} %get-tuple-element.75), channel_id=1, source_target_pairs={{0,112},{8,120},{16,96},{24,104},{32,16},{40,24},{48,0},{56,8},{64... | collective-permute-start | bytes 1572872 | tf_op jit(solution)/shard_map/ppermute | solution.py:282
  30.7 47.3 %collective-permute-start.6 = (bf16[4,128,512]{2,1,0:T(8,128)(2,1)}, bf16[4,128,512]{2,1,0:T(8,128)(2,1)S(1)}, u32[]{:S(2)}, u32[]{:S(2)}) collective-permute-start(bf16[4,128,512]{2,1,0:T(8,128)(2,1)} %get-tuple-element.76), channel_id=1, source_target_pairs={{0,32},{8,40},{16,48},{24,56},{32,64},{40,72},{48,80},{56,88},{64,... | collective-permute-start | bytes 1572872 | tf_op jit(solution)/shard_map/ppermute | solution.py:282
  33.3 48.3 %copy-start.2 = (bf16[4,128,512]{2,1,0:T(8,128)(2,1)}, bf16[4,128,512]{2,1,0:T(8,128)(2,1)S(1)}, u32[]{:S(2)}) copy-start(bf16[4,128,512]{2,1,0:T(8,128)(2,1)S(1)} %collective-permute-done.rest_0_) | copy-start | bytes 1572868
  33.3 44.7 %collective-permute-start.12 = (bf16[4,128,512]{2,1,0:T(8,128)(2,1)}, bf16[4,128,512]{2,1,0:T(8,128)(2,1)S(1)}, u32[]{:S(2)}, u32[]{:S(2)}) collective-permute-start(bf16[4,128,512]{2,1,0:T(8,128)(2,1)} %get-tuple-element.82), channel_id=1, source_target_pairs={{0,72},{8,80},{16,88},{24,64},{32,104},{40,112},{48,120},{56,96},{... | collective-permute-start | bytes 1572872 | tf_op jit(solution)/shard_map/ppermute | solution.py:282
  45.7 35.9 %collective-permute-start.7 = (bf16[4,128,512]{2,1,0:T(8,128)(2,1)}, bf16[4,128,512]{2,1,0:T(8,128)(2,1)S(1)}, u32[]{:S(2)}, u32[]{:S(2)}) collective-permute-start(bf16[4,128,512]{2,1,0:T(8,128)(2,1)} %get-tuple-element.77), channel_id=1, source_target_pairs={{0,24},{8,0},{16,8},{24,16},{32,56},{40,32},{48,40},{56,48},{64,88... | collective-permute-start | bytes 1572872 | tf_op jit(solution)/shard_map/ppermute | solution.py:282
  48.8 32.8 %copy-start.3 = (bf16[4,128,512]{2,1,0:T(8,128)(2,1)}, bf16[4,128,512]{2,1,0:T(8,128)(2,1)S(1)}, u32[]{:S(2)}) copy-start(bf16[4,128,512]{2,1,0:T(8,128)(2,1)S(1)} %collective-permute-done.4.rest_2_) | copy-start | bytes 1572868
  48.8 33.0 %collective-permute-start.8 = (bf16[4,128,512]{2,1,0:T(8,128)(2,1)}, bf16[4,128,512]{2,1,0:T(8,128)(2,1)S(1)}, u32[]{:S(2)}, u32[]{:S(2)}) collective-permute-start(bf16[4,128,512]{2,1,0:T(8,128)(2,1)} %get-tuple-element.78), channel_id=1, source_target_pairs={{0,88},{8,64},{16,72},{24,80},{32,120},{40,96},{48,104},{56,112},{... | collective-permute-start | bytes 1572872 | tf_op jit(solution)/shard_map/ppermute | solution.py:282
  60.1 21.6 %copy-start.4 = (bf16[4,128,512]{2,1,0:T(8,128)(2,1)}, bf16[4,128,512]{2,1,0:T(8,128)(2,1)S(1)}, u32[]{:S(2)}) copy-start(bf16[4,128,512]{2,1,0:T(8,128)(2,1)S(1)} %collective-permute-done.5.rest_3_) | copy-start | bytes 1572868
  60.1 21.7 %collective-permute-start.9 = (bf16[4,128,512]{2,1,0:T(8,128)(2,1)}, bf16[4,128,512]{2,1,0:T(8,128)(2,1)S(1)}, u32[]{:S(2)}, u32[]{:S(2)}) collective-permute-start(bf16[4,128,512]{2,1,0:T(8,128)(2,1)} %get-tuple-element.79), channel_id=1, source_target_pairs={{0,8},{8,16},{16,24},{24,0},{32,40},{40,48},{48,56},{56,32},{64,72... | collective-permute-start | bytes 1572872 | tf_op jit(solution)/shard_map/ppermute | solution.py:282
  78.0 3.7 %copy-start.5 = (bf16[4,128,512]{2,1,0:T(8,128)(2,1)}, bf16[4,128,512]{2,1,0:T(8,128)(2,1)S(1)}, u32[]{:S(2)}) copy-start(bf16[4,128,512]{2,1,0:T(8,128)(2,1)S(1)} %collective-permute-done.6.rest_4_) | copy-start | bytes 1572868
  78.0 14.7 %collective-permute-start.10 = (bf16[4,128,512]{2,1,0:T(8,128)(2,1)}, bf16[4,128,512]{2,1,0:T(8,128)(2,1)S(1)}, u32[]{:S(2)}, u32[]{:S(2)}) collective-permute-start(bf16[4,128,512]{2,1,0:T(8,128)(2,1)} %get-tuple-element.80), channel_id=1, source_target_pairs={{0,40},{8,48},{16,56},{24,32},{32,72},{40,80},{48,88},{56,64},{64,... | collective-permute-start | bytes 1572872 | tf_op jit(solution)/shard_map/ppermute | solution.py:282
  78.0 3.8 %copy-start.6 = (bf16[4,128,512]{2,1,0:T(8,128)(2,1)}, bf16[4,128,512]{2,1,0:T(8,128)(2,1)S(1)}, u32[]{:S(2)}) copy-start(bf16[4,128,512]{2,1,0:T(8,128)(2,1)S(1)} %collective-permute-done.12.rest_10_) | copy-start | bytes 1572868
  78.0 15.4 %collective-permute-start.11 = (bf16[4,128,512]{2,1,0:T(8,128)(2,1)}, bf16[4,128,512]{2,1,0:T(8,128)(2,1)S(1)}, u32[]{:S(2)}, u32[]{:S(2)}) collective-permute-start(bf16[4,128,512]{2,1,0:T(8,128)(2,1)} %get-tuple-element.81), channel_id=1, source_target_pairs={{0,120},{8,96},{16,104},{24,112},{32,24},{40,0},{48,8},{56,16},{64... | collective-permute-start | bytes 1572872 | tf_op jit(solution)/shard_map/ppermute | solution.py:282
  81.6 0.8 copy-start.7
  81.6 64.3 %collective-permute-start.20 = (bf16[256,2048]{1,0:T(8,128)(2,1)S(1)}, bf16[256,2048]{1,0:T(8,128)(2,1)}, u32[]{:S(2)}, u32[]{:S(2)}) collective-permute-start(bf16[256,2048]{1,0:T(8,128)(2,1)S(1)} %copy-done), channel_id=1, source_target_pairs={{0,4},{1,5},{2,6},{3,7},{4,0},{5,1},{6,2},{7,3},{8,12},{9,13},{10,... | collective-permute-start | bytes 3145736 | tf_op jit(solution)/shard_map/ppermute | solution.py:258
  81.7 5.0 %copy-start.8 = (bf16[4,128,512]{2,1,0:T(8,128)(2,1)}, bf16[4,128,512]{2,1,0:T(8,128)(2,1)S(1)}, u32[]{:S(2)}) copy-start(bf16[4,128,512]{2,1,0:T(8,128)(2,1)S(1)} %collective-permute-done.8.rest_6_) | copy-start | bytes 1572868
  81.8 36.1 %collective-permute-start.13 = (bf16[4,128,512]{2,1,0:T(8,128)(2,1)}, bf16[4,128,512]{2,1,0:T(8,128)(2,1)}, u32[]{:S(2)}, u32[]{:S(2)}) collective-permute-start(bf16[4,128,512]{2,1,0:T(8,128)(2,1)} %get-tuple-element.84), channel_id=1, source_target_pairs={{0,56},{8,32},{16,40},{24,48},{32,88},{40,64},{48,72},{56,80},{64,... | collective-permute-start | bytes 1572872 | tf_op jit(solution)/shard_map/ppermute | solution.py:282
  82.4 10.2 %copy-start.9 = (bf16[4,128,512]{2,1,0:T(8,128)(2,1)}, bf16[4,128,512]{2,1,0:T(8,128)(2,1)S(1)}, u32[]{:S(2)}) copy-start(bf16[4,128,512]{2,1,0:T(8,128)(2,1)S(1)} %collective-permute-done.9.rest_7_) | copy-start | bytes 1572868
  82.4 35.4 %collective-permute-start.14 = (bf16[4,128,512]{2,1,0:T(8,128)(2,1)}, bf16[4,128,512]{2,1,0:T(8,128)(2,1)}, u32[]{:S(2)}, u32[]{:S(2)}) collective-permute-start(bf16[4,128,512]{2,1,0:T(8,128)(2,1)} %get-tuple-element.85), channel_id=1, source_target_pairs={{0,104},{8,112},{16,120},{24,96},{32,8},{40,16},{48,24},{56,0},{64... | collective-permute-start | bytes 1572872 | tf_op jit(solution)/shard_map/ppermute | solution.py:282
  92.7 0.8 copy-start.10
  92.7 25.1 %collective-permute-start.15 = (bf16[4,128,512]{2,1,0:T(8,128)(2,1)}, bf16[4,128,512]{2,1,0:T(8,128)(2,1)}, u32[]{:S(2)}, u32[]{:S(2)}) collective-permute-start(bf16[4,128,512]{2,1,0:T(8,128)(2,1)} %get-tuple-element.86), channel_id=1, source_target_pairs={{0,16},{8,24},{16,0},{24,8},{32,48},{40,56},{48,32},{56,40},{64,80... | collective-permute-start | bytes 1572872 | tf_op jit(solution)/shard_map/ppermute | solution.py:282
  93.5 0.8 copy-start.11
  94.3 23.7 %collective-permute-start.16 = (bf16[4,128,512]{2,1,0:T(8,128)(2,1)}, bf16[4,128,512]{2,1,0:T(8,128)(2,1)}, u32[]{:S(2)}, u32[]{:S(2)}) collective-permute-start(bf16[4,128,512]{2,1,0:T(8,128)(2,1)} %get-tuple-element.87), channel_id=1, source_target_pairs={{0,64},{8,72},{16,80},{24,88},{32,96},{40,104},{48,112},{56,120},{... | collective-permute-start | bytes 1572872 | tf_op jit(solution)/shard_map/ppermute | solution.py:282
  129.0 10.3 %collective-permute-start.17 = (bf16[512,256]{1,0:T(8,128)(2,1)}, bf16[512,256]{1,0:T(8,128)(2,1)S(1)}, u32[]{:S(2)}, u32[]{:S(2)}) collective-permute-start(bf16[512,256]{1,0:T(8,128)(2,1)} %get-tuple-element.89), channel_id=1, source_target_pairs={{0,2},{1,3},{2,4},{3,5},{4,6},{5,7},{6,0},{7,1},{8,10},{9,11},{10,... | collective-permute-start | bytes 786440 | tf_op jit(solution)/shard_map/ppermute | solution.py:258
  131.9 14.0 %collective-permute-start.18 = (bf16[512,256]{1,0:T(8,128)(2,1)}, bf16[512,256]{1,0:T(8,128)(2,1)}, u32[]{:S(2)}, u32[]{:S(2)}) collective-permute-start(bf16[512,256]{1,0:T(8,128)(2,1)} %get-tuple-element.90), channel_id=1, source_target_pairs={{0,4},{1,5},{2,6},{3,7},{4,0},{5,1},{6,2},{7,3},{8,12},{9,13},{10,... | collective-permute-start | bytes 786440 | tf_op jit(solution)/shard_map/ppermute | solution.py:258
  134.6 11.3 %collective-permute-start.19 = (bf16[512,256]{1,0:T(8,128)(2,1)}, bf16[512,256]{1,0:T(8,128)(2,1)}, u32[]{:S(2)}, u32[]{:S(2)}) collective-permute-start(bf16[512,256]{1,0:T(8,128)(2,1)} %get-tuple-element.91), channel_id=1, source_target_pairs={{0,6},{1,7},{2,0},{3,1},{4,2},{5,3},{6,4},{7,5},{8,14},{9,15},{10,... | collective-permute-start | bytes 786440 | tf_op jit(solution)/shard_map/ppermute | solution.py:258
  145.9 1.0 copy-start.1
  149.6 4.7 %collective-permute-start.21 = (bf16[256,2048]{1,0:T(8,128)(2,1)S(1)}, bf16[256,2048]{1,0:T(8,128)(2,1)S(1)}, u32[]{:S(2)}, u32[]{:S(2)}) collective-permute-start(bf16[256,2048]{1,0:T(8,128)(2,1)S(1)} %mix.3), channel_id=1, source_target_pairs={{0,1},{1,0},{2,3},{3,2},{4,5},{5,4},{6,7},{7,6},{8,9},{9,8},{10,11... | collective-permute-start | bytes 3145736 | tf_op jit(solution)/shard_map/ppermute | solution.py:290

commit v6 on v5

--- a/solution.py
+++ b/solution.py
@@ -17,6 +17,7 @@
 SIDE = 4
 SHIFTS = (10, 6, 12, 14, 4, 3, 11, 1, 5, 15, 9, 7, 13, 2, 8)
 FIRST = 5
+STEPS = ((1, 2, 3), (0,))
 ALONE = 2
 LATE = 10
 COLUMNS = 1024
@@ -151,8 +152,9 @@
     )(me, chosen, held)
 
 
-def attend_kernel(first_ref, source_ref, queries_ref, own_ref, *rest, tiles, heads, pairs):
-    incoming_refs, out_refs, held, semaphores = rest[: -2 - pairs], rest[-2 - pairs : -2], rest[-2], rest[-1]
+def attend_kernel(first_ref, source_ref, queries_ref, own_ref, *rest, tiles, heads, pairs, steps):
+    count = len(steps)
+    incoming_refs, out_refs, held, semaphores = rest[: -2 - count], rest[-2 - count : -2], rest[-2], rest[-1]
     copies = []
     for p, shift in enumerate(SHIFTS):
         copies.append(
@@ -163,8 +165,8 @@
         copy.wait()
     scale = 1.0 / math.sqrt(HD) * math.log2(math.e)
     share = tiles // pairs
-    for start in range(0, tiles, GROUP):
-        block = (first_ref[1] + start // share) % pairs * share
+    for start in range(0, share * count, GROUP):
+        block = (first_ref[1] + steps[start // share]) % pairs * share
         group = [block + (start + g) % share for g in range(GROUP)]
         blocks = [
             [own_ref.at[i]] + [held.at[source_ref[j, first_ref[0] + i]] for j in range(1, KT)] for i in group
@@ -196,14 +198,14 @@
             ).astype(jnp.bfloat16)
 
 
-def attend(first, source, queries, own, incoming, pairs):
+def attend(first, source, queries, own, incoming, pairs, steps):
     tiles = own.shape[0]
     vmem, smem = pl.BlockSpec(memory_space=pltpu.VMEM), pl.BlockSpec(memory_space=pltpu.SMEM)
     return pl.pallas_call(
-        functools.partial(attend_kernel, tiles=tiles, heads=queries.shape[2] // HD, pairs=pairs),
+        functools.partial(attend_kernel, tiles=tiles, heads=queries.shape[2] // HD, pairs=pairs, steps=steps),
         in_specs=[smem, smem, vmem, vmem] + [pl.BlockSpec(memory_space=pl.ANY)] * len(incoming),
-        out_specs=[vmem] * pairs,
-        out_shape=[jax.ShapeDtypeStruct((tiles * TILE // pairs, queries.shape[2]), jnp.bfloat16)] * pairs,
+        out_specs=[vmem] * len(steps),
+        out_shape=[jax.ShapeDtypeStruct((tiles * TILE // pairs, queries.shape[2]), jnp.bfloat16)] * len(steps),
         scratch_shapes=[
             pltpu.VMEM((SIDE * SIDE * CAP,) + own.shape[1:], jnp.bfloat16),
             pltpu.SemaphoreType.DMA((len(incoming),)),
@@ -283,8 +285,11 @@
     late, incoming[LATE] = lax.optimization_barrier((out_weight, incoming[LATE]))
     mixers[2] = along(late, 2)
     first = jnp.stack([myself * tiles, pair]).astype(jnp.int32)
-    attended = attend(first, source, queries, own, incoming, pairs)
-    lefts = [attended[0]] + [along(attended[shift], shift) for shift in range(1, pairs)]
+    lefts = {}
+    for steps in STEPS:
+        for step, block in zip(steps, attend(first, source, queries, own, incoming, pairs, steps)):
+            lefts[step] = along(block, step) if step else block
+    lefts = [lefts[step] for step in range(pairs)]
     rights = [out_weight] + [mixers[shift] for shift in range(1, pairs)]
     give = mix(jnp.reshape(1 - core, (1,)).astype(jnp.int32), lefts, rights, jnp.bfloat16)
     got = lax.ppermute(give, "head", [(s, s + 1 - s % 2 * 2) for s in range(groups)])

time: 156 us -> 155 us (level)
  waiting for transfers between devices: 55.9 us -> 48.8 us
  Pallas kernels: 41.9 us -> 47.9 us
    ppermute x6, waiting for transfers between devices: 10.1 us -> 2.68 us  [along(): lax.ppermute(x, 'head', [(s, (s // 2 + shift) % pairs * 2 + s % 2) for s...]
    pallas_call x1 -> x2, Pallas kernels: 11 us -> 17.1 us  [attend(): pl.pallas_call(functools.partial(attend_kernel, tiles=tiles, heads=querie...]
  transfers between devices with their start and end apart: 22 -> 22, of which waited for: 9 -> 8; matrix products, arithmetic and copies ran while one was open for 0% -> 0% of each run, Pallas kernels for 25% -> 29%
where the time goes in v6:
time: 155 us; the launch traced here: 154 us
  starting transfers between devices  52.6 us (34%)
  waiting for transfers between devices  48.8 us (31%)
  Pallas kernels  47.9 us (31%)
  local copies, waits for them, and re-layouts  2.83 us (2%)
  other arithmetic  1.87 us (1%)
    ppermute x15, waiting for transfers between devices, body(): lax.ppermute(send, 'seq', [(s, shifted(s, shift)) for s in range(shards)])  46.2 us
    ppermute x15, starting transfers between devices, body(): lax.ppermute(send, 'seq', [(s, shifted(s, shift)) for s in range(shards)])  41 us
    pallas_call x2, Pallas kernels, attend(): pl.pallas_call(functools.partial(attend_kernel, tiles=tiles, heads=querie...  17.1 us
    pallas_call x2, Pallas kernels, project(): pl.pallas_call(functools.partial(project_kernel, widths=widths, scales=le...  16.4 us
    ppermute x6, starting transfers between devices, along(): lax.ppermute(x, 'head', [(s, (s // 2 + shift) % pairs * 2 + s % 2) for s...  9.66 us
    pallas_call x2, Pallas kernels, dispatch(): pl.pallas_call(functools.partial(dispatch_kernel, shifts=shifts), in_spec...  7.29 us
    pallas_call x2, Pallas kernels, mix(): pl.pallas_call(mix_kernel, grid_spec=pltpu.PrefetchScalarGridSpec(num_sca...  5.45 us
  transfers between devices with their start and end apart: 22, of which 8 were waited for; matrix products, arithmetic and copies ran while one was open for 0% of the time, Pallas kernels for 29%

profile of v6, /device:TPU:7, one launch (start us, length us, event | category | flops | bytes accessed | tf_op | source)
XLA Modules:
  0.0 154.3 jit_solution(5290916784639009382)
XLA Ops:
  0.0 1.3 collective-permute-start.2
  1.3 1.4 collective-permute-start.3
  2.7 1.7 %tables.1 = (s32[8,128]{1,0:T(8,128)}, s32[4,256]{1,0:T(4,128)}) custom-call(s32[1]{0:T(128)} %bitcast.3.me_ref, s32[4,256]{1,0:T(4,128)} %bitcast.21), custom_call_target="tpu_custom_call" | custom-call | tf_op jit(solution)/shard_map/tables/pallas_call | solution.py:262
  4.4 9.2 %project.2.held_ref.own_ref = bf16[16,128,512]{2,1,0:T(8,128)(2,1)} custom-call(bf16[2048,2048]{1,0:T(8,128)(2,1)} %refs_0_.2, f32[16,128]{1,0:T(8,128)} %bitcast.19, bf16[3,2048,256]{2,1,0:T(8,128)(2,1)} %bitcast.16, bf16[3,2048,256]{2,1,0:T(8,128)(2,1)} %bitcast.17), custom_call_target="tpu_custom_call" | custom-call | tf_op jit(solution)/shard_map/project/pallas_call | solution.py:106
  13.6 3.3 %dispatch.2 = (bf16[4,128,512]{2,1,0:T(8,128)(2,1)}, bf16[4,128,512]{2,1,0:T(8,128)(2,1)}, bf16[4,128,512]{2,1,0:T(8,128)(2,1)}, bf16[4,128,512]{2,1,0:T(8,128)(2,1)}, bf16[4,128,512]{2,1,0:T(8,128)(2,1)}) custom-call(s32[1]{0:T(128)} %bitcast.3.me_ref, s32[8,128]{1,0:T(8,128)} %get-tuple-element.50.chosen_ref, bf16[16,128,512]{2,1,0:T(8,128)(2,1)} %project.2.held_ref.own_ref), custom_call_target="tpu_custom_call" | custom-call | tf_op jit(solution)/shard_map/dispatch/pallas_call | solution.py:141
  16.9 4.5 %collective-permute-start = (bf16[4,128,512]{2,1,0:T(8,128)(2,1)}, bf16[4,128,512]{2,1,0:T(8,128)(2,1)S(1)}, u32[]{:S(2)}, u32[]{:S(2)}) collective-permute-start(bf16[4,128,512]{2,1,0:T(8,128)(2,1)} %get-tuple-element.57), channel_id=1, source_target_pairs={{0,80},{8,88},{16,64},{24,72},{32,112},{40,120},{48,96},{56,104},{... | collective-permute-start | bytes 1572872 | tf_op jit(solution)/shard_map/ppermute | solution.py:284
  21.4 2.3 %collective-permute-start.1 = (bf16[4,128,512]{2,1,0:T(8,128)(2,1)}, bf16[4,128,512]{2,1,0:T(8,128)(2,1)}, u32[]{:S(2)}, u32[]{:S(2)}) collective-permute-start(bf16[4,128,512]{2,1,0:T(8,128)(2,1)} %get-tuple-element.58), channel_id=1, source_target_pairs={{0,48},{8,56},{16,32},{24,40},{32,80},{40,88},{48,64},{56,72},{64,... | collective-permute-start | bytes 1572872 | tf_op jit(solution)/shard_map/ppermute | solution.py:284
  23.7 4.0 %dispatch.3 = (bf16[4,128,512]{2,1,0:T(8,128)(2,1)}, bf16[4,128,512]{2,1,0:T(8,128)(2,1)}, bf16[4,128,512]{2,1,0:T(8,128)(2,1)}, bf16[4,128,512]{2,1,0:T(8,128)(...) custom-call(s32[1]{0:T(128)} %bitcast.3.me_ref, ...), custom_call_target="tpu_custom_call" | custom-call | tf_op jit(solution)/shard_map/dispatch/pallas_call | solution.py:141
  27.7 0.0 collective-permute-done.2.refs_5_
  27.8 2.0 %collective-permute-start.4 = (bf16[4,128,512]{2,1,0:T(8,128)(2,1)}, bf16[4,128,512]{2,1,0:T(8,128)(2,1)S(1)}, u32[]{:S(2)}, u32[]{:S(2)}) collective-permute-start(bf16[4,128,512]{2,1,0:T(8,128)(2,1)} %get-tuple-element.73), channel_id=1, source_target_pairs={{0,96},{8,104},{16,112},{24,120},{32,0},{40,8},{48,16},{56,24},{64... | collective-permute-start | bytes 1572872 | tf_op jit(solution)/shard_map/ppermute | solution.py:284
  29.8 0.9 collective-permute-start.5
  30.7 1.4 collective-permute-start.6
  32.1 1.3 collective-permute-done.rest_0_
  33.3 3.5 %collective-permute-start.12 = (bf16[4,128,512]{2,1,0:T(8,128)(2,1)}, bf16[4,128,512]{2,1,0:T(8,128)(2,1)S(1)}, u32[]{:S(2)}, u32[]{:S(2)}) collective-permute-start(bf16[4,128,512]{2,1,0:T(8,128)(2,1)} %get-tuple-element.81), channel_id=1, source_target_pairs={{0,72},{8,80},{16,88},{24,64},{32,104},{40,112},{48,120},{56,96},{... | collective-permute-start | bytes 1572872 | tf_op jit(solution)/shard_map/ppermute | solution.py:284
  36.9 8.9 %collective-permute-done.1.rest_1_ = bf16[4,128,512]{2,1,0:T(8,128)(2,1)} collective-permute-done((bf16[4,128,512]{2,1,0:T(8,128)(2,1)}, bf16[4,128,512]{2,1,0:T(8,128)(2,1)}, u32[]{:S(2)}, u32[]{:S(2)}) %collective-permute-start.1) | collective-permute-done | bytes 524320 | tf_op jit(solution)/shard_map/ppermute | solution.py:284
  45.7 0.6 collective-permute-start.7
  46.4 2.4 %collective-permute-done.4.rest_2_ = bf16[4,128,512]{2,1,0:T(8,128)(2,1)S(1)} collective-permute-done((bf16[4,128,512]{2,1,0:T(8,128)(2,1)}, bf16[4,128,512]{2,1,0:T(8,128)(2,1)S(1)}, u32[]{:S(2)}, u32[]{:S(2)}) %collective-permute-start.4) | collective-permute-done | bytes 524320 | tf_op jit(solution)/shard_map/ppermute | solution.py:284
  48.8 11.4 %collective-permute-start.8 = (bf16[4,128,512]{2,1,0:T(8,128)(2,1)}, bf16[4,128,512]{2,1,0:T(8,128)(2,1)S(1)}, u32[]{:S(2)}, u32[]{:S(2)}) collective-permute-start(bf16[4,128,512]{2,1,0:T(8,128)(2,1)} %get-tuple-element.77), channel_id=1, source_target_pairs={{0,88},{8,64},{16,72},{24,80},{32,120},{40,96},{48,104},{56,112},{... | collective-permute-start | bytes 1572872 | tf_op jit(solution)/shard_map/ppermute | solution.py:284
  60.1 3.0 %collective-permute-start.9 = (bf16[4,128,512]{2,1,0:T(8,128)(2,1)}, bf16[4,128,512]{2,1,0:T(8,128)(2,1)S(1)}, u32[]{:S(2)}, u32[]{:S(2)}) collective-permute-start(bf16[4,128,512]{2,1,0:T(8,128)(2,1)} %get-tuple-element.78), channel_id=1, source_target_pairs={{0,8},{8,16},{16,24},{24,0},{32,40},{40,48},{48,56},{56,32},{64,72... | collective-permute-start | bytes 1572872 | tf_op jit(solution)/shard_map/ppermute | solution.py:284
  63.1 14.9 %collective-permute-done.6.rest_4_ = bf16[4,128,512]{2,1,0:T(8,128)(2,1)S(1)} collective-permute-done((bf16[4,128,512]{2,1,0:T(8,128)(2,1)}, bf16[4,128,512]{2,1,0:T(8,128)(2,1)S(1)}, u32[]{:S(2)}, u32[]{:S(2)}) %collective-permute-start.6) | collective-permute-done | bytes 524320 | tf_op jit(solution)/shard_map/ppermute | solution.py:284
  78.1 0.0 collective-permute-start.10
  78.1 0.0 collective-permute-done.12.rest_10_
  78.1 3.6 %collective-permute-start.11 = (bf16[4,128,512]{2,1,0:T(8,128)(2,1)}, bf16[4,128,512]{2,1,0:T(8,128)(2,1)S(1)}, u32[]{:S(2)}, u32[]{:S(2)}) collective-permute-start(bf16[4,128,512]{2,1,0:T(8,128)(2,1)} %get-tuple-element.80), channel_id=1, source_target_pairs={{0,120},{8,96},{16,104},{24,112},{32,24},{40,0},{48,8},{56,16},{64... | collective-permute-start | bytes 1572872 | tf_op jit(solution)/shard_map/ppermute | solution.py:284
  81.7 0.0 collective-permute-done.7.rest_5_
  81.7 0.1 collective-permute-start.20
  81.8 0.1 collective-permute-start.13
  81.9 0.6 copy-done.7
  82.5 4.3 %collective-permute-start.14 = (bf16[4,128,512]{2,1,0:T(8,128)(2,1)}, bf16[4,128,512]{2,1,0:T(8,128)(2,1)}, u32[]{:S(2)}, u32[]{:S(2)}) collective-permute-start(bf16[4,128,512]{2,1,0:T(8,128)(2,1)} %get-tuple-element.84), channel_id=1, source_target_pairs={{0,104},{8,112},{16,120},{24,96},{32,8},{40,16},{48,24},{56,0},{64... | collective-permute-start | bytes 1572872 | tf_op jit(solution)/shard_map/ppermute | solution.py:284
  86.8 6.1 %collective-permute-done.10.rest_8_ = bf16[4,128,512]{2,1,0:T(8,128)(2,1)S(1)} collective-permute-done((bf16[4,128,512]{2,1,0:T(8,128)(2,1)}, bf16[4,128,512]{2,1,0:T(8,128)(2,1)S(1)}, u32[]{:S(2)}, u32[]{:S(2)}) %collective-permute-start.10) | collective-permute-done | bytes 524320 | tf_op jit(solution)/shard_map/ppermute | solution.py:284
  92.8 0.3 collective-permute-start.15
  93.1 0.5 copy-done.10
  93.6 0.8 copy-done.11
  94.4 3.1 %collective-permute-start.16 = (bf16[4,128,512]{2,1,0:T(8,128)(2,1)}, bf16[4,128,512]{2,1,0:T(8,128)(2,1)}, u32[]{:S(2)}, u32[]{:S(2)}) collective-permute-start(bf16[4,128,512]{2,1,0:T(8,128)(2,1)} %get-tuple-element.86), channel_id=1, source_target_pairs={{0,64},{8,72},{16,80},{24,88},{32,96},{40,104},{48,112},{56,120},{... | collective-permute-start | bytes 1572872 | tf_op jit(solution)/shard_map/ppermute | solution.py:284
  97.6 7.2 %project.3.queries_ref = bf16[16,128,256]{2,1,0:T(8,128)(2,1)} custom-call(bf16[2048,2048]{1,0:T(8,128)(2,1)} %refs_0_.2, f32[16,128]{1,0:T(8,128)} %bitcast.20, bf16[3,2048,256]{2,1,0:T(8,128)(2,1)} %bitcast.18), custom_call_target="tpu_custom_call" | custom-call | tf_op jit(solution)/shard_map/project/pallas_call | solution.py:106
  104.8 0.6 pad_add_fusion.first_ref
  105.4 12.4 %collective-permute-done.13.rest_11_ = bf16[4,128,512]{2,1,0:T(8,128)(2,1)} collective-permute-done((bf16[4,128,512]{2,1,0:T(8,128)(2,1)}, bf16[4,128,512]{2,1,0:T(8,128)(2,1)}, u32[]{:S(2)}, u32[]{:S(2)}) %collective-permute-start.13) | collective-permute-done | bytes 524320 | tf_op jit(solution)/shard_map/ppermute | solution.py:284
  117.8 0.2 collective-permute-done.16.rest_14_
  118.0 9.8 %attend.3 = (bf16[512,256]{1,0:T(8,128)(2,1)}, bf16[512,256]{1,0:T(8,128)(2,1)}, bf16[512,256]{1,0:T(8,128)(2,1)}) custom-call(s32[2]{0:T(128)} %pad_add_fusion.first_ref, s32[4,256]{1,0:T(4,128)} %get-tuple-element.49.source_ref, bf16[16,128,256]{2,1,0:T(8,128)(2,1)} %project.3.queries_ref, bf16[16,128,512]{2,1,0:T(8,128)(2,1)} %project.2.held_ref.own_ref, ...), custom_call_target="tpu_custom_call" | custom-call | tf_op jit(solution)/shard_map/attend/pallas_call | solution.py:204
  127.8 2.9 %collective-permute-start.17 = (bf16[512,256]{1,0:T(8,128)(2,1)}, bf16[512,256]{1,0:T(8,128)(2,1)S(1)}, u32[]{:S(2)}, u32[]{:S(2)}) collective-permute-start(bf16[512,256]{1,0:T(8,128)(2,1)} %get-tuple-element.87), channel_id=1, source_target_pairs={{0,2},{1,3},{2,4},{3,5},{4,6},{5,7},{6,0},{7,1},{8,10},{9,11},{10,... | collective-permute-start | bytes 786440 | tf_op jit(solution)/shard_map/ppermute | solution.py:260
  130.7 2.7 %collective-permute-start.18 = (bf16[512,256]{1,0:T(8,128)(2,1)}, bf16[512,256]{1,0:T(8,128)(2,1)}, u32[]{:S(2)}, u32[]{:S(2)}) collective-permute-start(bf16[512,256]{1,0:T(8,128)(2,1)} %get-tuple-element.88), channel_id=1, source_target_pairs={{0,4},{1,5},{2,6},{3,7},{4,0},{5,1},{6,2},{7,3},{8,12},{9,13},{10,... | collective-permute-start | bytes 786440 | tf_op jit(solution)/shard_map/ppermute | solution.py:260
  133.4 1.2 collective-permute-start.19
  134.6 7.4 %attend.2 = bf16[512,256]{1,0:T(8,128)(2,1)} custom-call(s32[2]{0:T(128)} %pad_add_fusion.first_ref, s32[4,256]{1,0:T(4,128)} %get-tuple-element.49.source_ref, bf16[16,128,256]{2,1,0:T(8,128)(2,1)} %project.3.queries_ref, bf16[16,128,512]{2,1,0:T(8,128)(2,1)} %project.2.held_ref.own_ref, bf16[4,128,512]{2,1,0:T(8,128)(2,1)} %copy-done.2, ...), custom_call_target="tpu_custom_call" | custom-call | tf_op jit(solution)/shard_map/attend/pallas_call | solution.py:204
  142.0 2.7 %collective-permute-done.18 = bf16[512,256]{1,0:T(8,128)(2,1)} collective-permute-done((bf16[512,256]{1,0:T(8,128)(2,1)}, bf16[512,256]{1,0:T(8,128)(2,1)}, u32[]{:S(2)}, u32[]{:S(2)}) %collective-permute-start.18) | collective-permute-done | bytes 262176 | tf_op jit(solution)/shard_map/ppermute | solution.py:260
  144.7 0.9 copy-done.1
  145.6 2.7 %mix.3 = bf16[256,2048]{1,0:T(8,128)(2,1)S(1)} custom-call(s32[1]{0:T(128)} %bitcast.11.half_ref, bf16[2,256,256]{2,1,0:T(8,128)(2,1)S(1)} %bitcast.12, bf16[2,256,256]{2,1,0:T(8,128)(2,1)S(1)} %bitcast.14, bf16[2,256,256]{2,1,0:T(8,128)(2,1)} %bitcast.9.refs_2_, bf16[2,256,256]{2,1,0:T(8,128)(2,1)} %bitcast.10.refs_3_, bf16[256,2048]{1,0:T(8,128)(2,1)S(1)} %copy-done, ...), custom_call_target="tpu_custom_call" | custom-call | tf_op jit(solution)/shard_map/mix/pallas_call | solution.py:230
  148.3 2.0 %collective-permute-start.21 = (bf16[256,2048]{1,0:T(8,128)(2,1)S(1)}, bf16[256,2048]{1,0:T(8,128)(2,1)S(1)}, u32[]{:S(2)}, u32[]{:S(2)}) collective-permute-start(bf16[256,2048]{1,0:T(8,128)(2,1)S(1)} %mix.3), channel_id=1, source_target_pairs={{0,1},{1,0},{2,3},{3,2},{4,5},{5,4},{6,7},{7,6},{8,9},{9,8},{10,11... | collective-permute-start | bytes 3145736 | tf_op jit(solution)/shard_map/ppermute | solution.py:295
  150.3 2.8 %mix.2 = f32[256,2048]{1,0:T(8,128)S(1)} custom-call(s32[1]{0:T(128)} %bitcast.half_ref, bf16[2,256,256]{2,1,0:T(8,128)(2,1)S(1)} %bitcast.13, bf16[2,256,256]{2,1,0:T(8,128)(2,1)S(1)} %bitcast.15, bf16[2,256,256]{2,1,0:T(8,128)(2,1)} %bitcast.9.refs_2_, bf16[2,256,256]{2,1,0:T(8,128)(2,1)} %bitcast.10.refs_3_, bf16[256,2048]{1,0:T(8,128)(2,1)S(1)} %copy-done, ...), custom_call_target="tpu_custom_call" | custom-call | tf_op jit(solution)/shard_map/mix/pallas_call | solution.py:230
  153.1 1.3 add_convert_fusion
  (31 shorter events, 0.1 us)
Async XLA Ops:
  0.0 27.7 %collective-permute-start.2 = (bf16[256,2048]{1,0:T(8,128)(2,1)}, bf16[256,2048]{1,0:T(8,128)(2,1)S(1)}, u32[]{:S(2)}, u32[]{:S(2)}) collective-permute-start(bf16[256,2048]{1,0:T(8,128)(2,1)} %refs_4_.3), channel_id=1, source_target_pairs={{0,2},{1,3},{2,4},{3,5},{4,6},{5,7},{6,0},{7,1},{8,10},{9,11},{10,... | collective-permute-start | bytes 3145736 | tf_op jit(solution)/shard_map/ppermute | solution.py:260
  1.3 26.5 %collective-permute-start.3 = (bf16[256,2048]{1,0:T(8,128)(2,1)}, bf16[256,2048]{1,0:T(8,128)(2,1)S(1)}, u32[]{:S(2)}, u32[]{:S(2)}) collective-permute-start(bf16[256,2048]{1,0:T(8,128)(2,1)} %refs_4_.3), channel_id=1, source_target_pairs={{0,6},{1,7},{2,0},{3,1},{4,2},{5,3},{6,4},{7,5},{8,14},{9,15},{10,... | collective-permute-start | bytes 3145736 | tf_op jit(solution)/shard_map/ppermute | solution.py:260
  13.6 68.1 %copy-start = (bf16[256,2048]{1,0:T(8,128)(2,1)S(1)}, bf16[256,2048]{1,0:T(8,128)(2,1)}, u32[]{:S(2)}) copy-start(bf16[256,2048]{1,0:T(8,128)(2,1)} %refs_4_.3) | copy-start | bytes 3145732
  16.9 16.4 %collective-permute-start = (bf16[4,128,512]{2,1,0:T(8,128)(2,1)}, bf16[4,128,512]{2,1,0:T(8,128)(2,1)S(1)}, u32[]{:S(2)}, u32[]{:S(2)}) collective-permute-start(bf16[4,128,512]{2,1,0:T(8,128)(2,1)} %get-tuple-element.57), channel_id=1, source_target_pairs={{0,80},{8,88},{16,64},{24,72},{32,112},{40,120},{48,96},{56,104},{... | collective-permute-start | bytes 1572872 | tf_op jit(solution)/shard_map/ppermute | solution.py:284
  21.4 24.3 %collective-permute-start.1 = (bf16[4,128,512]{2,1,0:T(8,128)(2,1)}, bf16[4,128,512]{2,1,0:T(8,128)(2,1)}, u32[]{:S(2)}, u32[]{:S(2)}) collective-permute-start(bf16[4,128,512]{2,1,0:T(8,128)(2,1)} %get-tuple-element.58), channel_id=1, source_target_pairs={{0,48},{8,56},{16,32},{24,40},{32,80},{40,88},{48,64},{56,72},{64,... | collective-permute-start | bytes 1572872 | tf_op jit(solution)/shard_map/ppermute | solution.py:284
  27.8 21.0 %collective-permute-start.4 = (bf16[4,128,512]{2,1,0:T(8,128)(2,1)}, bf16[4,128,512]{2,1,0:T(8,128)(2,1)S(1)}, u32[]{:S(2)}, u32[]{:S(2)}) collective-permute-start(bf16[4,128,512]{2,1,0:T(8,128)(2,1)} %get-tuple-element.73), channel_id=1, source_target_pairs={{0,96},{8,104},{16,112},{24,120},{32,0},{40,8},{48,16},{56,24},{64... | collective-permute-start | bytes 1572872 | tf_op jit(solution)/shard_map/ppermute | solution.py:284
  29.8 30.4 %collective-permute-start.5 = (bf16[4,128,512]{2,1,0:T(8,128)(2,1)}, bf16[4,128,512]{2,1,0:T(8,128)(2,1)S(1)}, u32[]{:S(2)}, u32[]{:S(2)}) collective-permute-start(bf16[4,128,512]{2,1,0:T(8,128)(2,1)} %get-tuple-element.74), channel_id=1, source_target_pairs={{0,112},{8,120},{16,96},{24,104},{32,16},{40,24},{48,0},{56,8},{64... | collective-permute-start | bytes 1572872 | tf_op jit(solution)/shard_map/ppermute | solution.py:284
  30.7 47.4 %collective-permute-start.6 = (bf16[4,128,512]{2,1,0:T(8,128)(2,1)}, bf16[4,128,512]{2,1,0:T(8,128)(2,1)S(1)}, u32[]{:S(2)}, u32[]{:S(2)}) collective-permute-start(bf16[4,128,512]{2,1,0:T(8,128)(2,1)} %get-tuple-element.75), channel_id=1, source_target_pairs={{0,32},{8,40},{16,48},{24,56},{32,64},{40,72},{48,80},{56,88},{64,... | collective-permute-start | bytes 1572872 | tf_op jit(solution)/shard_map/ppermute | solution.py:284
  33.3 48.3 %copy-start.2 = (bf16[4,128,512]{2,1,0:T(8,128)(2,1)}, bf16[4,128,512]{2,1,0:T(8,128)(2,1)S(1)}, u32[]{:S(2)}) copy-start(bf16[4,128,512]{2,1,0:T(8,128)(2,1)S(1)} %collective-permute-done.rest_0_) | copy-start | bytes 1572868
  33.3 44.7 %collective-permute-start.12 = (bf16[4,128,512]{2,1,0:T(8,128)(2,1)}, bf16[4,128,512]{2,1,0:T(8,128)(2,1)S(1)}, u32[]{:S(2)}, u32[]{:S(2)}) collective-permute-start(bf16[4,128,512]{2,1,0:T(8,128)(2,1)} %get-tuple-element.81), channel_id=1, source_target_pairs={{0,72},{8,80},{16,88},{24,64},{32,104},{40,112},{48,120},{56,96},{... | collective-permute-start | bytes 1572872 | tf_op jit(solution)/shard_map/ppermute | solution.py:284
  45.7 35.9 %collective-permute-start.7 = (bf16[4,128,512]{2,1,0:T(8,128)(2,1)}, bf16[4,128,512]{2,1,0:T(8,128)(2,1)S(1)}, u32[]{:S(2)}, u32[]{:S(2)}) collective-permute-start(bf16[4,128,512]{2,1,0:T(8,128)(2,1)} %get-tuple-element.76), channel_id=1, source_target_pairs={{0,24},{8,0},{16,8},{24,16},{32,56},{40,32},{48,40},{56,48},{64,88... | collective-permute-start | bytes 1572872 | tf_op jit(solution)/shard_map/ppermute | solution.py:284
  48.8 32.9 %copy-start.3 = (bf16[4,128,512]{2,1,0:T(8,128)(2,1)}, bf16[4,128,512]{2,1,0:T(8,128)(2,1)S(1)}, u32[]{:S(2)}) copy-start(bf16[4,128,512]{2,1,0:T(8,128)(2,1)S(1)} %collective-permute-done.4.rest_2_) | copy-start | bytes 1572868
  48.8 33.0 %collective-permute-start.8 = (bf16[4,128,512]{2,1,0:T(8,128)(2,1)}, bf16[4,128,512]{2,1,0:T(8,128)(2,1)S(1)}, u32[]{:S(2)}, u32[]{:S(2)}) collective-permute-start(bf16[4,128,512]{2,1,0:T(8,128)(2,1)} %get-tuple-element.77), channel_id=1, source_target_pairs={{0,88},{8,64},{16,72},{24,80},{32,120},{40,96},{48,104},{56,112},{... | collective-permute-start | bytes 1572872 | tf_op jit(solution)/shard_map/ppermute | solution.py:284
  60.1 21.7 %copy-start.4 = (bf16[4,128,512]{2,1,0:T(8,128)(2,1)}, bf16[4,128,512]{2,1,0:T(8,128)(2,1)S(1)}, u32[]{:S(2)}) copy-start(bf16[4,128,512]{2,1,0:T(8,128)(2,1)S(1)} %collective-permute-done.5.rest_3_) | copy-start | bytes 1572868
  60.1 21.8 %collective-permute-start.9 = (bf16[4,128,512]{2,1,0:T(8,128)(2,1)}, bf16[4,128,512]{2,1,0:T(8,128)(2,1)S(1)}, u32[]{:S(2)}, u32[]{:S(2)}) collective-permute-start(bf16[4,128,512]{2,1,0:T(8,128)(2,1)} %get-tuple-element.78), channel_id=1, source_target_pairs={{0,8},{8,16},{16,24},{24,0},{32,40},{40,48},{48,56},{56,32},{64,72... | collective-permute-start | bytes 1572872 | tf_op jit(solution)/shard_map/ppermute | solution.py:284
  78.1 3.7 %copy-start.5 = (bf16[4,128,512]{2,1,0:T(8,128)(2,1)}, bf16[4,128,512]{2,1,0:T(8,128)(2,1)S(1)}, u32[]{:S(2)}) copy-start(bf16[4,128,512]{2,1,0:T(8,128)(2,1)S(1)} %collective-permute-done.6.rest_4_) | copy-start | bytes 1572868
  78.1 14.8 %collective-permute-start.10 = (bf16[4,128,512]{2,1,0:T(8,128)(2,1)}, bf16[4,128,512]{2,1,0:T(8,128)(2,1)S(1)}, u32[]{:S(2)}, u32[]{:S(2)}) collective-permute-start(bf16[4,128,512]{2,1,0:T(8,128)(2,1)} %get-tuple-element.79), channel_id=1, source_target_pairs={{0,40},{8,48},{16,56},{24,32},{32,72},{40,80},{48,88},{56,64},{64,... | collective-permute-start | bytes 1572872 | tf_op jit(solution)/shard_map/ppermute | solution.py:284
  78.1 3.8 %copy-start.6 = (bf16[4,128,512]{2,1,0:T(8,128)(2,1)}, bf16[4,128,512]{2,1,0:T(8,128)(2,1)S(1)}, u32[]{:S(2)}) copy-start(bf16[4,128,512]{2,1,0:T(8,128)(2,1)S(1)} %collective-permute-done.12.rest_10_) | copy-start | bytes 1572868
  78.1 15.5 %collective-permute-start.11 = (bf16[4,128,512]{2,1,0:T(8,128)(2,1)}, bf16[4,128,512]{2,1,0:T(8,128)(2,1)S(1)}, u32[]{:S(2)}, u32[]{:S(2)}) collective-permute-start(bf16[4,128,512]{2,1,0:T(8,128)(2,1)} %get-tuple-element.80), channel_id=1, source_target_pairs={{0,120},{8,96},{16,104},{24,112},{32,24},{40,0},{48,8},{56,16},{64... | collective-permute-start | bytes 1572872 | tf_op jit(solution)/shard_map/ppermute | solution.py:284
  81.7 0.8 copy-start.7
  81.7 63.0 %collective-permute-start.20 = (bf16[256,2048]{1,0:T(8,128)(2,1)S(1)}, bf16[256,2048]{1,0:T(8,128)(2,1)}, u32[]{:S(2)}, u32[]{:S(2)}) collective-permute-start(bf16[256,2048]{1,0:T(8,128)(2,1)S(1)} %copy-done), channel_id=1, source_target_pairs={{0,4},{1,5},{2,6},{3,7},{4,0},{5,1},{6,2},{7,3},{8,12},{9,13},{10,... | collective-permute-start | bytes 3145736 | tf_op jit(solution)/shard_map/ppermute | solution.py:260
  81.8 5.0 %copy-start.8 = (bf16[4,128,512]{2,1,0:T(8,128)(2,1)}, bf16[4,128,512]{2,1,0:T(8,128)(2,1)S(1)}, u32[]{:S(2)}) copy-start(bf16[4,128,512]{2,1,0:T(8,128)(2,1)S(1)} %collective-permute-done.8.rest_6_) | copy-start | bytes 1572868
  81.8 36.0 %collective-permute-start.13 = (bf16[4,128,512]{2,1,0:T(8,128)(2,1)}, bf16[4,128,512]{2,1,0:T(8,128)(2,1)}, u32[]{:S(2)}, u32[]{:S(2)}) collective-permute-start(bf16[4,128,512]{2,1,0:T(8,128)(2,1)} %get-tuple-element.83), channel_id=1, source_target_pairs={{0,56},{8,32},{16,40},{24,48},{32,88},{40,64},{48,72},{56,80},{64,... | collective-permute-start | bytes 1572872 | tf_op jit(solution)/shard_map/ppermute | solution.py:284
  82.5 10.4 %copy-start.9 = (bf16[4,128,512]{2,1,0:T(8,128)(2,1)}, bf16[4,128,512]{2,1,0:T(8,128)(2,1)S(1)}, u32[]{:S(2)}) copy-start(bf16[4,128,512]{2,1,0:T(8,128)(2,1)S(1)} %collective-permute-done.9.rest_7_) | copy-start | bytes 1572868
  82.5 35.3 %collective-permute-start.14 = (bf16[4,128,512]{2,1,0:T(8,128)(2,1)}, bf16[4,128,512]{2,1,0:T(8,128)(2,1)}, u32[]{:S(2)}, u32[]{:S(2)}) collective-permute-start(bf16[4,128,512]{2,1,0:T(8,128)(2,1)} %get-tuple-element.84), channel_id=1, source_target_pairs={{0,104},{8,112},{16,120},{24,96},{32,8},{40,16},{48,24},{56,0},{64... | collective-permute-start | bytes 1572872 | tf_op jit(solution)/shard_map/ppermute | solution.py:284
  92.8 0.8 copy-start.10
  92.8 25.0 %collective-permute-start.15 = (bf16[4,128,512]{2,1,0:T(8,128)(2,1)}, bf16[4,128,512]{2,1,0:T(8,128)(2,1)}, u32[]{:S(2)}, u32[]{:S(2)}) collective-permute-start(bf16[4,128,512]{2,1,0:T(8,128)(2,1)} %get-tuple-element.85), channel_id=1, source_target_pairs={{0,16},{8,24},{16,0},{24,8},{32,48},{40,56},{48,32},{56,40},{64,80... | collective-permute-start | bytes 1572872 | tf_op jit(solution)/shard_map/ppermute | solution.py:284
  93.6 0.8 copy-start.11
  94.4 23.5 %collective-permute-start.16 = (bf16[4,128,512]{2,1,0:T(8,128)(2,1)}, bf16[4,128,512]{2,1,0:T(8,128)(2,1)}, u32[]{:S(2)}, u32[]{:S(2)}) collective-permute-start(bf16[4,128,512]{2,1,0:T(8,128)(2,1)} %get-tuple-element.86), channel_id=1, source_target_pairs={{0,64},{8,72},{16,80},{24,88},{32,96},{40,104},{48,112},{56,120},{... | collective-permute-start | bytes 1572872 | tf_op jit(solution)/shard_map/ppermute | solution.py:284
  127.8 14.2 %collective-permute-start.17 = (bf16[512,256]{1,0:T(8,128)(2,1)}, bf16[512,256]{1,0:T(8,128)(2,1)S(1)}, u32[]{:S(2)}, u32[]{:S(2)}) collective-permute-start(bf16[512,256]{1,0:T(8,128)(2,1)} %get-tuple-element.87), channel_id=1, source_target_pairs={{0,2},{1,3},{2,4},{3,5},{4,6},{5,7},{6,0},{7,1},{8,10},{9,11},{10,... | collective-permute-start | bytes 786440 | tf_op jit(solution)/shard_map/ppermute | solution.py:260
  130.7 14.0 %collective-permute-start.18 = (bf16[512,256]{1,0:T(8,128)(2,1)}, bf16[512,256]{1,0:T(8,128)(2,1)}, u32[]{:S(2)}, u32[]{:S(2)}) collective-permute-start(bf16[512,256]{1,0:T(8,128)(2,1)} %get-tuple-element.88), channel_id=1, source_target_pairs={{0,4},{1,5},{2,6},{3,7},{4,0},{5,1},{6,2},{7,3},{8,12},{9,13},{10,... | collective-permute-start | bytes 786440 | tf_op jit(solution)/shard_map/ppermute | solution.py:260
  133.4 11.3 %collective-permute-start.19 = (bf16[512,256]{1,0:T(8,128)(2,1)}, bf16[512,256]{1,0:T(8,128)(2,1)}, u32[]{:S(2)}, u32[]{:S(2)}) collective-permute-start(bf16[512,256]{1,0:T(8,128)(2,1)} %get-tuple-element.89), channel_id=1, source_target_pairs={{0,6},{1,7},{2,0},{3,1},{4,2},{5,3},{6,4},{7,5},{8,14},{9,15},{10,... | collective-permute-start | bytes 786440 | tf_op jit(solution)/shard_map/ppermute | solution.py:260
  144.7 1.0 copy-start.1
  148.3 4.7 %collective-permute-start.21 = (bf16[256,2048]{1,0:T(8,128)(2,1)S(1)}, bf16[256,2048]{1,0:T(8,128)(2,1)S(1)}, u32[]{:S(2)}, u32[]{:S(2)}) collective-permute-start(bf16[256,2048]{1,0:T(8,128)(2,1)S(1)} %mix.3), channel_id=1, source_target_pairs={{0,1},{1,0},{2,3},{3,2},{4,5},{5,4},{6,7},{7,6},{8,9},{9,8},{10,11... | collective-permute-start | bytes 3145736 | tf_op jit(solution)/shard_map/ppermute | solution.py:295

commit v7 on v6

--- a/solution.py
+++ b/solution.py
@@ -16,7 +16,7 @@
 GROUP = 2
 SIDE = 4
 SHIFTS = (10, 6, 12, 14, 4, 3, 11, 1, 5, 15, 9, 7, 13, 2, 8)
-FIRST = 5
+FIRST = 2
 STEPS = ((1, 2, 3), (0,))
 ALONE = 2
 LATE = 10

time: 155 us -> 155 us (level)
  starting transfers between devices: 52.6 us -> 62.6 us
  waiting for transfers between devices: 48.8 us -> 39.9 us
    ppermute x15, starting transfers between devices: 41 us -> 54.3 us  [body(): lax.ppermute(send, 'seq', [(s, shifted(s, shift)) for s in range(shards)])]
    ppermute x15, waiting for transfers between devices: 46.2 us -> 36.1 us  [body(): lax.ppermute(send, 'seq', [(s, shifted(s, shift)) for s in range(shards)])]
    ppermute x6, starting transfers between devices: 9.66 us -> 6.63 us  [along(): lax.ppermute(x, 'head', [(s, (s // 2 + shift) % pairs * 2 + s % 2) for s...]
  transfers between devices with their start and end apart: 22 -> 22, of which waited for: 8 -> 11; matrix products, arithmetic and copies ran while one was open for 0% -> 0% of each run, Pallas kernels for 29% -> 29%
where the time goes in v7:
time: 155 us; the launch traced here: 154 us
  starting transfers between devices  62.6 us (40%)
  Pallas kernels  47.9 us (31%)
  waiting for transfers between devices  39.9 us (26%)
  other arithmetic  1.87 us (1%)
  local copies, waits for them, and re-layouts  1.81 us (1%)
    ppermute x15, starting transfers between devices, body(): lax.ppermute(send, 'seq', [(s, shifted(s, shift)) for s in range(shards)])  54.3 us
    ppermute x15, waiting for transfers between devices, body(): lax.ppermute(send, 'seq', [(s, shifted(s, shift)) for s in range(shards)])  36.1 us
    pallas_call x2, Pallas kernels, attend(): pl.pallas_call(functools.partial(attend_kernel, tiles=tiles, heads=querie...  17.1 us
    pallas_call x2, Pallas kernels, project(): pl.pallas_call(functools.partial(project_kernel, widths=widths, scales=le...  16.4 us
    pallas_call x2, Pallas kernels, dispatch(): pl.pallas_call(functools.partial(dispatch_kernel, shifts=shifts), in_spec...  7.27 us
    ppermute x6, starting transfers between devices, along(): lax.ppermute(x, 'head', [(s, (s // 2 + shift) % pairs * 2 + s % 2) for s...  6.63 us
    pallas_call x2, Pallas kernels, mix(): pl.pallas_call(mix_kernel, grid_spec=pltpu.PrefetchScalarGridSpec(num_sca...  5.45 us
    ppermute x6, waiting for transfers between devices, along(): lax.ppermute(x, 'head', [(s, (s // 2 + shift) % pairs * 2 + s % 2) for s...  3.81 us
  transfers between devices with their start and end apart: 22, of which 11 were waited for; matrix products, arithmetic and copies ran while one was open for 0% of the time, Pallas kernels for 29%

profile of v7, /device:TPU:7, one launch (start us, length us, event | category | flops | bytes accessed | tf_op | source)
XLA Modules:
  0.0 154.3 jit_solution(10746671510015786708)
XLA Ops:
  0.0 1.3 collective-permute-start.2
  1.3 1.4 collective-permute-start.3
  2.7 1.7 %tables.1 = (s32[8,128]{1,0:T(8,128)}, s32[4,256]{1,0:T(4,128)}) custom-call(s32[1]{0:T(128)} %bitcast.3.me_ref, s32[4,256]{1,0:T(4,128)} %bitcast.21), custom_call_target="tpu_custom_call" | custom-call | tf_op jit(solution)/shard_map/tables/pallas_call | solution.py:262
  4.4 9.2 %project.2.held_ref.own_ref = bf16[16,128,512]{2,1,0:T(8,128)(2,1)} custom-call(bf16[2048,2048]{1,0:T(8,128)(2,1)} %refs_0_.2, f32[16,128]{1,0:T(8,128)} %bitcast.19, bf16[3,2048,256]{2,1,0:T(8,128)(2,1)} %bitcast.16, bf16[3,2048,256]{2,1,0:T(8,128)(2,1)} %bitcast.17), custom_call_target="tpu_custom_call" | custom-call | tf_op jit(solution)/shard_map/project/pallas_call | solution.py:106
  13.6 2.7 %dispatch.2 = (bf16[4,128,512]{2,1,0:T(8,128)(2,1)}, bf16[4,128,512]{2,1,0:T(8,128)(2,1)}) custom-call(s32[1]{0:T(128)} %bitcast.3.me_ref, s32[8,128]{1,0:T(8,128)} %get-tuple-element.47.chosen_ref, bf16[16,128,512]{2,1,0:T(8,128)(2,1)} %project.2.held_ref.own_ref), custom_call_target="tpu_custom_call" | custom-call | tf_op jit(solution)/shard_map/dispatch/pallas_call | solution.py:141
  16.4 4.5 %collective-permute-start = (bf16[4,128,512]{2,1,0:T(8,128)(2,1)}, bf16[4,128,512]{2,1,0:T(8,128)(2,1)S(1)}, u32[]{:S(2)}, u32[]{:S(2)}) collective-permute-start(bf16[4,128,512]{2,1,0:T(8,128)(2,1)} %get-tuple-element.51), channel_id=1, source_target_pairs={{0,80},{8,88},{16,64},{24,72},{32,112},{40,120},{48,96},{56,104},{... | collective-permute-start | bytes 1572872 | tf_op jit(solution)/shard_map/ppermute | solution.py:284
  20.9 2.3 %collective-permute-start.1 = (bf16[4,128,512]{2,1,0:T(8,128)(2,1)}, bf16[4,128,512]{2,1,0:T(8,128)(2,1)}, u32[]{:S(2)}, u32[]{:S(2)}) collective-permute-start(bf16[4,128,512]{2,1,0:T(8,128)(2,1)} %get-tuple-element.52), channel_id=1, source_target_pairs={{0,48},{8,56},{16,32},{24,40},{32,80},{40,88},{48,64},{56,72},{64,... | collective-permute-start | bytes 1572872 | tf_op jit(solution)/shard_map/ppermute | solution.py:284
  23.2 4.5 %dispatch.3 = (bf16[4,128,512]{2,1,0:T(8,128)(2,1)}, bf16[4,128,512]{2,1,0:T(8,128)(2,1)}, bf16[4,128,512]{2,1,0:T(8,128)(2,1)}, bf16[4,128,512]{2,1,0:T(8,128)(...) custom-call(s32[1]{0:T(128)} %bitcast.3.me_ref, ...), custom_call_target="tpu_custom_call" | custom-call | tf_op jit(solution)/shard_map/dispatch/pallas_call | solution.py:141
  27.7 0.0 collective-permute-done.3.refs_7_
  27.7 2.0 %collective-permute-start.4 = (bf16[4,128,512]{2,1,0:T(8,128)(2,1)}, bf16[4,128,512]{2,1,0:T(8,128)(2,1)S(1)}, u32[]{:S(2)}, u32[]{:S(2)}) collective-permute-start(bf16[4,128,512]{2,1,0:T(8,128)(2,1)} %get-tuple-element.67), channel_id=1, source_target_pairs={{0,96},{8,104},{16,112},{24,120},{32,0},{40,8},{48,16},{56,24},{64... | collective-permute-start | bytes 1572872 | tf_op jit(solution)/shard_map/ppermute | solution.py:284
  29.7 0.9 collective-permute-start.5
  30.7 1.4 collective-permute-start.6
  32.1 0.7 collective-permute-done.rest_0_
  32.8 3.5 %collective-permute-start.12 = (bf16[4,128,512]{2,1,0:T(8,128)(2,1)}, bf16[4,128,512]{2,1,0:T(8,128)(2,1)S(1)}, u32[]{:S(2)}, u32[]{:S(2)}) collective-permute-start(bf16[4,128,512]{2,1,0:T(8,128)(2,1)} %get-tuple-element.75), channel_id=1, source_target_pairs={{0,72},{8,80},{16,88},{24,64},{32,104},{40,112},{48,120},{56,96},{... | collective-permute-start | bytes 1572872 | tf_op jit(solution)/shard_map/ppermute | solution.py:284
  36.3 8.9 %collective-permute-done.1.rest_1_ = bf16[4,128,512]{2,1,0:T(8,128)(2,1)} collective-permute-done((bf16[4,128,512]{2,1,0:T(8,128)(2,1)}, bf16[4,128,512]{2,1,0:T(8,128)(2,1)}, u32[]{:S(2)}, u32[]{:S(2)}) %collective-permute-start.1) | collective-permute-done | bytes 524320 | tf_op jit(solution)/shard_map/ppermute | solution.py:284
  45.2 0.6 collective-permute-start.7
  45.8 2.4 %collective-permute-done.4.rest_2_ = bf16[4,128,512]{2,1,0:T(8,128)(2,1)S(1)} collective-permute-done((bf16[4,128,512]{2,1,0:T(8,128)(2,1)}, bf16[4,128,512]{2,1,0:T(8,128)(2,1)S(1)}, u32[]{:S(2)}, u32[]{:S(2)}) %collective-permute-start.4) | collective-permute-done | bytes 524320 | tf_op jit(solution)/shard_map/ppermute | solution.py:284
  48.2 11.4 %collective-permute-start.8 = (bf16[4,128,512]{2,1,0:T(8,128)(2,1)}, bf16[4,128,512]{2,1,0:T(8,128)(2,1)S(1)}, u32[]{:S(2)}, u32[]{:S(2)}) collective-permute-start(bf16[4,128,512]{2,1,0:T(8,128)(2,1)} %get-tuple-element.71), channel_id=1, source_target_pairs={{0,88},{8,64},{16,72},{24,80},{32,120},{40,96},{48,104},{56,112},{... | collective-permute-start | bytes 1572872 | tf_op jit(solution)/shard_map/ppermute | solution.py:284
  59.6 0.0 collective-permute-done.5.rest_3_
  59.6 3.1 %collective-permute-start.9 = (bf16[4,128,512]{2,1,0:T(8,128)(2,1)}, bf16[4,128,512]{2,1,0:T(8,128)(2,1)S(1)}, u32[]{:S(2)}, u32[]{:S(2)}) collective-permute-start(bf16[4,128,512]{2,1,0:T(8,128)(2,1)} %get-tuple-element.72), channel_id=1, source_target_pairs={{0,8},{8,16},{16,24},{24,0},{32,40},{40,48},{48,56},{56,32},{64,72... | collective-permute-start | bytes 1572872 | tf_op jit(solution)/shard_map/ppermute | solution.py:284
  62.6 5.8 %collective-permute-done.6.rest_4_ = bf16[4,128,512]{2,1,0:T(8,128)(2,1)S(1)} collective-permute-done((bf16[4,128,512]{2,1,0:T(8,128)(2,1)}, bf16[4,128,512]{2,1,0:T(8,128)(2,1)S(1)}, u32[]{:S(2)}, u32[]{:S(2)}) %collective-permute-start.6) | collective-permute-done | bytes 524320 | tf_op jit(solution)/shard_map/ppermute | solution.py:284
  68.4 0.0 collective-permute-start.10
  68.5 9.4 %collective-permute-start.11 = (bf16[4,128,512]{2,1,0:T(8,128)(2,1)}, bf16[4,128,512]{2,1,0:T(8,128)(2,1)S(1)}, u32[]{:S(2)}, u32[]{:S(2)}) collective-permute-start(bf16[4,128,512]{2,1,0:T(8,128)(2,1)} %get-tuple-element.74), channel_id=1, source_target_pairs={{0,120},{8,96},{16,104},{24,112},{32,24},{40,0},{48,8},{56,16},{64... | collective-permute-start | bytes 1572872 | tf_op jit(solution)/shard_map/ppermute | solution.py:284
  77.9 0.1 collective-permute-start.20
  78.0 2.3 %collective-permute-done.8.rest_6_ = bf16[4,128,512]{2,1,0:T(8,128)(2,1)S(1)} collective-permute-done((bf16[4,128,512]{2,1,0:T(8,128)(2,1)}, bf16[4,128,512]{2,1,0:T(8,128)(2,1)S(1)}, u32[]{:S(2)}, u32[]{:S(2)}) %collective-permute-start.8) | collective-permute-done | bytes 524320 | tf_op jit(solution)/shard_map/ppermute | solution.py:284
  80.3 0.4 collective-permute-start.13
  80.7 4.4 %collective-permute-start.14 = (bf16[4,128,512]{2,1,0:T(8,128)(2,1)}, bf16[4,128,512]{2,1,0:T(8,128)(2,1)}, u32[]{:S(2)}, u32[]{:S(2)}) collective-permute-start(bf16[4,128,512]{2,1,0:T(8,128)(2,1)} %get-tuple-element.78), channel_id=1, source_target_pairs={{0,104},{8,112},{16,120},{24,96},{32,8},{40,16},{48,24},{56,0},{64... | collective-permute-start | bytes 1572872 | tf_op jit(solution)/shard_map/ppermute | solution.py:284
  85.2 3.1 %collective-permute-done.10.rest_8_ = bf16[4,128,512]{2,1,0:T(8,128)(2,1)S(1)} collective-permute-done((bf16[4,128,512]{2,1,0:T(8,128)(2,1)}, bf16[4,128,512]{2,1,0:T(8,128)(2,1)S(1)}, u32[]{:S(2)}, u32[]{:S(2)}) %collective-permute-start.10) | collective-permute-done | bytes 524320 | tf_op jit(solution)/shard_map/ppermute | solution.py:284
  88.3 6.3 %collective-permute-start.15 = (bf16[4,128,512]{2,1,0:T(8,128)(2,1)}, bf16[4,128,512]{2,1,0:T(8,128)(2,1)}, u32[]{:S(2)}, u32[]{:S(2)}) collective-permute-start(bf16[4,128,512]{2,1,0:T(8,128)(2,1)} %get-tuple-element.79), channel_id=1, source_target_pairs={{0,16},{8,24},{16,0},{24,8},{32,48},{40,56},{48,32},{56,40},{64,80... | collective-permute-start | bytes 1572872 | tf_op jit(solution)/shard_map/ppermute | solution.py:284
  94.7 0.8 copy-done.11
  95.5 4.0 %collective-permute-start.16 = (bf16[4,128,512]{2,1,0:T(8,128)(2,1)}, bf16[4,128,512]{2,1,0:T(8,128)(2,1)}, u32[]{:S(2)}, u32[]{:S(2)}) collective-permute-start(bf16[4,128,512]{2,1,0:T(8,128)(2,1)} %get-tuple-element.80), channel_id=1, source_target_pairs={{0,64},{8,72},{16,80},{24,88},{32,96},{40,104},{48,112},{56,120},{... | collective-permute-start | bytes 1572872 | tf_op jit(solution)/shard_map/ppermute | solution.py:284
  99.5 7.2 %project.3.queries_ref = bf16[16,128,256]{2,1,0:T(8,128)(2,1)} custom-call(bf16[2048,2048]{1,0:T(8,128)(2,1)} %refs_0_.2, f32[16,128]{1,0:T(8,128)} %bitcast.20, bf16[3,2048,256]{2,1,0:T(8,128)(2,1)} %bitcast.18), custom_call_target="tpu_custom_call" | custom-call | tf_op jit(solution)/shard_map/project/pallas_call | solution.py:106
  106.7 0.6 pad_add_fusion.first_ref
  107.3 2.9 %collective-permute-done.13.rest_11_ = bf16[4,128,512]{2,1,0:T(8,128)(2,1)} collective-permute-done((bf16[4,128,512]{2,1,0:T(8,128)(2,1)}, bf16[4,128,512]{2,1,0:T(8,128)(2,1)}, u32[]{:S(2)}, u32[]{:S(2)}) %collective-permute-start.13) | collective-permute-done | bytes 524320 | tf_op jit(solution)/shard_map/ppermute | solution.py:284
  110.2 3.4 %collective-permute-done.15.rest_13_ = bf16[4,128,512]{2,1,0:T(8,128)(2,1)} collective-permute-done((bf16[4,128,512]{2,1,0:T(8,128)(2,1)}, bf16[4,128,512]{2,1,0:T(8,128)(2,1)}, u32[]{:S(2)}, u32[]{:S(2)}) %collective-permute-start.15) | collective-permute-done | bytes 524320 | tf_op jit(solution)/shard_map/ppermute | solution.py:284
  113.6 6.6 %collective-permute-done.16.rest_14_ = bf16[4,128,512]{2,1,0:T(8,128)(2,1)} collective-permute-done((bf16[4,128,512]{2,1,0:T(8,128)(2,1)}, bf16[4,128,512]{2,1,0:T(8,128)(2,1)}, u32[]{:S(2)}, u32[]{:S(2)}) %collective-permute-start.16) | collective-permute-done | bytes 524320 | tf_op jit(solution)/shard_map/ppermute | solution.py:284
  120.2 9.8 %attend.3 = (bf16[512,256]{1,0:T(8,128)(2,1)}, bf16[512,256]{1,0:T(8,128)(2,1)}, bf16[512,256]{1,0:T(8,128)(2,1)}) custom-call(s32[2]{0:T(128)} %pad_add_fusion.first_ref, s32[4,256]{1,0:T(4,128)} %get-tuple-element.46.source_ref, bf16[16,128,256]{2,1,0:T(8,128)(2,1)} %project.3.queries_ref, bf16[16,128,512]{2,1,0:T(8,128)(2,1)} %project.2.held_ref.own_ref, ...), custom_call_target="tpu_custom_call" | custom-call | tf_op jit(solution)/shard_map/attend/pallas_call | solution.py:204
  130.0 0.1 collective-permute-start.17
  130.1 2.2 %collective-permute-start.18 = (bf16[512,256]{1,0:T(8,128)(2,1)}, bf16[512,256]{1,0:T(8,128)(2,1)}, u32[]{:S(2)}, u32[]{:S(2)}) collective-permute-start(bf16[512,256]{1,0:T(8,128)(2,1)} %get-tuple-element.82), channel_id=1, source_target_pairs={{0,4},{1,5},{2,6},{3,7},{4,0},{5,1},{6,2},{7,3},{8,12},{9,13},{10,... | collective-permute-start | bytes 786440 | tf_op jit(solution)/shard_map/ppermute | solution.py:260
  132.3 1.5 collective-permute-start.19
  133.8 7.4 %attend.2 = bf16[512,256]{1,0:T(8,128)(2,1)} custom-call(s32[2]{0:T(128)} %pad_add_fusion.first_ref, s32[4,256]{1,0:T(4,128)} %get-tuple-element.46.source_ref, bf16[16,128,256]{2,1,0:T(8,128)(2,1)} %project.3.queries_ref, bf16[16,128,512]{2,1,0:T(8,128)(2,1)} %project.2.held_ref.own_ref, bf16[4,128,512]{2,1,0:T(8,128)(2,1)} %copy-done.2, ...), custom_call_target="tpu_custom_call" | custom-call | tf_op jit(solution)/shard_map/attend/pallas_call | solution.py:204
  141.2 2.7 %collective-permute-done.18 = bf16[512,256]{1,0:T(8,128)(2,1)} collective-permute-done((bf16[512,256]{1,0:T(8,128)(2,1)}, bf16[512,256]{1,0:T(8,128)(2,1)}, u32[]{:S(2)}, u32[]{:S(2)}) %collective-permute-start.18) | collective-permute-done | bytes 262176 | tf_op jit(solution)/shard_map/ppermute | solution.py:260
  143.9 1.1 collective-permute-done.19
  145.0 0.9 copy-done.1
  146.0 2.7 %mix.3 = bf16[256,2048]{1,0:T(8,128)(2,1)S(1)} custom-call(s32[1]{0:T(128)} %bitcast.11.half_ref, bf16[2,256,256]{2,1,0:T(8,128)(2,1)S(1)} %bitcast.12, bf16[2,256,256]{2,1,0:T(8,128)(2,1)S(1)} %bitcast.14, bf16[2,256,256]{2,1,0:T(8,128)(2,1)} %bitcast.9.refs_2_, bf16[2,256,256]{2,1,0:T(8,128)(2,1)} %bitcast.10.refs_3_, bf16[256,2048]{1,0:T(8,128)(2,1)S(1)} %copy-done, ...), custom_call_target="tpu_custom_call" | custom-call | tf_op jit(solution)/shard_map/mix/pallas_call | solution.py:230
  148.7 1.6 %collective-permute-start.21 = (bf16[256,2048]{1,0:T(8,128)(2,1)S(1)}, bf16[256,2048]{1,0:T(8,128)(2,1)S(1)}, u32[]{:S(2)}, u32[]{:S(2)}) collective-permute-start(bf16[256,2048]{1,0:T(8,128)(2,1)S(1)} %mix.3), channel_id=1, source_target_pairs={{0,1},{1,0},{2,3},{3,2},{4,5},{5,4},{6,7},{7,6},{8,9},{9,8},{10,11... | collective-permute-start | bytes 3145736 | tf_op jit(solution)/shard_map/ppermute | solution.py:295
  150.3 2.8 %mix.2 = f32[256,2048]{1,0:T(8,128)S(1)} custom-call(s32[1]{0:T(128)} %bitcast.half_ref, bf16[2,256,256]{2,1,0:T(8,128)(2,1)S(1)} %bitcast.13, bf16[2,256,256]{2,1,0:T(8,128)(2,1)S(1)} %bitcast.15, bf16[2,256,256]{2,1,0:T(8,128)(2,1)} %bitcast.9.refs_2_, bf16[2,256,256]{2,1,0:T(8,128)(2,1)} %bitcast.10.refs_3_, bf16[256,2048]{1,0:T(8,128)(2,1)S(1)} %copy-done, ...), custom_call_target="tpu_custom_call" | custom-call | tf_op jit(solution)/shard_map/mix/pallas_call | solution.py:230
  153.1 1.3 add_convert_fusion
  (31 shorter events, 0.1 us)
Async XLA Ops:
  0.0 27.7 %collective-permute-start.2 = (bf16[256,2048]{1,0:T(8,128)(2,1)}, bf16[256,2048]{1,0:T(8,128)(2,1)S(1)}, u32[]{:S(2)}, u32[]{:S(2)}) collective-permute-start(bf16[256,2048]{1,0:T(8,128)(2,1)} %refs_4_.3), channel_id=1, source_target_pairs={{0,2},{1,3},{2,4},{3,5},{4,6},{5,7},{6,0},{7,1},{8,10},{9,11},{10,... | collective-permute-start | bytes 3145736 | tf_op jit(solution)/shard_map/ppermute | solution.py:260
  1.3 26.4 %collective-permute-start.3 = (bf16[256,2048]{1,0:T(8,128)(2,1)}, bf16[256,2048]{1,0:T(8,128)(2,1)S(1)}, u32[]{:S(2)}, u32[]{:S(2)}) collective-permute-start(bf16[256,2048]{1,0:T(8,128)(2,1)} %refs_4_.3), channel_id=1, source_target_pairs={{0,6},{1,7},{2,0},{3,1},{4,2},{5,3},{6,4},{7,5},{8,14},{9,15},{10,... | collective-permute-start | bytes 3145736 | tf_op jit(solution)/shard_map/ppermute | solution.py:260
  13.6 64.3 %copy-start = (bf16[256,2048]{1,0:T(8,128)(2,1)S(1)}, bf16[256,2048]{1,0:T(8,128)(2,1)}, u32[]{:S(2)}) copy-start(bf16[256,2048]{1,0:T(8,128)(2,1)} %refs_4_.3) | copy-start | bytes 3145732
  16.4 16.4 %collective-permute-start = (bf16[4,128,512]{2,1,0:T(8,128)(2,1)}, bf16[4,128,512]{2,1,0:T(8,128)(2,1)S(1)}, u32[]{:S(2)}, u32[]{:S(2)}) collective-permute-start(bf16[4,128,512]{2,1,0:T(8,128)(2,1)} %get-tuple-element.51), channel_id=1, source_target_pairs={{0,80},{8,88},{16,64},{24,72},{32,112},{40,120},{48,96},{56,104},{... | collective-permute-start | bytes 1572872 | tf_op jit(solution)/shard_map/ppermute | solution.py:284
  20.9 24.3 %collective-permute-start.1 = (bf16[4,128,512]{2,1,0:T(8,128)(2,1)}, bf16[4,128,512]{2,1,0:T(8,128)(2,1)}, u32[]{:S(2)}, u32[]{:S(2)}) collective-permute-start(bf16[4,128,512]{2,1,0:T(8,128)(2,1)} %get-tuple-element.52), channel_id=1, source_target_pairs={{0,48},{8,56},{16,32},{24,40},{32,80},{40,88},{48,64},{56,72},{64,... | collective-permute-start | bytes 1572872 | tf_op jit(solution)/shard_map/ppermute | solution.py:284
  27.7 20.5 %collective-permute-start.4 = (bf16[4,128,512]{2,1,0:T(8,128)(2,1)}, bf16[4,128,512]{2,1,0:T(8,128)(2,1)S(1)}, u32[]{:S(2)}, u32[]{:S(2)}) collective-permute-start(bf16[4,128,512]{2,1,0:T(8,128)(2,1)} %get-tuple-element.67), channel_id=1, source_target_pairs={{0,96},{8,104},{16,112},{24,120},{32,0},{40,8},{48,16},{56,24},{64... | collective-permute-start | bytes 1572872 | tf_op jit(solution)/shard_map/ppermute | solution.py:284
  29.7 29.8 %collective-permute-start.5 = (bf16[4,128,512]{2,1,0:T(8,128)(2,1)}, bf16[4,128,512]{2,1,0:T(8,128)(2,1)S(1)}, u32[]{:S(2)}, u32[]{:S(2)}) collective-permute-start(bf16[4,128,512]{2,1,0:T(8,128)(2,1)} %get-tuple-element.68), channel_id=1, source_target_pairs={{0,112},{8,120},{16,96},{24,104},{32,16},{40,24},{48,0},{56,8},{64... | collective-permute-start | bytes 1572872 | tf_op jit(solution)/shard_map/ppermute | solution.py:284
  30.7 37.8 %collective-permute-start.6 = (bf16[4,128,512]{2,1,0:T(8,128)(2,1)}, bf16[4,128,512]{2,1,0:T(8,128)(2,1)S(1)}, u32[]{:S(2)}, u32[]{:S(2)}) collective-permute-start(bf16[4,128,512]{2,1,0:T(8,128)(2,1)} %get-tuple-element.69), channel_id=1, source_target_pairs={{0,32},{8,40},{16,48},{24,56},{32,64},{40,72},{48,80},{56,88},{64,... | collective-permute-start | bytes 1572872 | tf_op jit(solution)/shard_map/ppermute | solution.py:284
  32.8 45.1 %copy-start.2 = (bf16[4,128,512]{2,1,0:T(8,128)(2,1)}, bf16[4,128,512]{2,1,0:T(8,128)(2,1)S(1)}, u32[]{:S(2)}) copy-start(bf16[4,128,512]{2,1,0:T(8,128)(2,1)S(1)} %collective-permute-done.rest_0_) | copy-start | bytes 1572868
  32.8 35.7 %collective-permute-start.12 = (bf16[4,128,512]{2,1,0:T(8,128)(2,1)}, bf16[4,128,512]{2,1,0:T(8,128)(2,1)S(1)}, u32[]{:S(2)}, u32[]{:S(2)}) collective-permute-start(bf16[4,128,512]{2,1,0:T(8,128)(2,1)} %get-tuple-element.75), channel_id=1, source_target_pairs={{0,72},{8,80},{16,88},{24,64},{32,104},{40,112},{48,120},{56,96},{... | collective-permute-start | bytes 1572872 | tf_op jit(solution)/shard_map/ppermute | solution.py:284
  45.2 32.7 %collective-permute-start.7 = (bf16[4,128,512]{2,1,0:T(8,128)(2,1)}, bf16[4,128,512]{2,1,0:T(8,128)(2,1)S(1)}, u32[]{:S(2)}, u32[]{:S(2)}) collective-permute-start(bf16[4,128,512]{2,1,0:T(8,128)(2,1)} %get-tuple-element.70), channel_id=1, source_target_pairs={{0,24},{8,0},{16,8},{24,16},{32,56},{40,32},{48,40},{56,48},{64,88... | collective-permute-start | bytes 1572872 | tf_op jit(solution)/shard_map/ppermute | solution.py:284
  48.2 29.7 %copy-start.3 = (bf16[4,128,512]{2,1,0:T(8,128)(2,1)}, bf16[4,128,512]{2,1,0:T(8,128)(2,1)S(1)}, u32[]{:S(2)}) copy-start(bf16[4,128,512]{2,1,0:T(8,128)(2,1)S(1)} %collective-permute-done.4.rest_2_) | copy-start | bytes 1572868
  48.2 32.1 %collective-permute-start.8 = (bf16[4,128,512]{2,1,0:T(8,128)(2,1)}, bf16[4,128,512]{2,1,0:T(8,128)(2,1)S(1)}, u32[]{:S(2)}, u32[]{:S(2)}) collective-permute-start(bf16[4,128,512]{2,1,0:T(8,128)(2,1)} %get-tuple-element.71), channel_id=1, source_target_pairs={{0,88},{8,64},{16,72},{24,80},{32,120},{40,96},{48,104},{56,112},{... | collective-permute-start | bytes 1572872 | tf_op jit(solution)/shard_map/ppermute | solution.py:284
  59.6 18.4 %copy-start.4 = (bf16[4,128,512]{2,1,0:T(8,128)(2,1)}, bf16[4,128,512]{2,1,0:T(8,128)(2,1)S(1)}, u32[]{:S(2)}) copy-start(bf16[4,128,512]{2,1,0:T(8,128)(2,1)S(1)} %collective-permute-done.5.rest_3_) | copy-start | bytes 1572868
  59.6 21.1 %collective-permute-start.9 = (bf16[4,128,512]{2,1,0:T(8,128)(2,1)}, bf16[4,128,512]{2,1,0:T(8,128)(2,1)S(1)}, u32[]{:S(2)}, u32[]{:S(2)}) collective-permute-start(bf16[4,128,512]{2,1,0:T(8,128)(2,1)} %get-tuple-element.72), channel_id=1, source_target_pairs={{0,8},{8,16},{16,24},{24,0},{32,40},{40,48},{48,56},{56,32},{64,72... | collective-permute-start | bytes 1572872 | tf_op jit(solution)/shard_map/ppermute | solution.py:284
  68.4 11.8 %copy-start.5 = (bf16[4,128,512]{2,1,0:T(8,128)(2,1)}, bf16[4,128,512]{2,1,0:T(8,128)(2,1)S(1)}, u32[]{:S(2)}) copy-start(bf16[4,128,512]{2,1,0:T(8,128)(2,1)S(1)} %collective-permute-done.6.rest_4_) | copy-start | bytes 1572868
  68.4 19.9 %collective-permute-start.10 = (bf16[4,128,512]{2,1,0:T(8,128)(2,1)}, bf16[4,128,512]{2,1,0:T(8,128)(2,1)S(1)}, u32[]{:S(2)}, u32[]{:S(2)}) collective-permute-start(bf16[4,128,512]{2,1,0:T(8,128)(2,1)} %get-tuple-element.73), channel_id=1, source_target_pairs={{0,40},{8,48},{16,56},{24,32},{32,72},{40,80},{48,88},{56,64},{64,... | collective-permute-start | bytes 1572872 | tf_op jit(solution)/shard_map/ppermute | solution.py:284
  68.5 12.3 %copy-start.6 = (bf16[4,128,512]{2,1,0:T(8,128)(2,1)}, bf16[4,128,512]{2,1,0:T(8,128)(2,1)S(1)}, u32[]{:S(2)}) copy-start(bf16[4,128,512]{2,1,0:T(8,128)(2,1)S(1)} %collective-permute-done.12.rest_10_) | copy-start | bytes 1572868
  68.5 26.2 %collective-permute-start.11 = (bf16[4,128,512]{2,1,0:T(8,128)(2,1)}, bf16[4,128,512]{2,1,0:T(8,128)(2,1)S(1)}, u32[]{:S(2)}, u32[]{:S(2)}) collective-permute-start(bf16[4,128,512]{2,1,0:T(8,128)(2,1)} %get-tuple-element.74), channel_id=1, source_target_pairs={{0,120},{8,96},{16,104},{24,112},{32,24},{40,0},{48,8},{56,16},{64... | collective-permute-start | bytes 1572872 | tf_op jit(solution)/shard_map/ppermute | solution.py:284
  77.9 2.8 %copy-start.7 = (bf16[4,128,512]{2,1,0:T(8,128)(2,1)}, bf16[4,128,512]{2,1,0:T(8,128)(2,1)S(1)}, u32[]{:S(2)}) copy-start(bf16[4,128,512]{2,1,0:T(8,128)(2,1)S(1)} %collective-permute-done.7.rest_5_) | copy-start | bytes 1572868
  77.9 67.1 %collective-permute-start.20 = (bf16[256,2048]{1,0:T(8,128)(2,1)S(1)}, bf16[256,2048]{1,0:T(8,128)(2,1)}, u32[]{:S(2)}, u32[]{:S(2)}) collective-permute-start(bf16[256,2048]{1,0:T(8,128)(2,1)S(1)} %copy-done), channel_id=1, source_target_pairs={{0,4},{1,5},{2,6},{3,7},{4,0},{5,1},{6,2},{7,3},{8,12},{9,13},{10,... | collective-permute-start | bytes 3145736 | tf_op jit(solution)/shard_map/ppermute | solution.py:260
  80.3 4.9 %copy-start.8 = (bf16[4,128,512]{2,1,0:T(8,128)(2,1)}, bf16[4,128,512]{2,1,0:T(8,128)(2,1)S(1)}, u32[]{:S(2)}) copy-start(bf16[4,128,512]{2,1,0:T(8,128)(2,1)S(1)} %collective-permute-done.8.rest_6_) | copy-start | bytes 1572868
  80.3 29.9 %collective-permute-start.13 = (bf16[4,128,512]{2,1,0:T(8,128)(2,1)}, bf16[4,128,512]{2,1,0:T(8,128)(2,1)}, u32[]{:S(2)}, u32[]{:S(2)}) collective-permute-start(bf16[4,128,512]{2,1,0:T(8,128)(2,1)} %get-tuple-element.77), channel_id=1, source_target_pairs={{0,56},{8,32},{16,40},{24,48},{32,88},{40,64},{48,72},{56,80},{64,... | collective-permute-start | bytes 1572872 | tf_op jit(solution)/shard_map/ppermute | solution.py:284
  80.7 7.6 %copy-start.9 = (bf16[4,128,512]{2,1,0:T(8,128)(2,1)}, bf16[4,128,512]{2,1,0:T(8,128)(2,1)S(1)}, u32[]{:S(2)}) copy-start(bf16[4,128,512]{2,1,0:T(8,128)(2,1)S(1)} %collective-permute-done.9.rest_7_) | copy-start | bytes 1572868
  80.7 29.5 %collective-permute-start.14 = (bf16[4,128,512]{2,1,0:T(8,128)(2,1)}, bf16[4,128,512]{2,1,0:T(8,128)(2,1)}, u32[]{:S(2)}, u32[]{:S(2)}) collective-permute-start(bf16[4,128,512]{2,1,0:T(8,128)(2,1)} %get-tuple-element.78), channel_id=1, source_target_pairs={{0,104},{8,112},{16,120},{24,96},{32,8},{40,16},{48,24},{56,0},{64... | collective-permute-start | bytes 1572872 | tf_op jit(solution)/shard_map/ppermute | solution.py:284
  88.3 6.3 %copy-start.10 = (bf16[4,128,512]{2,1,0:T(8,128)(2,1)}, bf16[4,128,512]{2,1,0:T(8,128)(2,1)S(1)}, u32[]{:S(2)}) copy-start(bf16[4,128,512]{2,1,0:T(8,128)(2,1)S(1)} %collective-permute-done.10.rest_8_) | copy-start | bytes 1572868
  88.3 25.3 %collective-permute-start.15 = (bf16[4,128,512]{2,1,0:T(8,128)(2,1)}, bf16[4,128,512]{2,1,0:T(8,128)(2,1)}, u32[]{:S(2)}, u32[]{:S(2)}) collective-permute-start(bf16[4,128,512]{2,1,0:T(8,128)(2,1)} %get-tuple-element.79), channel_id=1, source_target_pairs={{0,16},{8,24},{16,0},{24,8},{32,48},{40,56},{48,32},{56,40},{64,80... | collective-permute-start | bytes 1572872 | tf_op jit(solution)/shard_map/ppermute | solution.py:284
  94.7 0.8 copy-start.11
  95.5 24.7 %collective-permute-start.16 = (bf16[4,128,512]{2,1,0:T(8,128)(2,1)}, bf16[4,128,512]{2,1,0:T(8,128)(2,1)}, u32[]{:S(2)}, u32[]{:S(2)}) collective-permute-start(bf16[4,128,512]{2,1,0:T(8,128)(2,1)} %get-tuple-element.80), channel_id=1, source_target_pairs={{0,64},{8,72},{16,80},{24,88},{32,96},{40,104},{48,112},{56,120},{... | collective-permute-start | bytes 1572872 | tf_op jit(solution)/shard_map/ppermute | solution.py:284
  130.0 11.2 %collective-permute-start.17 = (bf16[512,256]{1,0:T(8,128)(2,1)}, bf16[512,256]{1,0:T(8,128)(2,1)S(1)}, u32[]{:S(2)}, u32[]{:S(2)}) collective-permute-start(bf16[512,256]{1,0:T(8,128)(2,1)} %get-tuple-element.81), channel_id=1, source_target_pairs={{0,2},{1,3},{2,4},{3,5},{4,6},{5,7},{6,0},{7,1},{8,10},{9,11},{10,... | collective-permute-start | bytes 786440 | tf_op jit(solution)/shard_map/ppermute | solution.py:260
  130.1 13.8 %collective-permute-start.18 = (bf16[512,256]{1,0:T(8,128)(2,1)}, bf16[512,256]{1,0:T(8,128)(2,1)}, u32[]{:S(2)}, u32[]{:S(2)}) collective-permute-start(bf16[512,256]{1,0:T(8,128)(2,1)} %get-tuple-element.82), channel_id=1, source_target_pairs={{0,4},{1,5},{2,6},{3,7},{4,0},{5,1},{6,2},{7,3},{8,12},{9,13},{10,... | collective-permute-start | bytes 786440 | tf_op jit(solution)/shard_map/ppermute | solution.py:260
  132.3 12.7 %collective-permute-start.19 = (bf16[512,256]{1,0:T(8,128)(2,1)}, bf16[512,256]{1,0:T(8,128)(2,1)}, u32[]{:S(2)}, u32[]{:S(2)}) collective-permute-start(bf16[512,256]{1,0:T(8,128)(2,1)} %get-tuple-element.83), channel_id=1, source_target_pairs={{0,6},{1,7},{2,0},{3,1},{4,2},{5,3},{6,4},{7,5},{8,14},{9,15},{10,... | collective-permute-start | bytes 786440 | tf_op jit(solution)/shard_map/ppermute | solution.py:260
  145.0 1.0 copy-start.1
  148.7 4.4 %collective-permute-start.21 = (bf16[256,2048]{1,0:T(8,128)(2,1)S(1)}, bf16[256,2048]{1,0:T(8,128)(2,1)S(1)}, u32[]{:S(2)}, u32[]{:S(2)}) collective-permute-start(bf16[256,2048]{1,0:T(8,128)(2,1)S(1)} %mix.3), channel_id=1, source_target_pairs={{0,1},{1,0},{2,3},{3,2},{4,5},{5,4},{6,7},{7,6},{8,9},{9,8},{10,11... | collective-permute-start | bytes 3145736 | tf_op jit(solution)/shard_map/ppermute | solution.py:295

commit v8 on v7

--- a/solution.py
+++ b/solution.py
@@ -13,7 +13,7 @@
 KT = 4
 CAP = 4
 BLOCK = 512
-GROUP = 2
+GROUP = 4
 SIDE = 4
 SHIFTS = (10, 6, 12, 14, 4, 3, 11, 1, 5, 15, 9, 7, 13, 2, 8)
 FIRST = 2

time: 155 us -> 154 us (level)
  no operation moved by 1% of the time
where the time goes in v8:
time: 154 us
  starting transfers between devices  62.6 us (41%)
  Pallas kernels  47.1 us (31%)
  waiting for transfers between devices  40.2 us (26%)
  other arithmetic  1.87 us (1%)
  local copies, waits for them, and re-layouts  1.81 us (1%)
    ppermute x15, starting transfers between devices, body(): lax.ppermute(send, 'seq', [(s, shifted(s, shift)) for s in range(shards)])  54.3 us
    ppermute x15, waiting for transfers between devices, body(): lax.ppermute(send, 'seq', [(s, shifted(s, shift)) for s in range(shards)])  36.1 us
    pallas_call x2, Pallas kernels, project(): pl.pallas_call(functools.partial(project_kernel, widths=widths, scales=le...  16.4 us
    pallas_call x2, Pallas kernels, attend(): pl.pallas_call(functools.partial(attend_kernel, tiles=tiles, heads=querie...  16.3 us
    pallas_call x2, Pallas kernels, dispatch(): pl.pallas_call(functools.partial(dispatch_kernel, shifts=shifts), in_spec...  7.27 us
    ppermute x6, starting transfers between devices, along(): lax.ppermute(x, 'head', [(s, (s // 2 + shift) % pairs * 2 + s % 2) for s...  6.63 us
    pallas_call x2, Pallas kernels, mix(): pl.pallas_call(mix_kernel, grid_spec=pltpu.PrefetchScalarGridSpec(num_sca...  5.45 us
    ppermute x6, waiting for transfers between devices, along(): lax.ppermute(x, 'head', [(s, (s // 2 + shift) % pairs * 2 + s % 2) for s...  4.03 us
  transfers between devices with their start and end apart: 22, of which 11 were waited for; matrix products, arithmetic and copies ran while one was open for 0% of the time, Pallas kernels for 29%

profile of v8, /device:TPU:7, one launch (start us, length us, event | category | flops | bytes accessed | tf_op | source)
XLA Modules:
  0.0 153.7 jit_solution(658021121546173382)
XLA Ops:
  0.0 1.3 collective-permute-start.2
  1.3 1.4 collective-permute-start.3
  2.7 1.7 %tables.1 = (s32[8,128]{1,0:T(8,128)}, s32[4,256]{1,0:T(4,128)}) custom-call(s32[1]{0:T(128)} %bitcast.3.me_ref, s32[4,256]{1,0:T(4,128)} %bitcast.21), custom_call_target="tpu_custom_call" | custom-call | tf_op jit(solution)/shard_map/tables/pallas_call | solution.py:262
  4.4 9.2 %project.2.held_ref.own_ref = bf16[16,128,512]{2,1,0:T(8,128)(2,1)} custom-call(bf16[2048,2048]{1,0:T(8,128)(2,1)} %refs_0_.2, f32[16,128]{1,0:T(8,128)} %bitcast.19, bf16[3,2048,256]{2,1,0:T(8,128)(2,1)} %bitcast.16, bf16[3,2048,256]{2,1,0:T(8,128)(2,1)} %bitcast.17), custom_call_target="tpu_custom_call" | custom-call | tf_op jit(solution)/shard_map/project/pallas_call | solution.py:106
  13.6 2.7 %dispatch.2 = (bf16[4,128,512]{2,1,0:T(8,128)(2,1)}, bf16[4,128,512]{2,1,0:T(8,128)(2,1)}) custom-call(s32[1]{0:T(128)} %bitcast.3.me_ref, s32[8,128]{1,0:T(8,128)} %get-tuple-element.47.chosen_ref, bf16[16,128,512]{2,1,0:T(8,128)(2,1)} %project.2.held_ref.own_ref), custom_call_target="tpu_custom_call" | custom-call | tf_op jit(solution)/shard_map/dispatch/pallas_call | solution.py:141
  16.4 4.5 %collective-permute-start = (bf16[4,128,512]{2,1,0:T(8,128)(2,1)}, bf16[4,128,512]{2,1,0:T(8,128)(2,1)S(1)}, u32[]{:S(2)}, u32[]{:S(2)}) collective-permute-start(bf16[4,128,512]{2,1,0:T(8,128)(2,1)} %get-tuple-element.51), channel_id=1, source_target_pairs={{0,80},{8,88},{16,64},{24,72},{32,112},{40,120},{48,96},{56,104},{... | collective-permute-start | bytes 1572872 | tf_op jit(solution)/shard_map/ppermute | solution.py:284
  20.9 2.3 %collective-permute-start.1 = (bf16[4,128,512]{2,1,0:T(8,128)(2,1)}, bf16[4,128,512]{2,1,0:T(8,128)(2,1)}, u32[]{:S(2)}, u32[]{:S(2)}) collective-permute-start(bf16[4,128,512]{2,1,0:T(8,128)(2,1)} %get-tuple-element.52), channel_id=1, source_target_pairs={{0,48},{8,56},{16,32},{24,40},{32,80},{40,88},{48,64},{56,72},{64,... | collective-permute-start | bytes 1572872 | tf_op jit(solution)/shard_map/ppermute | solution.py:284
  23.2 4.5 %dispatch.3 = (bf16[4,128,512]{2,1,0:T(8,128)(2,1)}, bf16[4,128,512]{2,1,0:T(8,128)(2,1)}, bf16[4,128,512]{2,1,0:T(8,128)(2,1)}, bf16[4,128,512]{2,1,0:T(8,128)(...) custom-call(s32[1]{0:T(128)} %bitcast.3.me_ref, ...), custom_call_target="tpu_custom_call" | custom-call | tf_op jit(solution)/shard_map/dispatch/pallas_call | solution.py:141
  27.7 0.0 collective-permute-done.3.refs_7_
  27.7 2.0 %collective-permute-start.4 = (bf16[4,128,512]{2,1,0:T(8,128)(2,1)}, bf16[4,128,512]{2,1,0:T(8,128)(2,1)S(1)}, u32[]{:S(2)}, u32[]{:S(2)}) collective-permute-start(bf16[4,128,512]{2,1,0:T(8,128)(2,1)} %get-tuple-element.67), channel_id=1, source_target_pairs={{0,96},{8,104},{16,112},{24,120},{32,0},{40,8},{48,16},{56,24},{64... | collective-permute-start | bytes 1572872 | tf_op jit(solution)/shard_map/ppermute | solution.py:284
  29.7 0.9 collective-permute-start.5
  30.7 1.4 collective-permute-start.6
  32.1 0.7 collective-permute-done.rest_0_
  32.8 3.5 %collective-permute-start.12 = (bf16[4,128,512]{2,1,0:T(8,128)(2,1)}, bf16[4,128,512]{2,1,0:T(8,128)(2,1)S(1)}, u32[]{:S(2)}, u32[]{:S(2)}) collective-permute-start(bf16[4,128,512]{2,1,0:T(8,128)(2,1)} %get-tuple-element.75), channel_id=1, source_target_pairs={{0,72},{8,80},{16,88},{24,64},{32,104},{40,112},{48,120},{56,96},{... | collective-permute-start | bytes 1572872 | tf_op jit(solution)/shard_map/ppermute | solution.py:284
  36.3 8.9 %collective-permute-done.1.rest_1_ = bf16[4,128,512]{2,1,0:T(8,128)(2,1)} collective-permute-done((bf16[4,128,512]{2,1,0:T(8,128)(2,1)}, bf16[4,128,512]{2,1,0:T(8,128)(2,1)}, u32[]{:S(2)}, u32[]{:S(2)}) %collective-permute-start.1) | collective-permute-done | bytes 524320 | tf_op jit(solution)/shard_map/ppermute | solution.py:284
  45.2 0.6 collective-permute-start.7
  45.8 2.4 %collective-permute-done.4.rest_2_ = bf16[4,128,512]{2,1,0:T(8,128)(2,1)S(1)} collective-permute-done((bf16[4,128,512]{2,1,0:T(8,128)(2,1)}, bf16[4,128,512]{2,1,0:T(8,128)(2,1)S(1)}, u32[]{:S(2)}, u32[]{:S(2)}) %collective-permute-start.4) | collective-permute-done | bytes 524320 | tf_op jit(solution)/shard_map/ppermute | solution.py:284
  48.2 11.4 %collective-permute-start.8 = (bf16[4,128,512]{2,1,0:T(8,128)(2,1)}, bf16[4,128,512]{2,1,0:T(8,128)(2,1)S(1)}, u32[]{:S(2)}, u32[]{:S(2)}) collective-permute-start(bf16[4,128,512]{2,1,0:T(8,128)(2,1)} %get-tuple-element.71), channel_id=1, source_target_pairs={{0,88},{8,64},{16,72},{24,80},{32,120},{40,96},{48,104},{56,112},{... | collective-permute-start | bytes 1572872 | tf_op jit(solution)/shard_map/ppermute | solution.py:284
  59.6 0.0 collective-permute-done.5.rest_3_
  59.6 3.1 %collective-permute-start.9 = (bf16[4,128,512]{2,1,0:T(8,128)(2,1)}, bf16[4,128,512]{2,1,0:T(8,128)(2,1)S(1)}, u32[]{:S(2)}, u32[]{:S(2)}) collective-permute-start(bf16[4,128,512]{2,1,0:T(8,128)(2,1)} %get-tuple-element.72), channel_id=1, source_target_pairs={{0,8},{8,16},{16,24},{24,0},{32,40},{40,48},{48,56},{56,32},{64,72... | collective-permute-start | bytes 1572872 | tf_op jit(solution)/shard_map/ppermute | solution.py:284
  62.6 5.8 %collective-permute-done.6.rest_4_ = bf16[4,128,512]{2,1,0:T(8,128)(2,1)S(1)} collective-permute-done((bf16[4,128,512]{2,1,0:T(8,128)(2,1)}, bf16[4,128,512]{2,1,0:T(8,128)(2,1)S(1)}, u32[]{:S(2)}, u32[]{:S(2)}) %collective-permute-start.6) | collective-permute-done | bytes 524320 | tf_op jit(solution)/shard_map/ppermute | solution.py:284
  68.4 0.0 collective-permute-start.10
  68.5 9.4 %collective-permute-start.11 = (bf16[4,128,512]{2,1,0:T(8,128)(2,1)}, bf16[4,128,512]{2,1,0:T(8,128)(2,1)S(1)}, u32[]{:S(2)}, u32[]{:S(2)}) collective-permute-start(bf16[4,128,512]{2,1,0:T(8,128)(2,1)} %get-tuple-element.74), channel_id=1, source_target_pairs={{0,120},{8,96},{16,104},{24,112},{32,24},{40,0},{48,8},{56,16},{64... | collective-permute-start | bytes 1572872 | tf_op jit(solution)/shard_map/ppermute | solution.py:284
  77.9 0.1 collective-permute-start.20
  78.0 2.3 %collective-permute-done.8.rest_6_ = bf16[4,128,512]{2,1,0:T(8,128)(2,1)S(1)} collective-permute-done((bf16[4,128,512]{2,1,0:T(8,128)(2,1)}, bf16[4,128,512]{2,1,0:T(8,128)(2,1)S(1)}, u32[]{:S(2)}, u32[]{:S(2)}) %collective-permute-start.8) | collective-permute-done | bytes 524320 | tf_op jit(solution)/shard_map/ppermute | solution.py:284
  80.3 0.4 collective-permute-start.13
  80.7 4.4 %collective-permute-start.14 = (bf16[4,128,512]{2,1,0:T(8,128)(2,1)}, bf16[4,128,512]{2,1,0:T(8,128)(2,1)}, u32[]{:S(2)}, u32[]{:S(2)}) collective-permute-start(bf16[4,128,512]{2,1,0:T(8,128)(2,1)} %get-tuple-element.78), channel_id=1, source_target_pairs={{0,104},{8,112},{16,120},{24,96},{32,8},{40,16},{48,24},{56,0},{64... | collective-permute-start | bytes 1572872 | tf_op jit(solution)/shard_map/ppermute | solution.py:284
  85.2 3.1 %collective-permute-done.10.rest_8_ = bf16[4,128,512]{2,1,0:T(8,128)(2,1)S(1)} collective-permute-done((bf16[4,128,512]{2,1,0:T(8,128)(2,1)}, bf16[4,128,512]{2,1,0:T(8,128)(2,1)S(1)}, u32[]{:S(2)}, u32[]{:S(2)}) %collective-permute-start.10) | collective-permute-done | bytes 524320 | tf_op jit(solution)/shard_map/ppermute | solution.py:284
  88.3 6.3 %collective-permute-start.15 = (bf16[4,128,512]{2,1,0:T(8,128)(2,1)}, bf16[4,128,512]{2,1,0:T(8,128)(2,1)}, u32[]{:S(2)}, u32[]{:S(2)}) collective-permute-start(bf16[4,128,512]{2,1,0:T(8,128)(2,1)} %get-tuple-element.79), channel_id=1, source_target_pairs={{0,16},{8,24},{16,0},{24,8},{32,48},{40,56},{48,32},{56,40},{64,80... | collective-permute-start | bytes 1572872 | tf_op jit(solution)/shard_map/ppermute | solution.py:284
  94.7 0.8 copy-done.11
  95.5 4.0 %collective-permute-start.16 = (bf16[4,128,512]{2,1,0:T(8,128)(2,1)}, bf16[4,128,512]{2,1,0:T(8,128)(2,1)}, u32[]{:S(2)}, u32[]{:S(2)}) collective-permute-start(bf16[4,128,512]{2,1,0:T(8,128)(2,1)} %get-tuple-element.80), channel_id=1, source_target_pairs={{0,64},{8,72},{16,80},{24,88},{32,96},{40,104},{48,112},{56,120},{... | collective-permute-start | bytes 1572872 | tf_op jit(solution)/shard_map/ppermute | solution.py:284
  99.5 7.2 %project.3.queries_ref = bf16[16,128,256]{2,1,0:T(8,128)(2,1)} custom-call(bf16[2048,2048]{1,0:T(8,128)(2,1)} %refs_0_.2, f32[16,128]{1,0:T(8,128)} %bitcast.20, bf16[3,2048,256]{2,1,0:T(8,128)(2,1)} %bitcast.18), custom_call_target="tpu_custom_call" | custom-call | tf_op jit(solution)/shard_map/project/pallas_call | solution.py:106
  106.7 0.6 pad_add_fusion.first_ref
  107.3 2.9 %collective-permute-done.13.rest_11_ = bf16[4,128,512]{2,1,0:T(8,128)(2,1)} collective-permute-done((bf16[4,128,512]{2,1,0:T(8,128)(2,1)}, bf16[4,128,512]{2,1,0:T(8,128)(2,1)}, u32[]{:S(2)}, u32[]{:S(2)}) %collective-permute-start.13) | collective-permute-done | bytes 524320 | tf_op jit(solution)/shard_map/ppermute | solution.py:284
  110.2 3.4 %collective-permute-done.15.rest_13_ = bf16[4,128,512]{2,1,0:T(8,128)(2,1)} collective-permute-done((bf16[4,128,512]{2,1,0:T(8,128)(2,1)}, bf16[4,128,512]{2,1,0:T(8,128)(2,1)}, u32[]{:S(2)}, u32[]{:S(2)}) %collective-permute-start.15) | collective-permute-done | bytes 524320 | tf_op jit(solution)/shard_map/ppermute | solution.py:284
  113.6 6.6 %collective-permute-done.16.rest_14_ = bf16[4,128,512]{2,1,0:T(8,128)(2,1)} collective-permute-done((bf16[4,128,512]{2,1,0:T(8,128)(2,1)}, bf16[4,128,512]{2,1,0:T(8,128)(2,1)}, u32[]{:S(2)}, u32[]{:S(2)}) %collective-permute-start.16) | collective-permute-done | bytes 524320 | tf_op jit(solution)/shard_map/ppermute | solution.py:284
  120.2 9.1 %attend.3 = (bf16[512,256]{1,0:T(8,128)(2,1)}, bf16[512,256]{1,0:T(8,128)(2,1)}, bf16[512,256]{1,0:T(8,128)(2,1)}) custom-call(s32[2]{0:T(128)} %pad_add_fusion.first_ref, s32[4,256]{1,0:T(4,128)} %get-tuple-element.46.source_ref, bf16[16,128,256]{2,1,0:T(8,128)(2,1)} %project.3.queries_ref, bf16[16,128,512]{2,1,0:T(8,128)(2,1)} %project.2.held_ref.own_ref, ...), custom_call_target="tpu_custom_call" | custom-call | tf_op jit(solution)/shard_map/attend/pallas_call | solution.py:204
  129.4 0.1 collective-permute-start.17
  129.5 2.2 %collective-permute-start.18 = (bf16[512,256]{1,0:T(8,128)(2,1)}, bf16[512,256]{1,0:T(8,128)(2,1)}, u32[]{:S(2)}, u32[]{:S(2)}) collective-permute-start(bf16[512,256]{1,0:T(8,128)(2,1)} %get-tuple-element.82), channel_id=1, source_target_pairs={{0,4},{1,5},{2,6},{3,7},{4,0},{5,1},{6,2},{7,3},{8,12},{9,13},{10,... | collective-permute-start | bytes 786440 | tf_op jit(solution)/shard_map/ppermute | solution.py:260
  131.7 1.5 collective-permute-start.19
  133.2 7.1 %attend.2 = bf16[512,256]{1,0:T(8,128)(2,1)} custom-call(s32[2]{0:T(128)} %pad_add_fusion.first_ref, s32[4,256]{1,0:T(4,128)} %get-tuple-element.46.source_ref, bf16[16,128,256]{2,1,0:T(8,128)(2,1)} %project.3.queries_ref, bf16[16,128,512]{2,1,0:T(8,128)(2,1)} %project.2.held_ref.own_ref, bf16[4,128,512]{2,1,0:T(8,128)(2,1)} %copy-done.2, ...), custom_call_target="tpu_custom_call" | custom-call | tf_op jit(solution)/shard_map/attend/pallas_call | solution.py:204
  140.4 2.9 %collective-permute-done.18 = bf16[512,256]{1,0:T(8,128)(2,1)} collective-permute-done((bf16[512,256]{1,0:T(8,128)(2,1)}, bf16[512,256]{1,0:T(8,128)(2,1)}, u32[]{:S(2)}, u32[]{:S(2)}) %collective-permute-start.18) | collective-permute-done | bytes 262176 | tf_op jit(solution)/shard_map/ppermute | solution.py:260
  143.2 1.1 collective-permute-done.19
  144.4 0.9 copy-done.1
  145.3 2.7 %mix.3 = bf16[256,2048]{1,0:T(8,128)(2,1)S(1)} custom-call(s32[1]{0:T(128)} %bitcast.11.half_ref, bf16[2,256,256]{2,1,0:T(8,128)(2,1)S(1)} %bitcast.12, bf16[2,256,256]{2,1,0:T(8,128)(2,1)S(1)} %bitcast.14, bf16[2,256,256]{2,1,0:T(8,128)(2,1)} %bitcast.9.refs_2_, bf16[2,256,256]{2,1,0:T(8,128)(2,1)} %bitcast.10.refs_3_, bf16[256,2048]{1,0:T(8,128)(2,1)S(1)} %copy-done, ...), custom_call_target="tpu_custom_call" | custom-call | tf_op jit(solution)/shard_map/mix/pallas_call | solution.py:230
  148.0 1.6 %collective-permute-start.21 = (bf16[256,2048]{1,0:T(8,128)(2,1)S(1)}, bf16[256,2048]{1,0:T(8,128)(2,1)S(1)}, u32[]{:S(2)}, u32[]{:S(2)}) collective-permute-start(bf16[256,2048]{1,0:T(8,128)(2,1)S(1)} %mix.3), channel_id=1, source_target_pairs={{0,1},{1,0},{2,3},{3,2},{4,5},{5,4},{6,7},{7,6},{8,9},{9,8},{10,11... | collective-permute-start | bytes 3145736 | tf_op jit(solution)/shard_map/ppermute | solution.py:295
  149.7 2.8 %mix.2 = f32[256,2048]{1,0:T(8,128)S(1)} custom-call(s32[1]{0:T(128)} %bitcast.half_ref, bf16[2,256,256]{2,1,0:T(8,128)(2,1)S(1)} %bitcast.13, bf16[2,256,256]{2,1,0:T(8,128)(2,1)S(1)} %bitcast.15, bf16[2,256,256]{2,1,0:T(8,128)(2,1)} %bitcast.9.refs_2_, bf16[2,256,256]{2,1,0:T(8,128)(2,1)} %bitcast.10.refs_3_, bf16[256,2048]{1,0:T(8,128)(2,1)S(1)} %copy-done, ...), custom_call_target="tpu_custom_call" | custom-call | tf_op jit(solution)/shard_map/mix/pallas_call | solution.py:230
  152.4 1.3 add_convert_fusion
  (31 shorter events, 0.1 us)
Async XLA Ops:
  0.0 27.7 %collective-permute-start.2 = (bf16[256,2048]{1,0:T(8,128)(2,1)}, bf16[256,2048]{1,0:T(8,128)(2,1)S(1)}, u32[]{:S(2)}, u32[]{:S(2)}) collective-permute-start(bf16[256,2048]{1,0:T(8,128)(2,1)} %refs_4_.3), channel_id=1, source_target_pairs={{0,2},{1,3},{2,4},{3,5},{4,6},{5,7},{6,0},{7,1},{8,10},{9,11},{10,... | collective-permute-start | bytes 3145736 | tf_op jit(solution)/shard_map/ppermute | solution.py:260
  1.3 26.4 %collective-permute-start.3 = (bf16[256,2048]{1,0:T(8,128)(2,1)}, bf16[256,2048]{1,0:T(8,128)(2,1)S(1)}, u32[]{:S(2)}, u32[]{:S(2)}) collective-permute-start(bf16[256,2048]{1,0:T(8,128)(2,1)} %refs_4_.3), channel_id=1, source_target_pairs={{0,6},{1,7},{2,0},{3,1},{4,2},{5,3},{6,4},{7,5},{8,14},{9,15},{10,... | collective-permute-start | bytes 3145736 | tf_op jit(solution)/shard_map/ppermute | solution.py:260
  13.6 64.3 %copy-start = (bf16[256,2048]{1,0:T(8,128)(2,1)S(1)}, bf16[256,2048]{1,0:T(8,128)(2,1)}, u32[]{:S(2)}) copy-start(bf16[256,2048]{1,0:T(8,128)(2,1)} %refs_4_.3) | copy-start | bytes 3145732
  16.4 16.4 %collective-permute-start = (bf16[4,128,512]{2,1,0:T(8,128)(2,1)}, bf16[4,128,512]{2,1,0:T(8,128)(2,1)S(1)}, u32[]{:S(2)}, u32[]{:S(2)}) collective-permute-start(bf16[4,128,512]{2,1,0:T(8,128)(2,1)} %get-tuple-element.51), channel_id=1, source_target_pairs={{0,80},{8,88},{16,64},{24,72},{32,112},{40,120},{48,96},{56,104},{... | collective-permute-start | bytes 1572872 | tf_op jit(solution)/shard_map/ppermute | solution.py:284
  20.9 24.3 %collective-permute-start.1 = (bf16[4,128,512]{2,1,0:T(8,128)(2,1)}, bf16[4,128,512]{2,1,0:T(8,128)(2,1)}, u32[]{:S(2)}, u32[]{:S(2)}) collective-permute-start(bf16[4,128,512]{2,1,0:T(8,128)(2,1)} %get-tuple-element.52), channel_id=1, source_target_pairs={{0,48},{8,56},{16,32},{24,40},{32,80},{40,88},{48,64},{56,72},{64,... | collective-permute-start | bytes 1572872 | tf_op jit(solution)/shard_map/ppermute | solution.py:284
  27.7 20.5 %collective-permute-start.4 = (bf16[4,128,512]{2,1,0:T(8,128)(2,1)}, bf16[4,128,512]{2,1,0:T(8,128)(2,1)S(1)}, u32[]{:S(2)}, u32[]{:S(2)}) collective-permute-start(bf16[4,128,512]{2,1,0:T(8,128)(2,1)} %get-tuple-element.67), channel_id=1, source_target_pairs={{0,96},{8,104},{16,112},{24,120},{32,0},{40,8},{48,16},{56,24},{64... | collective-permute-start | bytes 1572872 | tf_op jit(solution)/shard_map/ppermute | solution.py:284
  29.7 29.8 %collective-permute-start.5 = (bf16[4,128,512]{2,1,0:T(8,128)(2,1)}, bf16[4,128,512]{2,1,0:T(8,128)(2,1)S(1)}, u32[]{:S(2)}, u32[]{:S(2)}) collective-permute-start(bf16[4,128,512]{2,1,0:T(8,128)(2,1)} %get-tuple-element.68), channel_id=1, source_target_pairs={{0,112},{8,120},{16,96},{24,104},{32,16},{40,24},{48,0},{56,8},{64... | collective-permute-start | bytes 1572872 | tf_op jit(solution)/shard_map/ppermute | solution.py:284
  30.7 37.8 %collective-permute-start.6 = (bf16[4,128,512]{2,1,0:T(8,128)(2,1)}, bf16[4,128,512]{2,1,0:T(8,128)(2,1)S(1)}, u32[]{:S(2)}, u32[]{:S(2)}) collective-permute-start(bf16[4,128,512]{2,1,0:T(8,128)(2,1)} %get-tuple-element.69), channel_id=1, source_target_pairs={{0,32},{8,40},{16,48},{24,56},{32,64},{40,72},{48,80},{56,88},{64,... | collective-permute-start | bytes 1572872 | tf_op jit(solution)/shard_map/ppermute | solution.py:284
  32.8 45.1 %copy-start.2 = (bf16[4,128,512]{2,1,0:T(8,128)(2,1)}, bf16[4,128,512]{2,1,0:T(8,128)(2,1)S(1)}, u32[]{:S(2)}) copy-start(bf16[4,128,512]{2,1,0:T(8,128)(2,1)S(1)} %collective-permute-done.rest_0_) | copy-start | bytes 1572868
  32.8 35.7 %collective-permute-start.12 = (bf16[4,128,512]{2,1,0:T(8,128)(2,1)}, bf16[4,128,512]{2,1,0:T(8,128)(2,1)S(1)}, u32[]{:S(2)}, u32[]{:S(2)}) collective-permute-start(bf16[4,128,512]{2,1,0:T(8,128)(2,1)} %get-tuple-element.75), channel_id=1, source_target_pairs={{0,72},{8,80},{16,88},{24,64},{32,104},{40,112},{48,120},{56,96},{... | collective-permute-start | bytes 1572872 | tf_op jit(solution)/shard_map/ppermute | solution.py:284
  45.2 32.7 %collective-permute-start.7 = (bf16[4,128,512]{2,1,0:T(8,128)(2,1)}, bf16[4,128,512]{2,1,0:T(8,128)(2,1)S(1)}, u32[]{:S(2)}, u32[]{:S(2)}) collective-permute-start(bf16[4,128,512]{2,1,0:T(8,128)(2,1)} %get-tuple-element.70), channel_id=1, source_target_pairs={{0,24},{8,0},{16,8},{24,16},{32,56},{40,32},{48,40},{56,48},{64,88... | collective-permute-start | bytes 1572872 | tf_op jit(solution)/shard_map/ppermute | solution.py:284
  48.2 29.7 %copy-start.3 = (bf16[4,128,512]{2,1,0:T(8,128)(2,1)}, bf16[4,128,512]{2,1,0:T(8,128)(2,1)S(1)}, u32[]{:S(2)}) copy-start(bf16[4,128,512]{2,1,0:T(8,128)(2,1)S(1)} %collective-permute-done.4.rest_2_) | copy-start | bytes 1572868
  48.2 32.1 %collective-permute-start.8 = (bf16[4,128,512]{2,1,0:T(8,128)(2,1)}, bf16[4,128,512]{2,1,0:T(8,128)(2,1)S(1)}, u32[]{:S(2)}, u32[]{:S(2)}) collective-permute-start(bf16[4,128,512]{2,1,0:T(8,128)(2,1)} %get-tuple-element.71), channel_id=1, source_target_pairs={{0,88},{8,64},{16,72},{24,80},{32,120},{40,96},{48,104},{56,112},{... | collective-permute-start | bytes 1572872 | tf_op jit(solution)/shard_map/ppermute | solution.py:284
  59.6 18.4 %copy-start.4 = (bf16[4,128,512]{2,1,0:T(8,128)(2,1)}, bf16[4,128,512]{2,1,0:T(8,128)(2,1)S(1)}, u32[]{:S(2)}) copy-start(bf16[4,128,512]{2,1,0:T(8,128)(2,1)S(1)} %collective-permute-done.5.rest_3_) | copy-start | bytes 1572868
  59.6 21.1 %collective-permute-start.9 = (bf16[4,128,512]{2,1,0:T(8,128)(2,1)}, bf16[4,128,512]{2,1,0:T(8,128)(2,1)S(1)}, u32[]{:S(2)}, u32[]{:S(2)}) collective-permute-start(bf16[4,128,512]{2,1,0:T(8,128)(2,1)} %get-tuple-element.72), channel_id=1, source_target_pairs={{0,8},{8,16},{16,24},{24,0},{32,40},{40,48},{48,56},{56,32},{64,72... | collective-permute-start | bytes 1572872 | tf_op jit(solution)/shard_map/ppermute | solution.py:284
  68.4 11.8 %copy-start.5 = (bf16[4,128,512]{2,1,0:T(8,128)(2,1)}, bf16[4,128,512]{2,1,0:T(8,128)(2,1)S(1)}, u32[]{:S(2)}) copy-start(bf16[4,128,512]{2,1,0:T(8,128)(2,1)S(1)} %collective-permute-done.6.rest_4_) | copy-start | bytes 1572868
  68.4 19.9 %collective-permute-start.10 = (bf16[4,128,512]{2,1,0:T(8,128)(2,1)}, bf16[4,128,512]{2,1,0:T(8,128)(2,1)S(1)}, u32[]{:S(2)}, u32[]{:S(2)}) collective-permute-start(bf16[4,128,512]{2,1,0:T(8,128)(2,1)} %get-tuple-element.73), channel_id=1, source_target_pairs={{0,40},{8,48},{16,56},{24,32},{32,72},{40,80},{48,88},{56,64},{64,... | collective-permute-start | bytes 1572872 | tf_op jit(solution)/shard_map/ppermute | solution.py:284
  68.5 12.3 %copy-start.6 = (bf16[4,128,512]{2,1,0:T(8,128)(2,1)}, bf16[4,128,512]{2,1,0:T(8,128)(2,1)S(1)}, u32[]{:S(2)}) copy-start(bf16[4,128,512]{2,1,0:T(8,128)(2,1)S(1)} %collective-permute-done.12.rest_10_) | copy-start | bytes 1572868
  68.5 26.2 %collective-permute-start.11 = (bf16[4,128,512]{2,1,0:T(8,128)(2,1)}, bf16[4,128,512]{2,1,0:T(8,128)(2,1)S(1)}, u32[]{:S(2)}, u32[]{:S(2)}) collective-permute-start(bf16[4,128,512]{2,1,0:T(8,128)(2,1)} %get-tuple-element.74), channel_id=1, source_target_pairs={{0,120},{8,96},{16,104},{24,112},{32,24},{40,0},{48,8},{56,16},{64... | collective-permute-start | bytes 1572872 | tf_op jit(solution)/shard_map/ppermute | solution.py:284
  77.9 2.8 %copy-start.7 = (bf16[4,128,512]{2,1,0:T(8,128)(2,1)}, bf16[4,128,512]{2,1,0:T(8,128)(2,1)S(1)}, u32[]{:S(2)}) copy-start(bf16[4,128,512]{2,1,0:T(8,128)(2,1)S(1)} %collective-permute-done.7.rest_5_) | copy-start | bytes 1572868
  77.9 66.5 %collective-permute-start.20 = (bf16[256,2048]{1,0:T(8,128)(2,1)S(1)}, bf16[256,2048]{1,0:T(8,128)(2,1)}, u32[]{:S(2)}, u32[]{:S(2)}) collective-permute-start(bf16[256,2048]{1,0:T(8,128)(2,1)S(1)} %copy-done), channel_id=1, source_target_pairs={{0,4},{1,5},{2,6},{3,7},{4,0},{5,1},{6,2},{7,3},{8,12},{9,13},{10,... | collective-permute-start | bytes 3145736 | tf_op jit(solution)/shard_map/ppermute | solution.py:260
  80.3 4.9 %copy-start.8 = (bf16[4,128,512]{2,1,0:T(8,128)(2,1)}, bf16[4,128,512]{2,1,0:T(8,128)(2,1)S(1)}, u32[]{:S(2)}) copy-start(bf16[4,128,512]{2,1,0:T(8,128)(2,1)S(1)} %collective-permute-done.8.rest_6_) | copy-start | bytes 1572868
  80.3 29.9 %collective-permute-start.13 = (bf16[4,128,512]{2,1,0:T(8,128)(2,1)}, bf16[4,128,512]{2,1,0:T(8,128)(2,1)}, u32[]{:S(2)}, u32[]{:S(2)}) collective-permute-start(bf16[4,128,512]{2,1,0:T(8,128)(2,1)} %get-tuple-element.77), channel_id=1, source_target_pairs={{0,56},{8,32},{16,40},{24,48},{32,88},{40,64},{48,72},{56,80},{64,... | collective-permute-start | bytes 1572872 | tf_op jit(solution)/shard_map/ppermute | solution.py:284
  80.7 7.6 %copy-start.9 = (bf16[4,128,512]{2,1,0:T(8,128)(2,1)}, bf16[4,128,512]{2,1,0:T(8,128)(2,1)S(1)}, u32[]{:S(2)}) copy-start(bf16[4,128,512]{2,1,0:T(8,128)(2,1)S(1)} %collective-permute-done.9.rest_7_) | copy-start | bytes 1572868
  80.7 29.5 %collective-permute-start.14 = (bf16[4,128,512]{2,1,0:T(8,128)(2,1)}, bf16[4,128,512]{2,1,0:T(8,128)(2,1)}, u32[]{:S(2)}, u32[]{:S(2)}) collective-permute-start(bf16[4,128,512]{2,1,0:T(8,128)(2,1)} %get-tuple-element.78), channel_id=1, source_target_pairs={{0,104},{8,112},{16,120},{24,96},{32,8},{40,16},{48,24},{56,0},{64... | collective-permute-start | bytes 1572872 | tf_op jit(solution)/shard_map/ppermute | solution.py:284
  88.3 6.3 %copy-start.10 = (bf16[4,128,512]{2,1,0:T(8,128)(2,1)}, bf16[4,128,512]{2,1,0:T(8,128)(2,1)S(1)}, u32[]{:S(2)}) copy-start(bf16[4,128,512]{2,1,0:T(8,128)(2,1)S(1)} %collective-permute-done.10.rest_8_) | copy-start | bytes 1572868
  88.3 25.3 %collective-permute-start.15 = (bf16[4,128,512]{2,1,0:T(8,128)(2,1)}, bf16[4,128,512]{2,1,0:T(8,128)(2,1)}, u32[]{:S(2)}, u32[]{:S(2)}) collective-permute-start(bf16[4,128,512]{2,1,0:T(8,128)(2,1)} %get-tuple-element.79), channel_id=1, source_target_pairs={{0,16},{8,24},{16,0},{24,8},{32,48},{40,56},{48,32},{56,40},{64,80... | collective-permute-start | bytes 1572872 | tf_op jit(solution)/shard_map/ppermute | solution.py:284
  94.7 0.8 copy-start.11
  95.5 24.7 %collective-permute-start.16 = (bf16[4,128,512]{2,1,0:T(8,128)(2,1)}, bf16[4,128,512]{2,1,0:T(8,128)(2,1)}, u32[]{:S(2)}, u32[]{:S(2)}) collective-permute-start(bf16[4,128,512]{2,1,0:T(8,128)(2,1)} %get-tuple-element.80), channel_id=1, source_target_pairs={{0,64},{8,72},{16,80},{24,88},{32,96},{40,104},{48,112},{56,120},{... | collective-permute-start | bytes 1572872 | tf_op jit(solution)/shard_map/ppermute | solution.py:284
  129.4 11.0 %collective-permute-start.17 = (bf16[512,256]{1,0:T(8,128)(2,1)}, bf16[512,256]{1,0:T(8,128)(2,1)S(1)}, u32[]{:S(2)}, u32[]{:S(2)}) collective-permute-start(bf16[512,256]{1,0:T(8,128)(2,1)} %get-tuple-element.81), channel_id=1, source_target_pairs={{0,2},{1,3},{2,4},{3,5},{4,6},{5,7},{6,0},{7,1},{8,10},{9,11},{10,... | collective-permute-start | bytes 786440 | tf_op jit(solution)/shard_map/ppermute | solution.py:260
  129.5 13.8 %collective-permute-start.18 = (bf16[512,256]{1,0:T(8,128)(2,1)}, bf16[512,256]{1,0:T(8,128)(2,1)}, u32[]{:S(2)}, u32[]{:S(2)}) collective-permute-start(bf16[512,256]{1,0:T(8,128)(2,1)} %get-tuple-element.82), channel_id=1, source_target_pairs={{0,4},{1,5},{2,6},{3,7},{4,0},{5,1},{6,2},{7,3},{8,12},{9,13},{10,... | collective-permute-start | bytes 786440 | tf_op jit(solution)/shard_map/ppermute | solution.py:260
  131.7 12.7 %collective-permute-start.19 = (bf16[512,256]{1,0:T(8,128)(2,1)}, bf16[512,256]{1,0:T(8,128)(2,1)}, u32[]{:S(2)}, u32[]{:S(2)}) collective-permute-start(bf16[512,256]{1,0:T(8,128)(2,1)} %get-tuple-element.83), channel_id=1, source_target_pairs={{0,6},{1,7},{2,0},{3,1},{4,2},{5,3},{6,4},{7,5},{8,14},{9,15},{10,... | collective-permute-start | bytes 786440 | tf_op jit(solution)/shard_map/ppermute | solution.py:260
  144.4 1.0 copy-start.1
  148.0 4.4 %collective-permute-start.21 = (bf16[256,2048]{1,0:T(8,128)(2,1)S(1)}, bf16[256,2048]{1,0:T(8,128)(2,1)S(1)}, u32[]{:S(2)}, u32[]{:S(2)}) collective-permute-start(bf16[256,2048]{1,0:T(8,128)(2,1)S(1)} %mix.3), channel_id=1, source_target_pairs={{0,1},{1,0},{2,3},{3,2},{4,5},{5,4},{6,7},{7,6},{8,9},{9,8},{10,11... | collective-permute-start | bytes 3145736 | tf_op jit(solution)/shard_map/ppermute | solution.py:295

commit v9 on v8

--- a/solution.py
+++ b/solution.py
@@ -20,7 +20,7 @@
 STEPS = ((1, 2, 3), (0,))
 ALONE = 2
 LATE = 10
-COLUMNS = 1024
+COLUMNS = 512
 VMEM = 60 * 1024 * 1024
 MOST = 60 * 1024 * 1024
 LEAST = 16 * 1024 * 1024

time: 154 us -> 156 us (1.013)
  Pallas kernels: 47.1 us -> 48.8 us
    pallas_call x2, Pallas kernels: 5.45 us -> 7.2 us  [mix(): pl.pallas_call(mix_kernel, grid_spec=pltpu.PrefetchScalarGridSpec(num_sca...]
where the time goes in v9:
time: 156 us; the launch traced here: 155 us
  starting transfers between devices  62.6 us (40%)
  Pallas kernels  48.8 us (31%)
  waiting for transfers between devices  40.2 us (26%)
  other arithmetic  1.87 us (1%)
  local copies, waits for them, and re-layouts  1.81 us (1%)
    ppermute x15, starting transfers between devices, body(): lax.ppermute(send, 'seq', [(s, shifted(s, shift)) for s in range(shards)])  54.3 us
    ppermute x15, waiting for transfers between devices, body(): lax.ppermute(send, 'seq', [(s, shifted(s, shift)) for s in range(shards)])  36.1 us
    pallas_call x2, Pallas kernels, project(): pl.pallas_call(functools.partial(project_kernel, widths=widths, scales=le...  16.4 us
    pallas_call x2, Pallas kernels, attend(): pl.pallas_call(functools.partial(attend_kernel, tiles=tiles, heads=querie...  16.3 us
    pallas_call x2, Pallas kernels, dispatch(): pl.pallas_call(functools.partial(dispatch_kernel, shifts=shifts), in_spec...  7.27 us
    pallas_call x2, Pallas kernels, mix(): pl.pallas_call(mix_kernel, grid_spec=pltpu.PrefetchScalarGridSpec(num_sca...  7.2 us
    ppermute x6, starting transfers between devices, along(): lax.ppermute(x, 'head', [(s, (s // 2 + shift) % pairs * 2 + s % 2) for s...  6.63 us
    ppermute x6, waiting for transfers between devices, along(): lax.ppermute(x, 'head', [(s, (s // 2 + shift) % pairs * 2 + s % 2) for s...  4.03 us
  transfers between devices with their start and end apart: 22, of which 11 were waited for; matrix products, arithmetic and copies ran while one was open for 0% of the time, Pallas kernels for 29%

profile of v9, /device:TPU:7, one launch (start us, length us, event | category | flops | bytes accessed | tf_op | source)
XLA Modules:
  0.0 155.4 jit_solution(17596831146993365324)
XLA Ops:
  0.0 1.3 collective-permute-start.2
  1.3 1.4 collective-permute-start.3
  2.7 1.7 %tables.1 = (s32[8,128]{1,0:T(8,128)}, s32[4,256]{1,0:T(4,128)}) custom-call(s32[1]{0:T(128)} %bitcast.3.me_ref, s32[4,256]{1,0:T(4,128)} %bitcast.21), custom_call_target="tpu_custom_call" | custom-call | tf_op jit(solution)/shard_map/tables/pallas_call | solution.py:262
  4.4 9.2 %project.2.held_ref.own_ref = bf16[16,128,512]{2,1,0:T(8,128)(2,1)} custom-call(bf16[2048,2048]{1,0:T(8,128)(2,1)} %refs_0_.2, f32[16,128]{1,0:T(8,128)} %bitcast.19, bf16[3,2048,256]{2,1,0:T(8,128)(2,1)} %bitcast.16, bf16[3,2048,256]{2,1,0:T(8,128)(2,1)} %bitcast.17), custom_call_target="tpu_custom_call" | custom-call | tf_op jit(solution)/shard_map/project/pallas_call | solution.py:106
  13.6 2.7 %dispatch.2 = (bf16[4,128,512]{2,1,0:T(8,128)(2,1)}, bf16[4,128,512]{2,1,0:T(8,128)(2,1)}) custom-call(s32[1]{0:T(128)} %bitcast.3.me_ref, s32[8,128]{1,0:T(8,128)} %get-tuple-element.47.chosen_ref, bf16[16,128,512]{2,1,0:T(8,128)(2,1)} %project.2.held_ref.own_ref), custom_call_target="tpu_custom_call" | custom-call | tf_op jit(solution)/shard_map/dispatch/pallas_call | solution.py:141
  16.4 4.5 %collective-permute-start = (bf16[4,128,512]{2,1,0:T(8,128)(2,1)}, bf16[4,128,512]{2,1,0:T(8,128)(2,1)S(1)}, u32[]{:S(2)}, u32[]{:S(2)}) collective-permute-start(bf16[4,128,512]{2,1,0:T(8,128)(2,1)} %get-tuple-element.51), channel_id=1, source_target_pairs={{0,80},{8,88},{16,64},{24,72},{32,112},{40,120},{48,96},{56,104},{... | collective-permute-start | bytes 1572872 | tf_op jit(solution)/shard_map/ppermute | solution.py:284
  20.9 2.3 %collective-permute-start.1 = (bf16[4,128,512]{2,1,0:T(8,128)(2,1)}, bf16[4,128,512]{2,1,0:T(8,128)(2,1)}, u32[]{:S(2)}, u32[]{:S(2)}) collective-permute-start(bf16[4,128,512]{2,1,0:T(8,128)(2,1)} %get-tuple-element.52), channel_id=1, source_target_pairs={{0,48},{8,56},{16,32},{24,40},{32,80},{40,88},{48,64},{56,72},{64,... | collective-permute-start | bytes 1572872 | tf_op jit(solution)/shard_map/ppermute | solution.py:284
  23.2 4.5 %dispatch.3 = (bf16[4,128,512]{2,1,0:T(8,128)(2,1)}, bf16[4,128,512]{2,1,0:T(8,128)(2,1)}, bf16[4,128,512]{2,1,0:T(8,128)(2,1)}, bf16[4,128,512]{2,1,0:T(8,128)(...) custom-call(s32[1]{0:T(128)} %bitcast.3.me_ref, ...), custom_call_target="tpu_custom_call" | custom-call | tf_op jit(solution)/shard_map/dispatch/pallas_call | solution.py:141
  27.7 0.0 collective-permute-done.3.refs_7_
  27.7 2.0 %collective-permute-start.4 = (bf16[4,128,512]{2,1,0:T(8,128)(2,1)}, bf16[4,128,512]{2,1,0:T(8,128)(2,1)S(1)}, u32[]{:S(2)}, u32[]{:S(2)}) collective-permute-start(bf16[4,128,512]{2,1,0:T(8,128)(2,1)} %get-tuple-element.67), channel_id=1, source_target_pairs={{0,96},{8,104},{16,112},{24,120},{32,0},{40,8},{48,16},{56,24},{64... | collective-permute-start | bytes 1572872 | tf_op jit(solution)/shard_map/ppermute | solution.py:284
  29.7 0.9 collective-permute-start.5
  30.7 1.4 collective-permute-start.6
  32.1 0.7 collective-permute-done.rest_0_
  32.8 3.5 %collective-permute-start.12 = (bf16[4,128,512]{2,1,0:T(8,128)(2,1)}, bf16[4,128,512]{2,1,0:T(8,128)(2,1)S(1)}, u32[]{:S(2)}, u32[]{:S(2)}) collective-permute-start(bf16[4,128,512]{2,1,0:T(8,128)(2,1)} %get-tuple-element.75), channel_id=1, source_target_pairs={{0,72},{8,80},{16,88},{24,64},{32,104},{40,112},{48,120},{56,96},{... | collective-permute-start | bytes 1572872 | tf_op jit(solution)/shard_map/ppermute | solution.py:284
  36.3 8.9 %collective-permute-done.1.rest_1_ = bf16[4,128,512]{2,1,0:T(8,128)(2,1)} collective-permute-done((bf16[4,128,512]{2,1,0:T(8,128)(2,1)}, bf16[4,128,512]{2,1,0:T(8,128)(2,1)}, u32[]{:S(2)}, u32[]{:S(2)}) %collective-permute-start.1) | collective-permute-done | bytes 524320 | tf_op jit(solution)/shard_map/ppermute | solution.py:284
  45.2 0.6 collective-permute-start.7
  45.8 2.4 %collective-permute-done.4.rest_2_ = bf16[4,128,512]{2,1,0:T(8,128)(2,1)S(1)} collective-permute-done((bf16[4,128,512]{2,1,0:T(8,128)(2,1)}, bf16[4,128,512]{2,1,0:T(8,128)(2,1)S(1)}, u32[]{:S(2)}, u32[]{:S(2)}) %collective-permute-start.4) | collective-permute-done | bytes 524320 | tf_op jit(solution)/shard_map/ppermute | solution.py:284
  48.2 11.4 %collective-permute-start.8 = (bf16[4,128,512]{2,1,0:T(8,128)(2,1)}, bf16[4,128,512]{2,1,0:T(8,128)(2,1)S(1)}, u32[]{:S(2)}, u32[]{:S(2)}) collective-permute-start(bf16[4,128,512]{2,1,0:T(8,128)(2,1)} %get-tuple-element.71), channel_id=1, source_target_pairs={{0,88},{8,64},{16,72},{24,80},{32,120},{40,96},{48,104},{56,112},{... | collective-permute-start | bytes 1572872 | tf_op jit(solution)/shard_map/ppermute | solution.py:284
  59.6 0.0 collective-permute-done.5.rest_3_
  59.6 3.1 %collective-permute-start.9 = (bf16[4,128,512]{2,1,0:T(8,128)(2,1)}, bf16[4,128,512]{2,1,0:T(8,128)(2,1)S(1)}, u32[]{:S(2)}, u32[]{:S(2)}) collective-permute-start(bf16[4,128,512]{2,1,0:T(8,128)(2,1)} %get-tuple-element.72), channel_id=1, source_target_pairs={{0,8},{8,16},{16,24},{24,0},{32,40},{40,48},{48,56},{56,32},{64,72... | collective-permute-start | bytes 1572872 | tf_op jit(solution)/shard_map/ppermute | solution.py:284
  62.6 5.8 %collective-permute-done.6.rest_4_ = bf16[4,128,512]{2,1,0:T(8,128)(2,1)S(1)} collective-permute-done((bf16[4,128,512]{2,1,0:T(8,128)(2,1)}, bf16[4,128,512]{2,1,0:T(8,128)(2,1)S(1)}, u32[]{:S(2)}, u32[]{:S(2)}) %collective-permute-start.6) | collective-permute-done | bytes 524320 | tf_op jit(solution)/shard_map/ppermute | solution.py:284
  68.4 0.0 collective-permute-start.10
  68.5 9.4 %collective-permute-start.11 = (bf16[4,128,512]{2,1,0:T(8,128)(2,1)}, bf16[4,128,512]{2,1,0:T(8,128)(2,1)S(1)}, u32[]{:S(2)}, u32[]{:S(2)}) collective-permute-start(bf16[4,128,512]{2,1,0:T(8,128)(2,1)} %get-tuple-element.74), channel_id=1, source_target_pairs={{0,120},{8,96},{16,104},{24,112},{32,24},{40,0},{48,8},{56,16},{64... | collective-permute-start | bytes 1572872 | tf_op jit(solution)/shard_map/ppermute | solution.py:284
  77.9 0.1 collective-permute-start.20
  78.0 2.3 %collective-permute-done.8.rest_6_ = bf16[4,128,512]{2,1,0:T(8,128)(2,1)S(1)} collective-permute-done((bf16[4,128,512]{2,1,0:T(8,128)(2,1)}, bf16[4,128,512]{2,1,0:T(8,128)(2,1)S(1)}, u32[]{:S(2)}, u32[]{:S(2)}) %collective-permute-start.8) | collective-permute-done | bytes 524320 | tf_op jit(solution)/shard_map/ppermute | solution.py:284
  80.3 0.4 collective-permute-start.13
  80.7 4.4 %collective-permute-start.14 = (bf16[4,128,512]{2,1,0:T(8,128)(2,1)}, bf16[4,128,512]{2,1,0:T(8,128)(2,1)}, u32[]{:S(2)}, u32[]{:S(2)}) collective-permute-start(bf16[4,128,512]{2,1,0:T(8,128)(2,1)} %get-tuple-element.78), channel_id=1, source_target_pairs={{0,104},{8,112},{16,120},{24,96},{32,8},{40,16},{48,24},{56,0},{64... | collective-permute-start | bytes 1572872 | tf_op jit(solution)/shard_map/ppermute | solution.py:284
  85.2 3.1 %collective-permute-done.10.rest_8_ = bf16[4,128,512]{2,1,0:T(8,128)(2,1)S(1)} collective-permute-done((bf16[4,128,512]{2,1,0:T(8,128)(2,1)}, bf16[4,128,512]{2,1,0:T(8,128)(2,1)S(1)}, u32[]{:S(2)}, u32[]{:S(2)}) %collective-permute-start.10) | collective-permute-done | bytes 524320 | tf_op jit(solution)/shard_map/ppermute | solution.py:284
  88.3 6.3 %collective-permute-start.15 = (bf16[4,128,512]{2,1,0:T(8,128)(2,1)}, bf16[4,128,512]{2,1,0:T(8,128)(2,1)}, u32[]{:S(2)}, u32[]{:S(2)}) collective-permute-start(bf16[4,128,512]{2,1,0:T(8,128)(2,1)} %get-tuple-element.79), channel_id=1, source_target_pairs={{0,16},{8,24},{16,0},{24,8},{32,48},{40,56},{48,32},{56,40},{64,80... | collective-permute-start | bytes 1572872 | tf_op jit(solution)/shard_map/ppermute | solution.py:284
  94.7 0.8 copy-done.11
  95.5 4.0 %collective-permute-start.16 = (bf16[4,128,512]{2,1,0:T(8,128)(2,1)}, bf16[4,128,512]{2,1,0:T(8,128)(2,1)}, u32[]{:S(2)}, u32[]{:S(2)}) collective-permute-start(bf16[4,128,512]{2,1,0:T(8,128)(2,1)} %get-tuple-element.80), channel_id=1, source_target_pairs={{0,64},{8,72},{16,80},{24,88},{32,96},{40,104},{48,112},{56,120},{... | collective-permute-start | bytes 1572872 | tf_op jit(solution)/shard_map/ppermute | solution.py:284
  99.5 7.2 %project.3.queries_ref = bf16[16,128,256]{2,1,0:T(8,128)(2,1)} custom-call(bf16[2048,2048]{1,0:T(8,128)(2,1)} %refs_0_.2, f32[16,128]{1,0:T(8,128)} %bitcast.20, bf16[3,2048,256]{2,1,0:T(8,128)(2,1)} %bitcast.18), custom_call_target="tpu_custom_call" | custom-call | tf_op jit(solution)/shard_map/project/pallas_call | solution.py:106
  106.7 0.6 pad_add_fusion.first_ref
  107.3 2.9 %collective-permute-done.13.rest_11_ = bf16[4,128,512]{2,1,0:T(8,128)(2,1)} collective-permute-done((bf16[4,128,512]{2,1,0:T(8,128)(2,1)}, bf16[4,128,512]{2,1,0:T(8,128)(2,1)}, u32[]{:S(2)}, u32[]{:S(2)}) %collective-permute-start.13) | collective-permute-done | bytes 524320 | tf_op jit(solution)/shard_map/ppermute | solution.py:284
  110.2 3.4 %collective-permute-done.15.rest_13_ = bf16[4,128,512]{2,1,0:T(8,128)(2,1)} collective-permute-done((bf16[4,128,512]{2,1,0:T(8,128)(2,1)}, bf16[4,128,512]{2,1,0:T(8,128)(2,1)}, u32[]{:S(2)}, u32[]{:S(2)}) %collective-permute-start.15) | collective-permute-done | bytes 524320 | tf_op jit(solution)/shard_map/ppermute | solution.py:284
  113.6 6.6 %collective-permute-done.16.rest_14_ = bf16[4,128,512]{2,1,0:T(8,128)(2,1)} collective-permute-done((bf16[4,128,512]{2,1,0:T(8,128)(2,1)}, bf16[4,128,512]{2,1,0:T(8,128)(2,1)}, u32[]{:S(2)}, u32[]{:S(2)}) %collective-permute-start.16) | collective-permute-done | bytes 524320 | tf_op jit(solution)/shard_map/ppermute | solution.py:284
  120.2 9.1 %attend.3 = (bf16[512,256]{1,0:T(8,128)(2,1)}, bf16[512,256]{1,0:T(8,128)(2,1)}, bf16[512,256]{1,0:T(8,128)(2,1)}) custom-call(s32[2]{0:T(128)} %pad_add_fusion.first_ref, s32[4,256]{1,0:T(4,128)} %get-tuple-element.46.source_ref, bf16[16,128,256]{2,1,0:T(8,128)(2,1)} %project.3.queries_ref, bf16[16,128,512]{2,1,0:T(8,128)(2,1)} %project.2.held_ref.own_ref, ...), custom_call_target="tpu_custom_call" | custom-call | tf_op jit(solution)/shard_map/attend/pallas_call | solution.py:204
  129.4 0.1 collective-permute-start.17
  129.5 2.2 %collective-permute-start.18 = (bf16[512,256]{1,0:T(8,128)(2,1)}, bf16[512,256]{1,0:T(8,128)(2,1)}, u32[]{:S(2)}, u32[]{:S(2)}) collective-permute-start(bf16[512,256]{1,0:T(8,128)(2,1)} %get-tuple-element.82), channel_id=1, source_target_pairs={{0,4},{1,5},{2,6},{3,7},{4,0},{5,1},{6,2},{7,3},{8,12},{9,13},{10,... | collective-permute-start | bytes 786440 | tf_op jit(solution)/shard_map/ppermute | solution.py:260
  131.7 1.5 collective-permute-start.19
  133.2 7.1 %attend.2 = bf16[512,256]{1,0:T(8,128)(2,1)} custom-call(s32[2]{0:T(128)} %pad_add_fusion.first_ref, s32[4,256]{1,0:T(4,128)} %get-tuple-element.46.source_ref, bf16[16,128,256]{2,1,0:T(8,128)(2,1)} %project.3.queries_ref, bf16[16,128,512]{2,1,0:T(8,128)(2,1)} %project.2.held_ref.own_ref, bf16[4,128,512]{2,1,0:T(8,128)(2,1)} %copy-done.2, ...), custom_call_target="tpu_custom_call" | custom-call | tf_op jit(solution)/shard_map/attend/pallas_call | solution.py:204
  140.4 2.9 %collective-permute-done.18 = bf16[512,256]{1,0:T(8,128)(2,1)} collective-permute-done((bf16[512,256]{1,0:T(8,128)(2,1)}, bf16[512,256]{1,0:T(8,128)(2,1)}, u32[]{:S(2)}, u32[]{:S(2)}) %collective-permute-start.18) | collective-permute-done | bytes 262176 | tf_op jit(solution)/shard_map/ppermute | solution.py:260
  143.2 1.1 collective-permute-done.19
  144.4 0.9 copy-done.1
  145.3 3.6 %mix.3 = bf16[256,2048]{1,0:T(8,128)(2,1)S(1)} custom-call(s32[1]{0:T(128)} %bitcast.11.half_ref, bf16[2,256,256]{2,1,0:T(8,128)(2,1)S(1)} %bitcast.12, bf16[2,256,256]{2,1,0:T(8,128)(2,1)S(1)} %bitcast.14, bf16[2,256,256]{2,1,0:T(8,128)(2,1)} %bitcast.9.refs_2_, bf16[2,256,256]{2,1,0:T(8,128)(2,1)} %bitcast.10.refs_3_, bf16[256,2048]{1,0:T(8,128)(2,1)S(1)} %copy-done, ...), custom_call_target="tpu_custom_call" | custom-call | tf_op jit(solution)/shard_map/mix/pallas_call | solution.py:230
  148.9 1.6 %collective-permute-start.21 = (bf16[256,2048]{1,0:T(8,128)(2,1)S(1)}, bf16[256,2048]{1,0:T(8,128)(2,1)S(1)}, u32[]{:S(2)}, u32[]{:S(2)}) collective-permute-start(bf16[256,2048]{1,0:T(8,128)(2,1)S(1)} %mix.3), channel_id=1, source_target_pairs={{0,1},{1,0},{2,3},{3,2},{4,5},{5,4},{6,7},{7,6},{8,9},{9,8},{10,11... | collective-permute-start | bytes 3145736 | tf_op jit(solution)/shard_map/ppermute | solution.py:295
  150.5 3.6 %mix.2 = f32[256,2048]{1,0:T(8,128)S(1)} custom-call(s32[1]{0:T(128)} %bitcast.half_ref, bf16[2,256,256]{2,1,0:T(8,128)(2,1)S(1)} %bitcast.13, bf16[2,256,256]{2,1,0:T(8,128)(2,1)S(1)} %bitcast.15, bf16[2,256,256]{2,1,0:T(8,128)(2,1)} %bitcast.9.refs_2_, bf16[2,256,256]{2,1,0:T(8,128)(2,1)} %bitcast.10.refs_3_, bf16[256,2048]{1,0:T(8,128)(2,1)S(1)} %copy-done, ...), custom_call_target="tpu_custom_call" | custom-call | tf_op jit(solution)/shard_map/mix/pallas_call | solution.py:230
  154.2 1.3 add_convert_fusion
  (31 shorter events, 0.1 us)
Async XLA Ops:
  0.0 27.7 %collective-permute-start.2 = (bf16[256,2048]{1,0:T(8,128)(2,1)}, bf16[256,2048]{1,0:T(8,128)(2,1)S(1)}, u32[]{:S(2)}, u32[]{:S(2)}) collective-permute-start(bf16[256,2048]{1,0:T(8,128)(2,1)} %refs_4_.3), channel_id=1, source_target_pairs={{0,2},{1,3},{2,4},{3,5},{4,6},{5,7},{6,0},{7,1},{8,10},{9,11},{10,... | collective-permute-start | bytes 3145736 | tf_op jit(solution)/shard_map/ppermute | solution.py:260
  1.3 26.4 %collective-permute-start.3 = (bf16[256,2048]{1,0:T(8,128)(2,1)}, bf16[256,2048]{1,0:T(8,128)(2,1)S(1)}, u32[]{:S(2)}, u32[]{:S(2)}) collective-permute-start(bf16[256,2048]{1,0:T(8,128)(2,1)} %refs_4_.3), channel_id=1, source_target_pairs={{0,6},{1,7},{2,0},{3,1},{4,2},{5,3},{6,4},{7,5},{8,14},{9,15},{10,... | collective-permute-start | bytes 3145736 | tf_op jit(solution)/shard_map/ppermute | solution.py:260
  13.6 64.3 %copy-start = (bf16[256,2048]{1,0:T(8,128)(2,1)S(1)}, bf16[256,2048]{1,0:T(8,128)(2,1)}, u32[]{:S(2)}) copy-start(bf16[256,2048]{1,0:T(8,128)(2,1)} %refs_4_.3) | copy-start | bytes 3145732
  16.4 16.4 %collective-permute-start = (bf16[4,128,512]{2,1,0:T(8,128)(2,1)}, bf16[4,128,512]{2,1,0:T(8,128)(2,1)S(1)}, u32[]{:S(2)}, u32[]{:S(2)}) collective-permute-start(bf16[4,128,512]{2,1,0:T(8,128)(2,1)} %get-tuple-element.51), channel_id=1, source_target_pairs={{0,80},{8,88},{16,64},{24,72},{32,112},{40,120},{48,96},{56,104},{... | collective-permute-start | bytes 1572872 | tf_op jit(solution)/shard_map/ppermute | solution.py:284
  20.9 24.3 %collective-permute-start.1 = (bf16[4,128,512]{2,1,0:T(8,128)(2,1)}, bf16[4,128,512]{2,1,0:T(8,128)(2,1)}, u32[]{:S(2)}, u32[]{:S(2)}) collective-permute-start(bf16[4,128,512]{2,1,0:T(8,128)(2,1)} %get-tuple-element.52), channel_id=1, source_target_pairs={{0,48},{8,56},{16,32},{24,40},{32,80},{40,88},{48,64},{56,72},{64,... | collective-permute-start | bytes 1572872 | tf_op jit(solution)/shard_map/ppermute | solution.py:284
  27.7 20.5 %collective-permute-start.4 = (bf16[4,128,512]{2,1,0:T(8,128)(2,1)}, bf16[4,128,512]{2,1,0:T(8,128)(2,1)S(1)}, u32[]{:S(2)}, u32[]{:S(2)}) collective-permute-start(bf16[4,128,512]{2,1,0:T(8,128)(2,1)} %get-tuple-element.67), channel_id=1, source_target_pairs={{0,96},{8,104},{16,112},{24,120},{32,0},{40,8},{48,16},{56,24},{64... | collective-permute-start | bytes 1572872 | tf_op jit(solution)/shard_map/ppermute | solution.py:284
  29.7 29.8 %collective-permute-start.5 = (bf16[4,128,512]{2,1,0:T(8,128)(2,1)}, bf16[4,128,512]{2,1,0:T(8,128)(2,1)S(1)}, u32[]{:S(2)}, u32[]{:S(2)}) collective-permute-start(bf16[4,128,512]{2,1,0:T(8,128)(2,1)} %get-tuple-element.68), channel_id=1, source_target_pairs={{0,112},{8,120},{16,96},{24,104},{32,16},{40,24},{48,0},{56,8},{64... | collective-permute-start | bytes 1572872 | tf_op jit(solution)/shard_map/ppermute | solution.py:284
  30.7 37.8 %collective-permute-start.6 = (bf16[4,128,512]{2,1,0:T(8,128)(2,1)}, bf16[4,128,512]{2,1,0:T(8,128)(2,1)S(1)}, u32[]{:S(2)}, u32[]{:S(2)}) collective-permute-start(bf16[4,128,512]{2,1,0:T(8,128)(2,1)} %get-tuple-element.69), channel_id=1, source_target_pairs={{0,32},{8,40},{16,48},{24,56},{32,64},{40,72},{48,80},{56,88},{64,... | collective-permute-start | bytes 1572872 | tf_op jit(solution)/shard_map/ppermute | solution.py:284
  32.8 45.1 %copy-start.2 = (bf16[4,128,512]{2,1,0:T(8,128)(2,1)}, bf16[4,128,512]{2,1,0:T(8,128)(2,1)S(1)}, u32[]{:S(2)}) copy-start(bf16[4,128,512]{2,1,0:T(8,128)(2,1)S(1)} %collective-permute-done.rest_0_) | copy-start | bytes 1572868
  32.8 35.7 %collective-permute-start.12 = (bf16[4,128,512]{2,1,0:T(8,128)(2,1)}, bf16[4,128,512]{2,1,0:T(8,128)(2,1)S(1)}, u32[]{:S(2)}, u32[]{:S(2)}) collective-permute-start(bf16[4,128,512]{2,1,0:T(8,128)(2,1)} %get-tuple-element.75), channel_id=1, source_target_pairs={{0,72},{8,80},{16,88},{24,64},{32,104},{40,112},{48,120},{56,96},{... | collective-permute-start | bytes 1572872 | tf_op jit(solution)/shard_map/ppermute | solution.py:284
  45.2 32.7 %collective-permute-start.7 = (bf16[4,128,512]{2,1,0:T(8,128)(2,1)}, bf16[4,128,512]{2,1,0:T(8,128)(2,1)S(1)}, u32[]{:S(2)}, u32[]{:S(2)}) collective-permute-start(bf16[4,128,512]{2,1,0:T(8,128)(2,1)} %get-tuple-element.70), channel_id=1, source_target_pairs={{0,24},{8,0},{16,8},{24,16},{32,56},{40,32},{48,40},{56,48},{64,88... | collective-permute-start | bytes 1572872 | tf_op jit(solution)/shard_map/ppermute | solution.py:284
  48.2 29.7 %copy-start.3 = (bf16[4,128,512]{2,1,0:T(8,128)(2,1)}, bf16[4,128,512]{2,1,0:T(8,128)(2,1)S(1)}, u32[]{:S(2)}) copy-start(bf16[4,128,512]{2,1,0:T(8,128)(2,1)S(1)} %collective-permute-done.4.rest_2_) | copy-start | bytes 1572868
  48.2 32.1 %collective-permute-start.8 = (bf16[4,128,512]{2,1,0:T(8,128)(2,1)}, bf16[4,128,512]{2,1,0:T(8,128)(2,1)S(1)}, u32[]{:S(2)}, u32[]{:S(2)}) collective-permute-start(bf16[4,128,512]{2,1,0:T(8,128)(2,1)} %get-tuple-element.71), channel_id=1, source_target_pairs={{0,88},{8,64},{16,72},{24,80},{32,120},{40,96},{48,104},{56,112},{... | collective-permute-start | bytes 1572872 | tf_op jit(solution)/shard_map/ppermute | solution.py:284
  59.6 18.4 %copy-start.4 = (bf16[4,128,512]{2,1,0:T(8,128)(2,1)}, bf16[4,128,512]{2,1,0:T(8,128)(2,1)S(1)}, u32[]{:S(2)}) copy-start(bf16[4,128,512]{2,1,0:T(8,128)(2,1)S(1)} %collective-permute-done.5.rest_3_) | copy-start | bytes 1572868
  59.6 21.1 %collective-permute-start.9 = (bf16[4,128,512]{2,1,0:T(8,128)(2,1)}, bf16[4,128,512]{2,1,0:T(8,128)(2,1)S(1)}, u32[]{:S(2)}, u32[]{:S(2)}) collective-permute-start(bf16[4,128,512]{2,1,0:T(8,128)(2,1)} %get-tuple-element.72), channel_id=1, source_target_pairs={{0,8},{8,16},{16,24},{24,0},{32,40},{40,48},{48,56},{56,32},{64,72... | collective-permute-start | bytes 1572872 | tf_op jit(solution)/shard_map/ppermute | solution.py:284
  68.4 11.8 %copy-start.5 = (bf16[4,128,512]{2,1,0:T(8,128)(2,1)}, bf16[4,128,512]{2,1,0:T(8,128)(2,1)S(1)}, u32[]{:S(2)}) copy-start(bf16[4,128,512]{2,1,0:T(8,128)(2,1)S(1)} %collective-permute-done.6.rest_4_) | copy-start | bytes 1572868
  68.4 19.9 %collective-permute-start.10 = (bf16[4,128,512]{2,1,0:T(8,128)(2,1)}, bf16[4,128,512]{2,1,0:T(8,128)(2,1)S(1)}, u32[]{:S(2)}, u32[]{:S(2)}) collective-permute-start(bf16[4,128,512]{2,1,0:T(8,128)(2,1)} %get-tuple-element.73), channel_id=1, source_target_pairs={{0,40},{8,48},{16,56},{24,32},{32,72},{40,80},{48,88},{56,64},{64,... | collective-permute-start | bytes 1572872 | tf_op jit(solution)/shard_map/ppermute | solution.py:284
  68.5 12.3 %copy-start.6 = (bf16[4,128,512]{2,1,0:T(8,128)(2,1)}, bf16[4,128,512]{2,1,0:T(8,128)(2,1)S(1)}, u32[]{:S(2)}) copy-start(bf16[4,128,512]{2,1,0:T(8,128)(2,1)S(1)} %collective-permute-done.12.rest_10_) | copy-start | bytes 1572868
  68.5 26.2 %collective-permute-start.11 = (bf16[4,128,512]{2,1,0:T(8,128)(2,1)}, bf16[4,128,512]{2,1,0:T(8,128)(2,1)S(1)}, u32[]{:S(2)}, u32[]{:S(2)}) collective-permute-start(bf16[4,128,512]{2,1,0:T(8,128)(2,1)} %get-tuple-element.74), channel_id=1, source_target_pairs={{0,120},{8,96},{16,104},{24,112},{32,24},{40,0},{48,8},{56,16},{64... | collective-permute-start | bytes 1572872 | tf_op jit(solution)/shard_map/ppermute | solution.py:284
  77.9 2.8 %copy-start.7 = (bf16[4,128,512]{2,1,0:T(8,128)(2,1)}, bf16[4,128,512]{2,1,0:T(8,128)(2,1)S(1)}, u32[]{:S(2)}) copy-start(bf16[4,128,512]{2,1,0:T(8,128)(2,1)S(1)} %collective-permute-done.7.rest_5_) | copy-start | bytes 1572868
  77.9 66.5 %collective-permute-start.20 = (bf16[256,2048]{1,0:T(8,128)(2,1)S(1)}, bf16[256,2048]{1,0:T(8,128)(2,1)}, u32[]{:S(2)}, u32[]{:S(2)}) collective-permute-start(bf16[256,2048]{1,0:T(8,128)(2,1)S(1)} %copy-done), channel_id=1, source_target_pairs={{0,4},{1,5},{2,6},{3,7},{4,0},{5,1},{6,2},{7,3},{8,12},{9,13},{10,... | collective-permute-start | bytes 3145736 | tf_op jit(solution)/shard_map/ppermute | solution.py:260
  80.3 4.9 %copy-start.8 = (bf16[4,128,512]{2,1,0:T(8,128)(2,1)}, bf16[4,128,512]{2,1,0:T(8,128)(2,1)S(1)}, u32[]{:S(2)}) copy-start(bf16[4,128,512]{2,1,0:T(8,128)(2,1)S(1)} %collective-permute-done.8.rest_6_) | copy-start | bytes 1572868
  80.3 29.9 %collective-permute-start.13 = (bf16[4,128,512]{2,1,0:T(8,128)(2,1)}, bf16[4,128,512]{2,1,0:T(8,128)(2,1)}, u32[]{:S(2)}, u32[]{:S(2)}) collective-permute-start(bf16[4,128,512]{2,1,0:T(8,128)(2,1)} %get-tuple-element.77), channel_id=1, source_target_pairs={{0,56},{8,32},{16,40},{24,48},{32,88},{40,64},{48,72},{56,80},{64,... | collective-permute-start | bytes 1572872 | tf_op jit(solution)/shard_map/ppermute | solution.py:284
  80.7 7.6 %copy-start.9 = (bf16[4,128,512]{2,1,0:T(8,128)(2,1)}, bf16[4,128,512]{2,1,0:T(8,128)(2,1)S(1)}, u32[]{:S(2)}) copy-start(bf16[4,128,512]{2,1,0:T(8,128)(2,1)S(1)} %collective-permute-done.9.rest_7_) | copy-start | bytes 1572868
  80.7 29.5 %collective-permute-start.14 = (bf16[4,128,512]{2,1,0:T(8,128)(2,1)}, bf16[4,128,512]{2,1,0:T(8,128)(2,1)}, u32[]{:S(2)}, u32[]{:S(2)}) collective-permute-start(bf16[4,128,512]{2,1,0:T(8,128)(2,1)} %get-tuple-element.78), channel_id=1, source_target_pairs={{0,104},{8,112},{16,120},{24,96},{32,8},{40,16},{48,24},{56,0},{64... | collective-permute-start | bytes 1572872 | tf_op jit(solution)/shard_map/ppermute | solution.py:284
  88.3 6.3 %copy-start.10 = (bf16[4,128,512]{2,1,0:T(8,128)(2,1)}, bf16[4,128,512]{2,1,0:T(8,128)(2,1)S(1)}, u32[]{:S(2)}) copy-start(bf16[4,128,512]{2,1,0:T(8,128)(2,1)S(1)} %collective-permute-done.10.rest_8_) | copy-start | bytes 1572868
  88.3 25.3 %collective-permute-start.15 = (bf16[4,128,512]{2,1,0:T(8,128)(2,1)}, bf16[4,128,512]{2,1,0:T(8,128)(2,1)}, u32[]{:S(2)}, u32[]{:S(2)}) collective-permute-start(bf16[4,128,512]{2,1,0:T(8,128)(2,1)} %get-tuple-element.79), channel_id=1, source_target_pairs={{0,16},{8,24},{16,0},{24,8},{32,48},{40,56},{48,32},{56,40},{64,80... | collective-permute-start | bytes 1572872 | tf_op jit(solution)/shard_map/ppermute | solution.py:284
  94.7 0.8 copy-start.11
  95.5 24.7 %collective-permute-start.16 = (bf16[4,128,512]{2,1,0:T(8,128)(2,1)}, bf16[4,128,512]{2,1,0:T(8,128)(2,1)}, u32[]{:S(2)}, u32[]{:S(2)}) collective-permute-start(bf16[4,128,512]{2,1,0:T(8,128)(2,1)} %get-tuple-element.80), channel_id=1, source_target_pairs={{0,64},{8,72},{16,80},{24,88},{32,96},{40,104},{48,112},{56,120},{... | collective-permute-start | bytes 1572872 | tf_op jit(solution)/shard_map/ppermute | solution.py:284
  129.4 11.0 %collective-permute-start.17 = (bf16[512,256]{1,0:T(8,128)(2,1)}, bf16[512,256]{1,0:T(8,128)(2,1)S(1)}, u32[]{:S(2)}, u32[]{:S(2)}) collective-permute-start(bf16[512,256]{1,0:T(8,128)(2,1)} %get-tuple-element.81), channel_id=1, source_target_pairs={{0,2},{1,3},{2,4},{3,5},{4,6},{5,7},{6,0},{7,1},{8,10},{9,11},{10,... | collective-permute-start | bytes 786440 | tf_op jit(solution)/shard_map/ppermute | solution.py:260
  129.5 13.8 %collective-permute-start.18 = (bf16[512,256]{1,0:T(8,128)(2,1)}, bf16[512,256]{1,0:T(8,128)(2,1)}, u32[]{:S(2)}, u32[]{:S(2)}) collective-permute-start(bf16[512,256]{1,0:T(8,128)(2,1)} %get-tuple-element.82), channel_id=1, source_target_pairs={{0,4},{1,5},{2,6},{3,7},{4,0},{5,1},{6,2},{7,3},{8,12},{9,13},{10,... | collective-permute-start | bytes 786440 | tf_op jit(solution)/shard_map/ppermute | solution.py:260
  131.7 12.7 %collective-permute-start.19 = (bf16[512,256]{1,0:T(8,128)(2,1)}, bf16[512,256]{1,0:T(8,128)(2,1)}, u32[]{:S(2)}, u32[]{:S(2)}) collective-permute-start(bf16[512,256]{1,0:T(8,128)(2,1)} %get-tuple-element.83), channel_id=1, source_target_pairs={{0,6},{1,7},{2,0},{3,1},{4,2},{5,3},{6,4},{7,5},{8,14},{9,15},{10,... | collective-permute-start | bytes 786440 | tf_op jit(solution)/shard_map/ppermute | solution.py:260
  144.4 1.0 copy-start.1
  148.9 5.3 %collective-permute-start.21 = (bf16[256,2048]{1,0:T(8,128)(2,1)S(1)}, bf16[256,2048]{1,0:T(8,128)(2,1)S(1)}, u32[]{:S(2)}, u32[]{:S(2)}) collective-permute-start(bf16[256,2048]{1,0:T(8,128)(2,1)S(1)} %mix.3), channel_id=1, source_target_pairs={{0,1},{1,0},{2,3},{3,2},{4,5},{5,4},{6,7},{7,6},{8,9},{9,8},{10,11... | collective-permute-start | bytes 3145736 | tf_op jit(solution)/shard_map/ppermute | solution.py:295
